TPU v7x, 32 devices: a whole 2x2x4 slice. The times are simulated.
32 devices in a mesh: pipe: 2 (over core), tensor: 4 (over y, x), dp: 4 (over z).
Axes of the slice: x: 2, y: 2, z: 4, core: 2. Of those that a mesh axis runs over, the one named last changes fastest.
Arguments:
- ends: bfloat16 [2, 8, 1536, 1024], P('pipe', 'dp', 'tensor'), may hold values from -6 to 6
- segments: int32 [8, 1536], P('dp'), may hold values from 0 to 5, never falling along the last dimension, each value on 1 to 1024 neighbouring positions
- ln_gain: bfloat16 [2, 2, 1024], P('pipe'), may hold values from 0.5 to 1.5
- ln_bias: bfloat16 [2, 2, 1024], P('pipe'), may hold values from -2 to 2
- w_qkv: bfloat16 [2, 1024, 3072], P('pipe', None, 'tensor'), may hold values from -0.1875 to 0.1875
- b_qkv: bfloat16 [2, 3072], P('pipe', 'tensor'), may hold values from -2 to 2
- w_out: bfloat16 [2, 1024, 1024], P('pipe', 'tensor'), may hold values from -1 to 1
- w_in: bfloat16 [2, 1024, 4096], P('pipe', None, 'tensor'), may hold values from -0.1875 to 0.1875
- b_in: bfloat16 [2, 4096], P('pipe', 'tensor'), may hold values from -3 to 3
- w_fc2: bfloat16 [2, 4096, 1024], P('pipe', 'tensor'), may hold values from -0.09375 to 0.09375
- out_bias: bfloat16 [2, 2, 1024], P('pipe'), may hold values from -2 to 2
Outputs:
- boundary: bfloat16 [2, 8, 1536, 1024], P('pipe', 'dp', 'tensor')
- g_ln_gain: float32 [2, 2, 1024], P('pipe', None, ('tensor', 'dp'))
- g_ln_bias: float32 [2, 2, 1024], P('pipe', None, ('tensor', 'dp'))
- g_w_qkv: float32 [2, 1024, 3072], P('pipe', 'dp', 'tensor')
- g_b_qkv: float32 [2, 3072], P('pipe', ('tensor', 'dp'))
- g_w_out: float32 [2, 1024, 1024], P('pipe', ('tensor', 'dp'))
- g_w_in: float32 [2, 1024, 4096], P('pipe', 'dp', 'tensor')
- g_b_in: float32 [2, 4096], P('pipe', ('tensor', 'dp'))
- g_w_fc2: float32 [2, 4096, 1024], P('pipe', ('tensor', 'dp'))
- g_out_bias: float32 [2, 2, 1024], P('pipe', None, ('tensor', 'dp'))
Inputs may be any that keep to these rules, and one draw needn't show every extreme that they name: `segments`: each micro-batch of 1536 slots holds 6 whole documents in order, numbered from 0, each of 1 to 1024 tokens, one of exactly 1024.
All inputs are finite; a program needn't handle non-finite values.
Results may differ from a plain program's by a relative error of at most 0.014.
Values may be sent and summed in bfloat16 or wider, within the bound.
No kernel may reach another device: no remote copies, remote signals or barrier semaphores. Data moves between devices by JAX's collectives and lax.ppermute only.
A program may use at most 256 MiB of HBM per device.

v0:
```python
import math

import jax
import jax.numpy as jnp
from jax import lax
from jax.sharding import PartitionSpec as P

HEAD_DIM = 64
ROT = 16
QBLK = 512


EPSILON = 1e-05
MASKED = -1e30


def shifted_2(block, axis, distance):
    devices = range(lax.axis_size(axis))
    route = [(i - distance, i) for i in devices if i - distance in devices]
    return lax.ppermute(block, axis, route)


def positions_of(segment_row):
    length = segment_row.shape[0]
    places = jnp.arange(length, dtype=jnp.int32)
    begins = jnp.concatenate([jnp.ones((1,), dtype=jnp.bool_), segment_row[1:] != segment_row[:-1]])
    starts = lax.cummax(jnp.where(begins, places, 0), axis=0)
    return places - starts


def rotary_tables(positions):
    half_rot = ROT // 2
    frequency = jnp.power(10000.0, -2.0 * jnp.arange(half_rot, dtype=jnp.float32) / ROT)
    angles = positions.astype(jnp.float32)[:, None] * frequency[None, :]
    return (jnp.cos(angles)[:, None, :], jnp.sin(angles)[:, None, :])


def rotate(values, cosine_table, sine_table, direction):
    half_rot = ROT // 2
    front = values[..., :half_rot]
    second = values[..., half_rot:ROT]
    new_front = front * cosine_table - direction * second * sine_table
    new_second = second * cosine_table + direction * front * sine_table
    return jnp.concatenate([new_front, new_second, values[..., ROT:]], axis=-1)


def normalize(inputs):
    centre = jnp.mean(inputs, axis=-1, keepdims=True)
    shifted = inputs - centre
    inverse_std = lax.rsqrt(jnp.mean(shifted * shifted, axis=-1, keepdims=True) + EPSILON)
    return (shifted * inverse_std, inverse_std)


def norm_back(grad_sum, normal_rows, inverse_std):
    mean_grad = jnp.mean(grad_sum, axis=-1, keepdims=True)
    mean_cross = jnp.mean(grad_sum * normal_rows, axis=-1, keepdims=True)
    return (grad_sum - mean_grad - normal_rows * mean_cross) * inverse_std


def gelu_slope(values):
    cumulative = 0.5 * (1.0 + lax.erf(values * (1.0 / math.sqrt(2.0))))
    density = jnp.exp(-0.5 * values * values) * (1.0 / math.sqrt(2.0 * math.pi))
    return cumulative + values * density


def contract_rows(left_rows, right_rows):
    return jnp.einsum("ti,to->io", left_rows, right_rows, preferred_element_type=jnp.float32)


def allowed_mask(block_index, segment_row):
    length = segment_row.shape[0]
    query_places = block_index * QBLK + jnp.arange(QBLK, dtype=jnp.int32)
    query_segments = lax.dynamic_slice_in_dim(segment_row, block_index * QBLK, QBLK)
    key_places = jnp.arange(length, dtype=jnp.int32)
    return jnp.logical_and(
        key_places[None, :] <= query_places[:, None],
        segment_row[None, :] == query_segments[:, None],
    )


def pair_products(left_block, right_whole):
    return jnp.einsum("qhd,khd->hqk", left_block, right_whole, preferred_element_type=jnp.float32)


def attend_forward(queries, keys_rot, values, segment_row):
    length, head_count, head_width = queries.shape
    blocks = length // QBLK
    factor = 1.0 / math.sqrt(head_width)

    def one_block(item):
        block_index, query_block = item
        raw_scores = pair_products(query_block, keys_rot)
        scores = jnp.where(
            allowed_mask(block_index, segment_row)[None], raw_scores * factor, MASKED
        )
        top_score = jnp.max(scores, axis=-1, keepdims=True)
        exp_scores = jnp.exp(scores - top_score)
        totals = jnp.sum(exp_scores, axis=-1, keepdims=True)
        attention_weights = (exp_scores / totals).astype(jnp.bfloat16)
        mixed_block = jnp.einsum(
            "hqk,khd->qhd", attention_weights, values, preferred_element_type=jnp.float32
        )
        return (mixed_block, (top_score + jnp.log(totals))[..., 0])

    mixed, log_totals = lax.map(
        one_block,
        (
            jnp.arange(blocks, dtype=jnp.int32),
            queries.reshape(blocks, QBLK, head_count, head_width),
        ),
    )
    return (mixed.reshape(length, head_count * head_width).astype(jnp.bfloat16), log_totals)


def attend_backward(queries, keys_rot, values, mixed_grad, log_totals, segment_row):
    length, head_count, head_width = queries.shape
    blocks = length // QBLK
    factor = 1.0 / math.sqrt(head_width)

    def one_block(carry, item):
        key_grad, value_grad = carry
        block_index, query_block, grad_block, block_totals = item
        raw_scores = pair_products(query_block, keys_rot)
        allowed = allowed_mask(block_index, segment_row)[None]
        attention_weights = jnp.where(
            allowed, jnp.exp(raw_scores * factor - block_totals[..., None]), 0.0
        )
        weight_grad = pair_products(grad_block, values)
        inner_sum = jnp.sum(attention_weights * weight_grad, axis=-1, keepdims=True)
        score_grad = (attention_weights * (weight_grad - inner_sum)).astype(jnp.bfloat16)
        query_grad = (
            jnp.einsum("hqk,khd->qhd", score_grad, keys_rot, preferred_element_type=jnp.float32)
            * factor
        )
        key_grad = (
            key_grad
            + jnp.einsum(
                "hqk,qhd->khd", score_grad, query_block, preferred_element_type=jnp.float32
            )
            * factor
        )
        value_grad = value_grad + jnp.einsum(
            "hqk,qhd->khd",
            attention_weights.astype(jnp.bfloat16),
            grad_block,
            preferred_element_type=jnp.float32,
        )
        return ((key_grad, value_grad), query_grad)

    empty_grad = jnp.zeros((length, head_count, head_width), jnp.float32)
    shaped = (blocks, QBLK, head_count, head_width)
    (key_grad, value_grad), query_grad = lax.scan(
        one_block,
        (empty_grad, empty_grad),
        (
            jnp.arange(blocks, dtype=jnp.int32),
            queries.reshape(shaped),
            mixed_grad.reshape(shaped),
            log_totals,
        ),
    )
    return (query_grad.reshape(length, head_count, head_width), key_grad, value_grad)


def forward_section(incoming, segment_row, params):
    gains, biases, qkv_weight, qkv_bias, out_weight, in_weight, in_bias, fc2_weight, out_biases = (
        params
    )
    share_rows = incoming.astype(jnp.float32)
    normal_rows, inverse_std = normalize(share_rows)
    one_share = (normal_rows * gains[0] + biases[0]).astype(jnp.bfloat16)
    two_share = (normal_rows * gains[1] + biases[1]).astype(jnp.bfloat16)
    normed_one, normed_two = (
        lax.all_gather(one_share, "tensor", axis=0, tiled=True),
        lax.all_gather(two_share, "tensor", axis=0, tiled=True),
    )
    length = normed_one.shape[0]
    cosine_table, sine_table = rotary_tables(positions_of(segment_row))
    projected = jnp.dot(normed_one, qkv_weight, preferred_element_type=jnp.float32) + qkv_bias
    projected = projected.reshape(length, -1, 3, HEAD_DIM)
    queries = rotate(projected[:, :, 0], cosine_table, sine_table, 1.0).astype(jnp.bfloat16)
    keys_rot = rotate(projected[:, :, 1], cosine_table, sine_table, 1.0).astype(jnp.bfloat16)
    values = projected[:, :, 2].astype(jnp.bfloat16)
    mixed, log_totals = attend_forward(queries, keys_rot, values, segment_row)
    hidden_pre = jnp.dot(normed_two, in_weight, preferred_element_type=jnp.float32) + in_bias
    activated = jax.nn.gelu(hidden_pre, approximate=False).astype(jnp.bfloat16)
    summed = lax.psum_scatter(
        jnp.dot(mixed, out_weight, preferred_element_type=jnp.float32)
        + jnp.dot(activated, fc2_weight, preferred_element_type=jnp.float32),
        "tensor",
        scatter_dimension=0,
        tiled=True,
    )
    result = share_rows + summed + out_biases[0] + out_biases[1]
    kept = (
        normed_one,
        normed_two,
        normal_rows,
        inverse_std,
        queries,
        keys_rot,
        values,
        log_totals,
        mixed,
        hidden_pre,
        activated,
    )
    return (result, kept)


def backward_section(grad_share, segment_row, params, kept):
    gains, biases, qkv_weight, qkv_bias, out_weight, in_weight, in_bias, fc2_weight, out_biases = (
        params
    )
    (
        normed_one,
        normed_two,
        normal_rows,
        inverse_std,
        queries,
        keys_rot,
        values,
        log_totals,
        mixed,
        hidden_pre,
        activated,
    ) = kept
    grad_whole = lax.all_gather(grad_share, "tensor", axis=0, tiled=True)
    length = grad_whole.shape[0]
    share_grad = grad_share.astype(jnp.float32)
    out_bias_part = jnp.sum(share_grad, axis=0)
    out_weight_grad = contract_rows(mixed, grad_whole)
    fc2_weight_grad = contract_rows(activated, grad_whole)
    mixed_grad = jnp.einsum("to,io->ti", grad_whole, out_weight, preferred_element_type=jnp.float32)
    mixed_grad = mixed_grad.astype(jnp.bfloat16).reshape(length, -1, HEAD_DIM)
    active_grad = jnp.einsum(
        "to,io->ti", grad_whole, fc2_weight, preferred_element_type=jnp.float32
    )
    hidden_grad = (active_grad * gelu_slope(hidden_pre)).astype(jnp.bfloat16)
    in_bias_grad = jnp.sum(hidden_grad.astype(jnp.float32), axis=0)
    in_weight_grad = contract_rows(normed_two, hidden_grad)
    query_grad, key_grad, value_grad = attend_backward(
        queries, keys_rot, values, mixed_grad, log_totals, segment_row
    )
    cosine_table, sine_table = rotary_tables(positions_of(segment_row))
    qkv_grad = (
        jnp.stack(
            [
                rotate(query_grad, cosine_table, sine_table, -1.0),
                rotate(key_grad, cosine_table, sine_table, -1.0),
                value_grad,
            ],
            axis=2,
        )
        .reshape(length, -1)
        .astype(jnp.bfloat16)
    )
    qkv_bias_grad = jnp.sum(qkv_grad.astype(jnp.float32), axis=0)
    qkv_weight_grad = contract_rows(normed_one, qkv_grad)
    one_grad = jnp.einsum("tc,ic->ti", qkv_grad, qkv_weight, preferred_element_type=jnp.float32)
    two_grad = jnp.einsum("tc,ic->ti", hidden_grad, in_weight, preferred_element_type=jnp.float32)
    one_share, two_share = (
        lax.psum_scatter(one_grad, "tensor", scatter_dimension=0, tiled=True),
        lax.psum_scatter(two_grad, "tensor", scatter_dimension=0, tiled=True),
    )
    gain_part = jnp.stack(
        [jnp.sum(one_share * normal_rows, axis=0), jnp.sum(two_share * normal_rows, axis=0)]
    )
    norm_bias_part = jnp.stack([jnp.sum(one_share, axis=0), jnp.sum(two_share, axis=0)])
    input_grad = share_grad + norm_back(
        gains[0] * one_share + gains[1] * two_share, normal_rows, inverse_std
    )
    grads = (
        gain_part,
        norm_bias_part,
        jnp.stack([out_bias_part, out_bias_part]),
        qkv_weight_grad,
        qkv_bias_grad,
        out_weight_grad,
        in_weight_grad,
        in_bias_grad,
        fc2_weight_grad,
    )
    return (input_grad, grads)


def send_ahead(values):
    return shifted_2(values, "pipe", 1)


def send_behind(values):
    return shifted_2(values, "pipe", -1)


def body(ends, segments, ln_gain, ln_bias, w_qkv, b_qkv, w_out, w_in, b_in, w_fc2, out_bias):
    is_first = lax.axis_index("pipe") == 0
    params = tuple(
        (
            member[0]
            for member in (ln_gain, ln_bias, w_qkv, b_qkv, w_out, w_in, b_in, w_fc2, out_bias)
        )
    )
    shares = ends[0]
    rounds = shares.shape[0]
    received = jnp.zeros_like(shares[0])
    kept_all = []
    outputs = []
    for moment in range(rounds + 1):
        own_index = min(moment, rounds - 1)
        late_index = max(moment - 1, 0)
        incoming = jnp.where(is_first, shares[own_index], received)
        segment_row = jnp.where(is_first, segments[own_index], segments[late_index])
        result, kept = forward_section(incoming, segment_row, params)
        kept_all.append((segment_row, kept))
        if moment >= 1:
            outputs.append(result.astype(jnp.bfloat16))
        if moment < rounds:
            received = send_ahead(result.astype(jnp.bfloat16))
    returned = jnp.zeros_like(shares[0])
    input_grads = []
    total_grads = None
    for moment in range(rounds + 1):
        early_pick = kept_all[max(moment - 1, 0)]
        late_pick = kept_all[min(moment + 1, rounds)]
        segment_row, kept = jax.tree.map(
            lambda early_part, late_part: jnp.where(is_first, early_part, late_part),
            early_pick,
            late_pick,
        )
        cotangent = jnp.where(is_first, returned, shares[min(moment, rounds - 1)])
        live_step = jnp.where(is_first, moment >= 1, moment < rounds).astype(jnp.float32)
        input_grad, step_grads = backward_section(cotangent, segment_row, params, kept)
        scaled = jax.tree.map(lambda grad_part: grad_part * live_step, step_grads)
        total_grads = scaled if moment == 0 else jax.tree.map(jnp.add, total_grads, scaled)
        if moment >= 1:
            input_grads.append(input_grad.astype(jnp.bfloat16))
        if moment < rounds:
            returned = send_behind(input_grad.astype(jnp.bfloat16))
    boundary = jnp.where(is_first, jnp.stack(input_grads), jnp.stack(outputs))[None]
    (
        gain_grad,
        norm_bias_grad,
        out_bias_grad,
        qkv_weight_grad,
        qkv_bias_grad,
        out_weight_grad,
        in_weight_grad,
        in_bias_grad,
        fc2_weight_grad,
    ) = total_grads
    gain_sum, norm_bias_sum, out_bias_sum = (
        lax.psum_scatter(gain_grad[None], ("tensor", "dp"), scatter_dimension=2, tiled=True),
        lax.psum_scatter(norm_bias_grad[None], ("tensor", "dp"), scatter_dimension=2, tiled=True),
        lax.psum_scatter(out_bias_grad[None], ("tensor", "dp"), scatter_dimension=2, tiled=True),
    )
    qkv_sum, qkv_bias_sum, out_sum, in_sum, in_bias_sum, fc2_sum = (
        lax.psum_scatter(
            qkv_weight_grad[None].astype(jnp.bfloat16), "dp", scatter_dimension=1, tiled=True
        ).astype(jnp.float32),
        lax.psum_scatter(
            qkv_bias_grad[None].astype(jnp.bfloat16), "dp", scatter_dimension=1, tiled=True
        ).astype(jnp.float32),
        lax.psum_scatter(
            out_weight_grad[None].astype(jnp.bfloat16), "dp", scatter_dimension=1, tiled=True
        ).astype(jnp.float32),
        lax.psum_scatter(
            in_weight_grad[None].astype(jnp.bfloat16), "dp", scatter_dimension=1, tiled=True
        ).astype(jnp.float32),
        lax.psum_scatter(
            in_bias_grad[None].astype(jnp.bfloat16), "dp", scatter_dimension=1, tiled=True
        ).astype(jnp.float32),
        lax.psum_scatter(
            fc2_weight_grad[None].astype(jnp.bfloat16), "dp", scatter_dimension=1, tiled=True
        ).astype(jnp.float32),
    )
    return (
        boundary,
        gain_sum,
        norm_bias_sum,
        qkv_sum,
        qkv_bias_sum,
        out_sum,
        in_sum,
        in_bias_sum,
        fc2_sum,
        out_bias_sum,
    )


def solution(mesh):
    placed = (
        P("pipe", "dp", "tensor", None),
        P("dp", None),
        P("pipe", None, None),
        P("pipe", None, None),
        P("pipe", None, "tensor"),
        P("pipe", "tensor"),
        P("pipe", "tensor", None),
        P("pipe", None, "tensor"),
        P("pipe", "tensor"),
        P("pipe", "tensor", None),
        P("pipe", None, None),
    )
    return jax.shard_map(
        body,
        mesh=mesh,
        in_specs=placed,
        out_specs=(
            P("pipe", "dp", "tensor", None),
            P("pipe", None, ("tensor", "dp")),
            P("pipe", None, ("tensor", "dp")),
            P("pipe", "dp", "tensor"),
            P("pipe", ("tensor", "dp")),
            P("pipe", ("tensor", "dp"), None),
            P("pipe", "dp", "tensor"),
            P("pipe", ("tensor", "dp")),
            P("pipe", ("tensor", "dp"), None),
            P("pipe", None, ("tensor", "dp")),
        ),
        check_vma=False,
    )
```

profile of v0, /device:TPU:0, one launch (start us, length us, event | category | flops | bytes accessed | tf_op | source)
XLA Modules:
  0.0 2119.4 jit_solution(5296645789956730730)
XLA Ops:
  26.6 37.1 %all-gather.11.cloned.1.call-done = bf16[1536,1024]{1,0:T(8,128)(2,1)} async-done(((bf16[384,1024]{1,0:T(8,128)(2,1)}), bf16[1536,1024]{1,0:T(8,128)(2,1)}) %all-gather.11.cloned.1.call-update) | async-done | bytes 3145744 | tf_op jit(solution)/shard_map/all_gather | solution.py:174
  80.0 73.1 %while.81 = (s32[]{:T(128)}, bf16[3,512,4,64]{1,0,3,2:T(4,128)(2,1)}, f32[3,4,512]{2,1,0:T(4,128)S(1)}, s32[3]{0:T(128)S(1)}, s32[1536]{0:T(1024)S(1)}, /*index=...) while((s32[]{:T(128)}, ...), condition=%wide.region_7.8_spmd, body=%wide.region_4.7_spmd.sunk | while | flops 845412864 | bytes 47268568 | solution.py:105
  94.1 10.3 dynamic_update_slice.45
  118.5 10.3 dynamic_update_slice.45
  142.8 10.3 dynamic_update_slice.45
  154.7 19.3 fusion.110
  181.8 69.7 %reduce-scatter.29.cloned.1.call-done = f32[384,1024]{1,0:T(8,128)} async-done(((f32[1536,1024]{1,0:T(8,128)}), f32[384,1024]{1,0:T(8,128)}) %reduce-scatter.29.cloned.1.call-update) | async-done | bytes 1572880 | tf_op jit(solution)/shard_map/reduce_scatter | solution.py:187
  261.5 36.4 %all-gather.27.cloned.1.call-done = bf16[1,1,1536,1024]{3,2,1,0:T(8,128)(2,1)} async-done(((bf16[1,1,384,1024]{3,2,1,0:T(8,128)(2,1)}), bf16[1,1,1536,1024]{3,2,1,0:T(8,128)(2,1)}) %all-gather.27.cloned.1.call-update) | async-done | bytes 3145744 | tf_op jit(solution)/shard_map/all_gather | solution.py:228
  306.2 37.4 %all-gather.15.cloned.1.call-done = bf16[1536,1024]{1,0:T(8,128)(2,1)} async-done(((bf16[384,1024]{1,0:T(8,128)(2,1)}), bf16[1536,1024]{1,0:T(8,128)(2,1)}) %all-gather.15.cloned.1.call-update) | async-done | bytes 3145744 | tf_op jit(solution)/shard_map/all_gather | solution.py:174
  369.4 73.9 %while.82 = (s32[]{:T(128)}, bf16[3,512,4,64]{1,0,3,2:T(4,128)(2,1)}, f32[3,4,512]{2,1,0:T(4,128)S(1)}, s32[3]{0:T(128)S(1)}, s32[1536]{0:T(1024)S(1)}, /*index=...) while((s32[]{:T(128)}, ...), condition=%wide.region_16.17_spmd, body=%wide.region_13.16_spmd.sunk | while | flops 845412864 | bytes 47268568 | solution.py:105
  383.7 10.3 dynamic_update_slice.47
  433.0 10.3 dynamic_update_slice.47
  447.3 142.7 %while.84 = (s32[]{:T(128)}, f32[1536,4,64]{0,2,1:T(8,128)}, f32[1536,4,64]{0,2,1:T(8,128)}, f32[3,512,4,64]{1,0,3,2:T(4,128)}, bf16[3,512,4,64]{1,3,2,0:T(8,128...) while((s32[]{:T(128)}, f32[1536,4,64]{0,2,1:T(8,128)}, ...), condition=%wide.region_19.20_spmd.clone, body=%wide.region_17.19_spmd.clone.sunk | while | flops 2046032384 | bytes 168094064 | solution.py:152
  471.2 11.1 dynamic_update_slice.50
  518.1 11.1 dynamic_update_slice.50
  565.8 11.1 dynamic_update_slice.50
  608.1 18.8 fusion.119
  655.2 23.3 %reduce-scatter.31.cloned.1.call-done = f32[384,1024]{1,0:T(8,128)} async-done(((f32[1536,1024]{1,0:T(8,128)}), f32[384,1024]{1,0:T(8,128)}) %reduce-scatter.31.cloned.1.call-update) | async-done | bytes 1572880 | tf_op jit(solution)/shard_map/reduce_scatter | solution.py:263
  678.5 73.2 %reduce-scatter.33.cloned.1.call-done = f32[384,1024]{1,0:T(8,128)} async-done(((f32[1536,1024]{1,0:T(8,128)}), f32[384,1024]{1,0:T(8,128)}) %reduce-scatter.33.cloned.1.call-update) | async-done | bytes 1572880 | tf_op jit(solution)/shard_map/reduce_scatter | solution.py:264
  756.9 68.1 %reduce-scatter.35.cloned.1.call-done = f32[384,1024]{1,0:T(8,128)} async-done(((f32[1536,1024]{1,0:T(8,128)}), f32[384,1024]{1,0:T(8,128)}) %reduce-scatter.35.cloned.1.call-update) | async-done | bytes 1572880 | tf_op jit(solution)/shard_map/reduce_scatter | solution.py:187
  840.5 42.8 %all-gather.19.cloned.1.call-done = bf16[1536,1024]{1,0:T(8,128)(2,1)} async-done(((bf16[384,1024]{1,0:T(8,128)(2,1)}), bf16[1536,1024]{1,0:T(8,128)(2,1)}) %all-gather.19.cloned.1.call-update) | async-done | bytes 3145744 | tf_op jit(solution)/shard_map/all_gather | solution.py:174
  905.2 23.9 %all-gather.23.cloned.1.call-done = bf16[1536,1024]{1,0:T(8,128)(2,1)} async-done(((bf16[384,1024]{1,0:T(8,128)(2,1)}), bf16[1536,1024]{1,0:T(8,128)(2,1)}) %all-gather.23.cloned.1.call-update) | async-done | bytes 3145744 | tf_op jit(solution)/shard_map/all_gather | solution.py:175
  929.1 19.2 fusion.134
  948.3 27.1 %all-gather.21.cloned.1.call-done = bf16[1536,1024]{1,0:T(8,128)(2,1)} async-done(((bf16[384,1024]{1,0:T(8,128)(2,1)}), bf16[1536,1024]{1,0:T(8,128)(2,1)}) %all-gather.21.cloned.1.call-update) | async-done | bytes 3145744 | tf_op jit(solution)/shard_map/all_gather | solution.py:228
  975.4 12.0 convert_reduce_fusion.1
  999.5 74.2 %while.83 = (s32[]{:T(128)}, bf16[3,512,4,64]{1,0,3,2:T(4,128)(2,1)}, f32[3,4,512]{2,1,0:T(4,128)S(1)}, s32[3]{0:T(128)S(1)}, s32[1536]{0:T(1024)S(1)}, /*index=...) while((s32[]{:T(128)}, ...), condition=%wide.region_34.35_spmd, body=%wide.region_31.34_spmd.sunk | while | flops 845412864 | bytes 47268568 | solution.py:105
  1014.0 10.3 dynamic_update_slice.49
  1038.7 10.3 dynamic_update_slice.49
  1063.4 10.3 dynamic_update_slice.49
  1089.1 142.6 %while.85 = (s32[]{:T(128)}, f32[1536,4,64]{0,2,1:T(8,128)}, f32[1536,4,64]{0,2,1:T(8,128)}, f32[3,512,4,64]{1,0,3,2:T(4,128)}, bf16[3,512,4,64]{1,3,2,0:T(8,128...) while((s32[]{:T(128)}, f32[1536,4,64]{0,2,1:T(8,128)}, ...), condition=%wide.region_37.38_spmd.clone, body=%wide.region_35.37_spmd.clone.sunk | while | flops 2046032384 | bytes 168094064 | solution.py:152
  1112.8 11.1 dynamic_update_slice.51
  1159.7 11.1 dynamic_update_slice.51
  1207.5 11.1 dynamic_update_slice.51
  1260.8 59.3 %reduce-scatter.37.cloned.1.call-done = f32[384,1024]{1,0:T(8,128)} async-done(((f32[1536,1024]{1,0:T(8,128)}), f32[384,1024]{1,0:T(8,128)}) %reduce-scatter.37.cloned.1.call-update) | async-done | bytes 1572880 | tf_op jit(solution)/shard_map/reduce_scatter | solution.py:263
  1325.2 67.9 %reduce-scatter.45.cloned.1.call-done = f32[384,1024]{1,0:T(8,128)} async-done(((f32[1536,1024]{1,0:T(8,128)}), f32[384,1024]{1,0:T(8,128)}) %reduce-scatter.45.cloned.1.call-update) | async-done | bytes 1572880 | tf_op jit(solution)/shard_map/reduce_scatter | solution.py:187
  1418.8 27.6 %all-gather.25.cloned.1.call-done = bf16[1536,1024]{1,0:T(8,128)(2,1)} async-done(((bf16[384,1024]{1,0:T(8,128)(2,1)}), bf16[1536,1024]{1,0:T(8,128)(2,1)}) %all-gather.25.cloned.1.call-update) | async-done | bytes 3145744 | tf_op jit(solution)/shard_map/all_gather | solution.py:228
  1459.0 144.1 %while.86 = (s32[]{:T(128)}, f32[1536,4,64]{0,2,1:T(8,128)}, f32[1536,4,64]{0,2,1:T(8,128)}, f32[3,512,4,64]{1,0,3,2:T(4,128)}, bf16[3,512,4,64]{1,3,2,0:T(8,128...) while((s32[]{:T(128)}, f32[1536,4,64]{0,2,1:T(8,128)}, ...), condition=%wide.region_46.47_spmd.clone, body=%wide.region_44.46_spmd.clone.sunk | while | flops 2046032384 | bytes 164948304 | solution.py:152
  1483.1 11.1 dynamic_update_slice.52
  1530.6 11.1 dynamic_update_slice.52
  1578.9 11.1 dynamic_update_slice.52
  1616.1 12.7 convert_reduce_fusion
  1698.2 17.5 reduce-scatter.47.cloned.1.call-done
  1717.6 43.3 %reduce-scatter.53.cloned.1.call-done = bf16[1,256,1024]{2,1,0:T(8,128)(2,1)} async-done(((bf16[1,1024,1024]{2,1,0:T(8,128)(2,1)}), bf16[1,256,1024]{2,1,0:T(8,128)(2,1)}) %reduce-scatter.53.cloned.1.call-update) | async-done | bytes 524304 | tf_op jit(solution)/shard_map/reduce_scatter | solution.py:372
  1763.1 43.4 %reduce-scatter.51.cloned.1.call-done = bf16[1,256,1024]{2,1,0:T(8,128)(2,1)} async-done(((bf16[1,1024,1024]{2,1,0:T(8,128)(2,1)}), bf16[1,256,1024]{2,1,0:T(8,128)(2,1)}) %reduce-scatter.51.cloned.1.call-update) | async-done | bytes 524304 | tf_op jit(solution)/shard_map/reduce_scatter | solution.py:366
  1808.7 70.5 %reduce-scatter.43.cloned.1.call-done = f32[384,1024]{1,0:T(8,128)} async-done(((f32[1536,1024]{1,0:T(8,128)}), f32[384,1024]{1,0:T(8,128)}) %reduce-scatter.43.cloned.1.call-update) | async-done | bytes 1572880 | tf_op jit(solution)/shard_map/reduce_scatter | solution.py:264
  1879.1 73.5 %reduce-scatter.41.cloned.1.call-done = f32[384,1024]{1,0:T(8,128)} async-done(((f32[1536,1024]{1,0:T(8,128)}), f32[384,1024]{1,0:T(8,128)}) %reduce-scatter.41.cloned.1.call-update) | async-done | bytes 1572880 | tf_op jit(solution)/shard_map/reduce_scatter | solution.py:263
  1963.8 71.6 %reduce-scatter.57.cloned.1.call-done = f32[64,2]{1,0:T(8,128)} async-done(((f32[1024,2]{1,0:T(8,128)}), f32[64,2]{1,0:T(8,128)}) %reduce-scatter.57.cloned.1.call-update) | async-done | bytes 528
  2036.8 74.1 %reduce-scatter.55.cloned.1.call-done = f32[64,2]{1,0:T(8,128)} async-done(((f32[1024,2]{1,0:T(8,128)}), f32[64,2]{1,0:T(8,128)}) %reduce-scatter.55.cloned.1.call-update) | async-done | bytes 528
  (924 shorter events, 837.1 us)
Async XLA Ops:
  7.2 56.5 %all-gather.11.cloned.1.call-start = ((), (), s32[]{:S(2)}) async-start(), calls=%async_computation.18 | async-start | bytes 3932160 | tf_op jit(solution)/shard_map/all_gather | solution.py:174
  16.8 137.8 %all-gather.13.cloned.1.call-start = ((), (), s32[]{:S(2)}) async-start(), calls=%async_computation.19 | async-start | bytes 3932160 | tf_op jit(solution)/shard_map/all_gather | solution.py:175
  17.6 234.0 %reduce-scatter.29.cloned.1.call-start = ((), (), s32[]{:S(2)}) async-start(), calls=%async_computation.20 | async-start | bytes 7864320 | tf_op jit(solution)/shard_map/reduce_scatter | solution.py:187
  181.2 116.7 %all-gather.27.cloned.1.call-start = ((), (), s32[]{:S(2)}) async-start(), calls=%async_computation.39 | async-start | bytes 3932160 | tf_op jit(solution)/shard_map/all_gather | solution.py:228
  181.7 161.8 %all-gather.15.cloned.1.call-start = ((), (), s32[]{:S(2)}) async-start(), calls=%async_computation.21 | async-start | bytes 3932160 | tf_op jit(solution)/shard_map/all_gather | solution.py:174
  253.7 3.8 collective-permute-start
  260.4 347.1 %all-gather.17.cloned.1.call-start = ((), (), s32[]{:S(2)}) async-start(), calls=%async_computation.23 | async-start | bytes 3932160 | tf_op jit(solution)/shard_map/all_gather | solution.py:175
  305.9 372.6 %reduce-scatter.31.cloned.1.call-start = ((), (), s32[]{:S(2)}) async-start(), calls=%async_computation.22 | async-start | bytes 7864320 | tf_op jit(solution)/shard_map/reduce_scatter | solution.py:263
  607.4 144.3 %reduce-scatter.33.cloned.1.call-start = ((), (), s32[]{:S(2)}) async-start(), calls=%async_computation.24 | async-start | bytes 7864320 | tf_op jit(solution)/shard_map/reduce_scatter | solution.py:264
  643.8 181.2 %reduce-scatter.35.cloned.1.call-start = ((), (), s32[]{:S(2)}) async-start(), calls=%async_computation.25 | async-start | bytes 7864320 | tf_op jit(solution)/shard_map/reduce_scatter | solution.py:187
  655.2 169.8 %copy-start.119 = (f32[1,1,1024]{2,1,0:T(1,128)S(1)}, f32[1,1,1024]{2,1,0:T(1,128)}, u32[]{:S(2)}) copy-start(f32[1,1,1024]{2,1,0:T(1,128)} %copy-done.118) | copy-start | bytes 12292
  655.2 169.8 %copy-start.122 = (f32[1,1,1024]{2,1,0:T(1,128)S(1)}, f32[1,1,1024]{2,1,0:T(1,128)}, u32[]{:S(2)}) copy-start(f32[1,1,1024]{2,1,0:T(1,128)} %copy-done.121) | copy-start | bytes 12292
  655.2 169.8 %copy-start.150 = (f32[384]{0:T(512)S(1)}, f32[384]{0:T(512)}, u32[]{:S(2)}) copy-start(f32[384]{0:T(512)} %get-tuple-element.909) | copy-start | bytes 4612
  655.2 228.1 %all-gather.19.cloned.1.call-start = ((), (), s32[]{:S(2)}) async-start(), calls=%async_computation.26 | async-start | bytes 3932160 | tf_op jit(solution)/shard_map/all_gather | solution.py:174
  828.1 4.6 collective-permute-start.1
  829.5 5.0 collective-permute-start.2
  839.1 90.0 %all-gather.23.cloned.1.call-start = ((), (), s32[]{:S(2)}) async-start(), calls=%async_computation.29 | async-start | bytes 3932160 | tf_op jit(solution)/shard_map/all_gather | solution.py:175
  839.8 135.6 %all-gather.21.cloned.1.call-start = ((), (), s32[]{:S(2)}) async-start(), calls=%async_computation.27 | async-start | bytes 3932160 | tf_op jit(solution)/shard_map/all_gather | solution.py:228
  840.4 420.3 %reduce-scatter.39.cloned.1.call-start = ((), (), s32[]{:S(2)}) async-start(), calls=%async_computation.30 | async-start | bytes 7864320 | tf_op jit(solution)/shard_map/reduce_scatter | solution.py:264
  994.6 325.5 %reduce-scatter.37.cloned.1.call-start = ((), (), s32[]{:S(2)}) async-start(), calls=%async_computation.28 | async-start | bytes 7864320 | tf_op jit(solution)/shard_map/reduce_scatter | solution.py:263
  1249.4 143.8 %reduce-scatter.45.cloned.1.call-start = ((), (), s32[]{:S(2)}) async-start(), calls=%async_computation.34 | async-start | bytes 7864320 | tf_op jit(solution)/shard_map/reduce_scatter | solution.py:187
  1260.7 185.7 %all-gather.25.cloned.1.call-start = ((), (), s32[]{:S(2)}) async-start(), calls=%async_computation.31 | async-start | bytes 3932160 | tf_op jit(solution)/shard_map/all_gather | solution.py:228
  1396.9 4.2 collective-permute-start.3
  1402.2 290.0 %reduce-scatter.63.cloned.1.call-start = ((), (), s32[]{:S(2)}) async-start(), calls=%async_computation.44 | async-start | bytes 557056
  1418.7 274.9 %reduce-scatter.59.cloned.1.call-start = ((), (), s32[]{:S(2)}) async-start(), calls=%async_computation.42 | async-start | bytes 245760
  1616.0 79.0 %reduce-scatter.61.cloned.1.call-start = ((), (), s32[]{:S(2)}) async-start(), calls=%async_computation.43 | async-start | bytes 327680
  1629.7 66.9 %reduce-scatter.49.cloned.1.call-start = ((), (), s32[]{:S(2)}) async-start(), calls=%async_computation.36 | async-start | bytes 655360 | tf_op jit(solution)/shard_map/reduce_scatter | solution.py:363
  1633.7 81.9 %reduce-scatter.47.cloned.1.call-start = ((), (), s32[]{:S(2)}) async-start(), calls=%async_computation.35 | async-start | bytes 1966080 | tf_op jit(solution)/shard_map/reduce_scatter | solution.py:357
  1646.5 114.4 %reduce-scatter.53.cloned.1.call-start = ((), (), s32[]{:S(2)}) async-start(), calls=%async_computation.38 | async-start | bytes 2621440 | tf_op jit(solution)/shard_map/reduce_scatter | solution.py:372
  1661.5 144.9 %reduce-scatter.51.cloned.1.call-start = ((), (), s32[]{:S(2)}) async-start(), calls=%async_computation.37 | async-start | bytes 2621440 | tf_op jit(solution)/shard_map/reduce_scatter | solution.py:366
  1676.8 202.3 %reduce-scatter.43.cloned.1.call-start = ((), (), s32[]{:S(2)}) async-start(), calls=%async_computation.33 | async-start | bytes 7864320 | tf_op jit(solution)/shard_map/reduce_scatter | solution.py:264
  1684.2 268.4 %reduce-scatter.41.cloned.1.call-start = ((), (), s32[]{:S(2)}) async-start(), calls=%async_computation.32 | async-start | bytes 7864320 | tf_op jit(solution)/shard_map/reduce_scatter | solution.py:263
  1691.8 260.8 %copy-start.18 = (bf16[384,1024]{1,0:T(8,128)(2,1)S(1)}, bf16[384,1024]{1,0:T(8,128)(2,1)}, u32[]{:S(2)}) copy-start(bf16[384,1024]{1,0:T(8,128)(2,1)} %copy-done.16) | copy-start | bytes 2359300
  1691.9 260.8 %copy-start.83 = (f32[1,1,1024]{2,1,0:T(1,128)S(1)}, f32[1,1,1024]{2,1,0:T(1,128)}, u32[]{:S(2)}) copy-start(f32[1,1,1024]{2,1,0:T(1,128)} %copy-done.79) | copy-start | bytes 12292
  1691.9 260.8 %copy-start.88 = (f32[1,1,1024]{2,1,0:T(1,128)S(1)}, f32[1,1,1024]{2,1,0:T(1,128)}, u32[]{:S(2)}) copy-start(f32[1,1,1024]{2,1,0:T(1,128)} %copy-done.84) | copy-start | bytes 12292
  1691.9 260.8 %copy-start.102 = (f32[384]{0:T(512)S(1)}, f32[384]{0:T(512)}, u32[]{:S(2)}) copy-start(f32[384]{0:T(512)} %copy-done.100) | copy-start | bytes 4612
  1691.9 260.8 %copy-start.105 = (f32[384]{0:T(512)S(1)}, f32[384]{0:T(512)}, u32[]{:S(2)}) copy-start(f32[384]{0:T(512)} %copy-done.103) | copy-start | bytes 4612
  1691.9 260.8 %copy-start.111 = (f32[384]{0:T(512)S(1)}, f32[384]{0:T(512)}, u32[]{:S(2)}) copy-start(f32[384]{0:T(512)} %copy-done.109) | copy-start | bytes 4612
  1691.9 260.8 %copy-start.114 = (f32[384]{0:T(512)S(1)}, f32[384]{0:T(512)}, u32[]{:S(2)}) copy-start(f32[384]{0:T(512)} %copy-done.112) | copy-start | bytes 4612
  1691.9 343.5 %reduce-scatter.57.cloned.1.call-start = ((), (), s32[]{:S(2)}) async-start(), calls=%async_computation.41 | async-start | bytes 557056
  1808.6 148.6 %copy-start.143 = (f32[1024]{0:T(1024)S(1)}, f32[1024]{0:T(1024)}, u32[]{:S(2)}) copy-start(f32[1024]{0:T(1024)} %get-tuple-element.657) | copy-start | bytes 12292
  1808.6 148.6 %copy-start.144 = (f32[1024]{0:T(1024)S(1)}, f32[1024]{0:T(1024)}, u32[]{:S(2)}) copy-start(f32[1024]{0:T(1024)} %get-tuple-element.659) | copy-start | bytes 12292
  1808.6 149.8 %copy-start.137 = (f32[1024]{0:T(1024)S(1)}, f32[1024]{0:T(1024)}, u32[]{:S(2)}) copy-start(f32[1024]{0:T(1024)} %get-tuple-element.646) | copy-start | bytes 12292
  1808.6 149.8 %copy-start.138 = (f32[1024]{0:T(1024)S(1)}, f32[1024]{0:T(1024)}, u32[]{:S(2)}) copy-start(f32[1024]{0:T(1024)} %get-tuple-element.647) | copy-start | bytes 12292
  1808.6 149.8 %copy-start.141 = (f32[1024]{0:T(1024)S(1)}, f32[1024]{0:T(1024)}, u32[]{:S(2)}) copy-start(f32[1024]{0:T(1024)} %get-tuple-element.643) | copy-start | bytes 12292
  1808.6 149.8 %copy-start.142 = (f32[1024]{0:T(1024)S(1)}, f32[1024]{0:T(1024)}, u32[]{:S(2)}) copy-start(f32[1024]{0:T(1024)} %get-tuple-element.644) | copy-start | bytes 12292
  1808.7 150.9 %copy-start.148 = (f32[384]{0:T(512)S(1)}, f32[384]{0:T(512)}, u32[]{:S(2)}) copy-start(f32[384]{0:T(512)} %get-tuple-element.906) | copy-start | bytes 4612
  1958.3 152.6 %reduce-scatter.55.cloned.1.call-start = ((), (), s32[]{:S(2)}) async-start(), calls=%async_computation.40 | async-start | bytes 557056
  (194 other events, 3770.2 us)
Sparse Core Ops, SparseCore 0:
  17.0 46.6 all-gather.10
  66.1 43.9 all-gather.12
  181.3 70.2 reduce-scatter.28
  253.8 43.9 all-gather.26
  299.5 43.9 all-gather.14
  345.2 43.9 all-gather.16
  607.6 70.9 reduce-scatter.30
  681.5 70.1 reduce-scatter.32
  754.7 70.1 reduce-scatter.34
  839.2 43.9 all-gather.18
  885.1 43.9 all-gather.22
  931.4 43.9 all-gather.20
  994.8 70.2 reduce-scatter.38
  1249.5 70.5 reduce-scatter.36
  1322.9 70.2 reduce-scatter.44
  1402.4 43.9 all-gather.24
  1448.4 77.1 reduce-scatter.62
  1616.1 19.4 reduce-scatter.58
  1638.4 17.7 reduce-scatter.60
  1659.0 19.9 reduce-scatter.48
  1682.0 33.6 reduce-scatter.46
  1718.1 42.8 reduce-scatter.52
  1763.2 43.1 reduce-scatter.50
  1809.6 69.5 reduce-scatter.42
  1882.4 70.1 reduce-scatter.40
  1958.4 76.9 reduce-scatter.56
  2037.5 73.3 reduce-scatter.54
where the time goes:
time: 2130 us; the launch traced here: 2120 us
  waiting for transfers between devices  997 us (47%)
  matrix products  542 us (25%)
  local copies, waits for them, and re-layouts  361 us (17%)
  other arithmetic  179 us (8%)
    reduce_scatter x3, waiting for transfers between devices, forward_section(): lax.psum_scatter(jnp.dot(mixed, out_weight, preferred_element_type=jnp.fl...  206 us
    dynamic_update_slice x36, local copies, waits for them, and re-layouts, attend_forward(): lax.map(one_block, (jnp.arange(blocks, dtype=jnp.int32), queries.reshape(...  201 us
    reduce_scatter x3, waiting for transfers between devices, backward_section(): lax.psum_scatter(one_grad, 'tensor', scatter_dimension=0, tiled=True)  156 us
    unnamed x32, waiting for transfers between devices  149 us
    reduce_scatter x3, waiting for transfers between devices, backward_section(): lax.psum_scatter(two_grad, 'tensor', scatter_dimension=0, tiled=True)  144 us
    all_gather x3, waiting for transfers between devices, forward_section(): lax.all_gather(one_share, 'tensor', axis=0, tiled=True)  117 us
    dot_general x27, matrix products, pair_products(): jnp.einsum('qhd,khd->hqk', left_block, right_whole, preferred_element_typ...  109 us
    all_gather x3, waiting for transfers between devices, backward_section(): grad_whole = lax.all_gather(grad_share, 'tensor', axis=0, tiled=True)  91.1 us
  transfers between devices with their start and end apart: 31, of which 23 were waited for; matrix products, arithmetic and copies ran while one was open for 46% of the time, Pallas kernels for 0%

commit v1 on v0

v1 whole, which is shorter than its diff:
```python
import functools
import math

import jax
import jax.numpy as jnp
from jax import lax
from jax.experimental import pallas as pl
from jax.experimental.pallas import tpu as pltpu
from jax.sharding import PartitionSpec as P

HEAD_DIM = 64
ROT = 16
EPSILON = 1e-05
MASKED = -1e30
TILE = 256
SUB = 128
LANES = 128
BF = jnp.bfloat16
F32 = jnp.float32

VM = pltpu.VMEM
NT = (((1,), (1,)), ((), ()))
TN = (((0,), (0,)), ((), ()))


def dot_nn(a, b):
    return jnp.dot(a, b, preferred_element_type=F32)


def dot_nt(a, b):
    return lax.dot_general(a, b, NT, preferred_element_type=F32)


def dot_tn(a, b):
    return lax.dot_general(a, b, TN, preferred_element_type=F32)


def whole(shape):
    return pl.BlockSpec(shape, lambda *_: (0,) * len(shape))


SMEM_SPEC = pl.BlockSpec(memory_space=pltpu.SMEM)
ANY_SPEC = pl.BlockSpec(memory_space=pl.ANY)
PARAMS = pltpu.CompilerParams(vmem_limit_bytes=56 * 1024 * 1024)


def norm_rows(rows):
    centre = jnp.mean(rows, axis=-1, keepdims=True)
    shifted = rows - centre
    inverse_std = lax.rsqrt(jnp.mean(shifted * shifted, axis=-1, keepdims=True) + EPSILON)
    return shifted * inverse_std, inverse_std


def turn(values, tables, direction):
    cos_t, sin_a, sin_b = tables
    width = values.shape[-1]
    times = width // LANES
    wide = lambda t: jnp.concatenate([t] * times, axis=1)
    ahead = pltpu.roll(values, width - ROT // 2, 1)
    behind = pltpu.roll(values, ROT // 2, 1)
    return values * wide(cos_t) + direction * (ahead * wide(sin_a) + behind * wide(sin_b))


def pre_kernel(n_alias, x_ref, gain_ref, bias_ref, wqkv_ref, bqkv_ref, win_ref, bin_ref,
               cos_ref, sa_ref, sb_ref, *rest):
    n1_ref, n2_ref, q_ref, k_ref, v_ref, g_ref, slope_ref, n2_keep = rest[n_alias:]

    @pl.when(pl.program_id(0) == 0)
    def _():
        normal, _ = norm_rows(x_ref[...].astype(F32))
        gains = gain_ref[...].astype(F32)
        biases = bias_ref[...].astype(F32)
        n1 = (normal * gains[0:1] + biases[0:1]).astype(BF)
        n2 = (normal * gains[1:2] + biases[1:2]).astype(BF)
        n1_ref[0] = n1
        n2_ref[0] = n2
        n2_keep[...] = n2
        tables = (cos_ref[...], sa_ref[...], sb_ref[...])
        wide = q_ref.shape[-1]
        scale = 1.0 / math.sqrt(HEAD_DIM)
        bq = bqkv_ref[...].astype(F32)
        part = lambda i: dot_nn(n1, wqkv_ref[:, i * wide:(i + 1) * wide]) + bq[:, i * wide:(i + 1) * wide]
        q_ref[0] = (turn(part(0), tables, 1.0).astype(BF).astype(F32) * scale).astype(BF)
        k_ref[0] = turn(part(1), tables, 1.0).astype(BF)
        v_ref[0] = part(2).astype(BF)

    f = dot_nn(n2_keep[...], win_ref[...]) + bin_ref[...].astype(F32)
    phi = 0.5 * (1.0 + lax.erf(f * (1.0 / math.sqrt(2.0))))
    density = jnp.exp(-0.5 * f * f) * (1.0 / math.sqrt(2.0 * math.pi))
    g_ref[0] = (f * phi).astype(BF)
    slope_ref[0] = (phi + f * density).astype(BF)


def slot_call(kernel, slot, args, in_specs, outs, kept, grid, scratch):
    n_alias = 0 if kept is None else len(outs)
    specs = list(in_specs)
    operands = list(args)
    aliases = {}
    if kept is not None:
        for i, buf in enumerate(kept):
            aliases[len(operands)] = i
            operands.append(buf)
            specs.append(ANY_SPEC)
    return pl.pallas_call(
        functools.partial(kernel, n_alias),
        grid=grid,
        in_specs=specs,
        out_specs=[pl.BlockSpec(block, index) for _, _, block, index in outs],
        out_shape=[jax.ShapeDtypeStruct(shape, dtype) for shape, dtype, _, _ in outs],
        input_output_aliases=aliases,
        scratch_shapes=scratch,
        compiler_params=PARAMS,
    )(*operands)


def pre_slot(slot, slots, x, lp, tables, kept):
    rows, d = x.shape
    wide = lp["w_qkv"].shape[1]
    units = lp["w_in"].shape[1]
    cols = wide // 3
    ck = min(TILE, units)
    first = lambda j: (slot, 0, 0)
    moving = lambda j: (slot, 0, j)
    outs = [((slots, rows, d), BF, (1, rows, d), first)] * 2
    outs += [((slots, rows, cols), BF, (1, rows, cols), first)] * 3
    outs += [((slots, rows, units), BF, (1, rows, ck), moving)] * 2
    in_specs = [whole((rows, d)), whole((2, d)), whole((2, d)), whole((d, wide)), whole((1, wide)),
                pl.BlockSpec((d, ck), lambda j: (0, j)), pl.BlockSpec((1, ck), lambda j: (0, j))]
    in_specs += [pl.BlockSpec((None, rows, LANES), first)] * 3
    args = [x, lp["ln_gain"], lp["ln_bias"], lp["w_qkv"], lp["b_qkv"], lp["w_in"], lp["b_in"], *tables]
    return slot_call(pre_kernel, slot, args, in_specs, outs, kept, (units // ck,), [VM((rows, d), BF)])


def post_kernel(half, o_ref, g_ref, wout_ref, wfc_ref, *rest):
    out_ref = rest[-1]
    part = dot_nn(o_ref[...], wout_ref[...]) + dot_nn(g_ref[...], wfc_ref[...])
    out_ref[...] = part.astype(out_ref.dtype)
    if half is not None:
        rows = rest[0].shape[0]
        at = half * rows
        summed = part[at:at + rows] + rest[0][...].astype(F32)
        out_ref[at:at + rows, :] = summed.astype(out_ref.dtype)


def post_slot(slot, o_all, g_all, lp, half, addend, dtype):
    _, rows, cols = o_all.shape
    units, d = lp["w_fc2"].shape
    ck = min(TILE, d)
    fixed = lambda j: (slot, 0, 0)
    in_specs = [pl.BlockSpec((None, rows, cols), fixed), pl.BlockSpec((None, rows, units), fixed),
                pl.BlockSpec((cols, ck), lambda j: (0, j)), pl.BlockSpec((units, ck), lambda j: (0, j))]
    args = [o_all, g_all, lp["w_out"], lp["w_fc2"]]
    if half is not None:
        in_specs.append(pl.BlockSpec((rows // 2, ck), lambda j: (0, j)))
        args.append(addend)
    return pl.pallas_call(
        functools.partial(post_kernel, half),
        grid=(d // ck,),
        in_specs=in_specs,
        out_specs=pl.BlockSpec((rows, ck), lambda j: (0, j)),
        out_shape=jax.ShapeDtypeStruct((rows, d), dtype),
        compiler_params=PARAMS,
    )(*args)


def bpre_kernel(n_alias, e_ref, wout_ref, wfc_ref, slope_ref, *rest):
    eall_ref, do_ref, df_ref, sums_ref = rest[n_alias:]

    @pl.when(pl.program_id(0) == 0)
    def _():
        eall_ref[0] = e_ref[...]
        do_ref[0] = dot_nt(e_ref[...], wout_ref[...]).astype(BF)

    df = (dot_nt(e_ref[...], wfc_ref[...]) * slope_ref[...].astype(F32)).astype(BF)
    df_ref[0] = df
    sums_ref[0] = jnp.sum(df.astype(F32), axis=0, keepdims=True)


def bpre_slot(slot, slots, e, slope_all, lp, kept):
    rows, d = e.shape
    cols = lp["w_out"].shape[0]
    units = lp["w_fc2"].shape[0]
    ck = min(TILE, units)
    first = lambda j: (slot, 0, 0)
    moving = lambda j: (slot, 0, j)
    outs = [((slots, rows, d), BF, (1, rows, d), first), ((slots, rows, cols), BF, (1, rows, cols), first),
            ((slots, rows, units), BF, (1, rows, ck), moving), ((slots, 1, units), F32, (1, 1, ck), moving)]
    in_specs = [whole((rows, d)), whole((cols, d)), pl.BlockSpec((ck, d), lambda j: (j, 0)),
                pl.BlockSpec((None, rows, ck), moving)]
    args = [e, lp["w_out"], lp["w_fc2"], slope_all]
    return slot_call(bpre_kernel, slot, args, in_specs, outs, kept, (units // ck,), [])


def bpost_kernel(half, ck, x_ref, gain_ref, dqkv_ref, df_ref, wqkv_ref, win_ref, *rest):
    out_ref, sums_ref, normal_keep = rest[-3:]
    j = pl.program_id(0)

    @pl.when(j == 0)
    def _():
        normal, _ = norm_rows(x_ref[...].astype(F32))
        for c in range(normal_keep.shape[0]):
            normal_keep[c] = normal[:, c * ck:(c + 1) * ck]

    one = dot_nt(dqkv_ref[...], wqkv_ref[...])
    two = dot_nt(df_ref[...], win_ref[...])
    normal = normal_keep[j]
    total = lambda v: jnp.sum(v, axis=0, keepdims=True)
    sums_ref[0:1, :] = total(one * normal)
    sums_ref[1:2, :] = total(two * normal)
    sums_ref[2:3, :] = total(one)
    sums_ref[3:4, :] = total(two)
    gains = gain_ref[...].astype(F32)
    part = one * gains[0:1] + two * gains[1:2]
    out_ref[...] = part.astype(out_ref.dtype)
    if half is not None:
        rows = rest[0].shape[0]
        at = half * rows
        summed = part[at:at + rows] + rest[0][...].astype(F32)
        out_ref[at:at + rows, :] = summed.astype(out_ref.dtype)


def bpost_slot(slot, x, dqkv_all, df_all, lp, half, addend, dtype):
    rows, d = x.shape
    wide = dqkv_all.shape[-1]
    units = df_all.shape[-1]
    ck = min(TILE, d)
    fixed = lambda j: (slot, 0, 0)
    in_specs = [whole((rows, d)), pl.BlockSpec((2, ck), lambda j: (0, j)),
                pl.BlockSpec((None, rows, wide), fixed), pl.BlockSpec((None, rows, units), fixed),
                pl.BlockSpec((ck, wide), lambda j: (j, 0)), pl.BlockSpec((ck, units), lambda j: (j, 0))]
    args = [x, lp["ln_gain"], dqkv_all, df_all, lp["w_qkv"], lp["w_in"]]
    if half is not None:
        in_specs.append(pl.BlockSpec((rows // 2, ck), lambda j: (0, j)))
        args.append(addend)
    return pl.pallas_call(
        functools.partial(bpost_kernel, half, ck),
        grid=(d // ck,),
        in_specs=in_specs,
        out_specs=[pl.BlockSpec((rows, ck), lambda j: (0, j)), pl.BlockSpec((4, ck), lambda j: (0, j))],
        out_shape=[jax.ShapeDtypeStruct((rows, d), dtype), jax.ShapeDtypeStruct((4, d), F32)],
        scratch_shapes=[VM((d // ck, rows, ck), F32)],
        compiler_params=PARAMS,
    )(*args)


def head_lanes(shape):
    return lax.broadcasted_iota(jnp.int32, shape, len(shape) - 1) // HEAD_DIM


def by_head(columns, shape):
    group = head_lanes(shape)
    out = jnp.broadcast_to(columns[0], shape)
    for h in range(1, len(columns)):
        out = jnp.where(group == h, columns[h], out)
    return out


def attend_kernel(order_ref, low_ref, q_ref, k_ref, v_ref, start_ref, o_ref, lse_ref,
                  k_abs, v_abs, acc, top, tot):
    subs, _, cols = q_ref.shape
    heads = cols // HEAD_DIM
    per = TILE // SUB
    for i in range(subs):
        src = order_ref[i]
        k_abs[i * SUB:(i + 1) * SUB, :] = k_ref[src]
        v = v_ref[src]
        for h in range(heads):
            v_abs[h, i * SUB:(i + 1) * SUB, :] = jnp.where(head_lanes(v.shape) == h, v, jnp.zeros_like(v))

    def one_query(qb, _):
        q = jnp.concatenate([q_ref[order_ref[qb * per + u]] for u in range(per)], axis=0)
        base = pl.multiple_of(qb * TILE, TILE)
        starts = start_ref[pl.ds(base, TILE), 0:1]
        places = base + lax.broadcasted_iota(jnp.int32, (TILE, 1), 0)
        group = head_lanes(q.shape)
        qs = [jnp.where(group == h, q, jnp.zeros_like(q)) for h in range(heads)]
        lane = lax.broadcasted_iota(jnp.int32, (TILE, TILE), 1)

        def scores(kb):
            at = pl.multiple_of(kb * TILE, TILE)
            keys = k_abs[pl.ds(at, TILE), :]
            allowed = jnp.logical_and(lane + at >= starts, lane + at <= places)
            return at, [jnp.where(allowed, dot_nt(qs[h], keys), MASKED) for h in range(heads)]

        at, found = scores(qb)
        mixed = None
        for h in range(heads):
            m = jnp.max(found[h], axis=1, keepdims=True)
            p = jnp.exp(found[h] - m)
            top[h] = m
            tot[h] = jnp.sum(p, axis=1, keepdims=True)
            pv = dot_nn(p.astype(BF), v_abs[h, pl.ds(at, TILE), :])
            mixed = pv if mixed is None else mixed + pv
        acc[...] = mixed

        def one_key(kb, _):
            at, found = scores(kb)
            fades = []
            mixed = None
            for h in range(heads):
                old = top[h]
                m = jnp.maximum(old, jnp.max(found[h], axis=1, keepdims=True))
                fade = jnp.exp(old - m)
                p = jnp.exp(found[h] - m)
                top[h] = m
                tot[h] = tot[h] * fade + jnp.sum(p, axis=1, keepdims=True)
                pv = dot_nn(p.astype(BF), v_abs[h, pl.ds(at, TILE), :])
                mixed = pv if mixed is None else mixed + pv
                fades.append(fade)
            acc[...] = acc[...] * by_head(fades, (TILE, cols)) + mixed
            return 0

        lax.fori_loop(low_ref[qb], qb, one_key, 0)
        out = (acc[...] / by_head([tot[h] for h in range(heads)], (TILE, cols))).astype(BF)
        for u in range(per):
            o_ref[order_ref[qb * per + u]] = out[u * SUB:(u + 1) * SUB]
        which = lax.broadcasted_iota(jnp.int32, (TILE, LANES), 1)
        logs = jnp.zeros((TILE, LANES), F32)
        for h in range(heads):
            logs = jnp.where(which == h, top[h] + jnp.log(tot[h]), logs)
        lse_ref[pl.ds(base, TILE), :] = logs
        return 0

    lax.fori_loop(0, subs // per, one_query, 0)


def attend(order, low, q, k, v, start_cols):
    subs, _, cols = q.shape
    length = subs * SUB
    heads = cols // HEAD_DIM
    full = [whole(a.shape) for a in (q, k, v, start_cols)]
    return pl.pallas_call(
        attend_kernel,
        grid=(1,),
        in_specs=[SMEM_SPEC, SMEM_SPEC] + full,
        out_specs=[whole(q.shape), whole((length, LANES))],
        out_shape=[jax.ShapeDtypeStruct(q.shape, BF), jax.ShapeDtypeStruct((length, LANES), F32)],
        scratch_shapes=[VM((length, cols), BF), VM((heads, length, cols), BF), VM((TILE, cols), F32),
                        VM((heads, TILE, 1), F32), VM((heads, TILE, 1), F32)],
        compiler_params=PARAMS,
    )(order, low, q, k, v, start_cols)


def attend_back_kernel(order_ref, low_ref, q_ref, k_ref, v_ref, do_ref, o_ref, lse_ref, start_ref,
                       cos_ref, sa_ref, sb_ref, out_ref, sums_ref,
                       k_abs, v_abs, km, dk, dv, dq, qm, dom, stat):
    subs, _, cols = q_ref.shape
    heads = cols // HEAD_DIM
    per = TILE // SUB
    scale = 1.0 / math.sqrt(HEAD_DIM)
    for i in range(subs):
        src = order_ref[i]
        rows = slice(i * SUB, (i + 1) * SUB)
        key = k_ref[src]
        k_abs[rows, :] = key
        v_abs[rows, :] = v_ref[src]
        for h in range(heads):
            km[h, rows, :] = jnp.where(head_lanes(key.shape) == h, key, jnp.zeros_like(key))
        dk[rows, :] = jnp.zeros((SUB, cols), F32)
        dv[rows, :] = jnp.zeros((SUB, cols), F32)
    sums_ref[...] = jnp.zeros(sums_ref.shape, F32)

    def tables(src):
        return cos_ref[src], sa_ref[src], sb_ref[src]

    def emit(src, at, values):
        low = values.astype(BF)
        out_ref[src, :, at:at + cols] = low
        sums_ref[:, at:at + cols] += jnp.sum(low.astype(F32), axis=0, keepdims=True)

    def one_query(qb, _):
        base = pl.multiple_of(qb * TILE, TILE)
        srcs = [order_ref[qb * per + u] for u in range(per)]
        q = jnp.concatenate([q_ref[s] for s in srcs], axis=0)
        do = jnp.concatenate([do_ref[s] for s in srcs], axis=0)
        o = jnp.concatenate([o_ref[s] for s in srcs], axis=0)
        group = head_lanes(q.shape)
        logs = jnp.transpose(lse_ref[pl.ds(base, TILE), :])
        inner = jnp.transpose(do.astype(F32) * o.astype(F32))
        for h in range(heads):
            qm[h] = jnp.where(group == h, q, jnp.zeros_like(q))
            dom[h] = jnp.where(group == h, do, jnp.zeros_like(do))
            stat[h, 0:1, :] = logs[h:h + 1, :]
            stat[h, 1:2, :] = jnp.sum(inner[h * HEAD_DIM:(h + 1) * HEAD_DIM, :], axis=0, keepdims=True)
        dq[...] = jnp.zeros((TILE, cols), F32)
        starts = start_ref[qb]
        places = base + lax.broadcasted_iota(jnp.int32, (1, TILE), 1)
        down = lax.broadcasted_iota(jnp.int32, (TILE, TILE), 0)

        def one_key(kb, _):
            at = pl.multiple_of(kb * TILE, TILE)
            keys = k_abs[pl.ds(at, TILE), :]
            vals = v_abs[pl.ds(at, TILE), :]
            allowed = jnp.logical_and(down + at >= starts, down + at <= places)
            dk_new = dv_new = dq_new = None
            more = lambda old, new: new if old is None else old + new
            for h in range(heads):
                s = dot_nt(keys, qm[h])
                p = jnp.exp(jnp.where(allowed, s - stat[h, 0:1, :], MASKED))
                dp = dot_nt(vals, dom[h])
                ds = (p * (dp - stat[h, 1:2, :])).astype(BF)
                dv_new = more(dv_new, dot_nn(p.astype(BF), dom[h]))
                dk_new = more(dk_new, dot_nn(ds, qm[h]))
                dq_new = more(dq_new, dot_tn(ds, km[h, pl.ds(at, TILE), :]))
            dv[pl.ds(at, TILE), :] += dv_new
            dk[pl.ds(at, TILE), :] += dk_new
            dq[...] += dq_new
            return 0

        lax.fori_loop(low_ref[qb], qb + 1, one_key, 0)
        for u in range(per):
            emit(srcs[u], 0, turn(dq[u * SUB:(u + 1) * SUB, :] * scale, tables(srcs[u]), -1.0))
        return 0

    lax.fori_loop(0, subs // per, one_query, 0)
    for i in range(subs):
        src = order_ref[i]
        rows = slice(i * SUB, (i + 1) * SUB)
        emit(src, cols, turn(dk[rows, :], tables(src), -1.0))
        emit(src, 2 * cols, dv[rows, :])


def attend_back(order, low, q, k, v, do, o, lse, start_rows, tables):
    subs, _, cols = q.shape
    length = subs * SUB
    heads = cols // HEAD_DIM
    args = (q, k, v, do, o, lse, start_rows, *tables)
    return pl.pallas_call(
        attend_back_kernel,
        grid=(1,),
        in_specs=[SMEM_SPEC, SMEM_SPEC] + [whole(a.shape) for a in args],
        out_specs=[whole((subs, SUB, 3 * cols)), whole((1, 3 * cols))],
        out_shape=[jax.ShapeDtypeStruct((subs, SUB, 3 * cols), BF), jax.ShapeDtypeStruct((1, 3 * cols), F32)],
        scratch_shapes=[VM((length, cols), BF), VM((length, cols), BF), VM((heads, length, cols), BF),
                        VM((length, cols), F32), VM((length, cols), F32), VM((TILE, cols), F32),
                        VM((heads, TILE, cols), BF), VM((heads, TILE, cols), BF), VM((heads, 2, TILE), F32)],
        compiler_params=PARAMS,
    )(order, low, *args)


def across(x, k):
    n = lax.axis_size("tensor")
    return lax.ppermute(x, "tensor", [(i, i ^ k) for i in range(n)])


def swap(x):
    return lax.ppermute(x, "pipe", [(0, 1), (1, 0)])


def gather_slots(x):
    half = x.shape[0] // 2
    one = across(x, 1)
    two = across(x, 2)
    far_a = across(one[:half], 2)
    far_b = across(two[half:], 1)
    return [x, one, two, jnp.concatenate([far_a, far_b], axis=0)]


def reduce_slots(make):
    far, *extra3 = make(3, None, None, BF)
    half = far.shape[0] // 2
    from_one = across(far[:half], 1)
    from_two = across(far[half:], 2)
    own, *extra0 = make(0, None, None, F32)
    first, *extra1 = make(1, 1, from_two, BF)
    got_one = across(first, 1)
    second, *extra2 = make(2, 0, from_one, BF)
    got_two = across(second, 2)
    total = own + got_one.astype(F32) + got_two.astype(F32)
    return total, [extra0, extra1, extra2, extra3]


def line_reduce(blocks, axis):
    n = lax.axis_size(axis)
    me = lax.axis_index(axis)
    take = lambda i: lax.dynamic_index_in_dim(blocks, jnp.clip(i, 0, n - 1), 0, keepdims=False)
    right = left = None
    for step in range(1, n):
        reach = n - step
        up, down = take(me + reach), take(me - reach)
        if right is not None:
            up = (up.astype(F32) + right.astype(F32)).astype(blocks.dtype)
            down = (down.astype(F32) + left.astype(F32)).astype(blocks.dtype)
        right = lax.ppermute(up, axis, [(i, i + 1) for i in range(n - 1) if i + reach <= n - 1])
        left = lax.ppermute(down, axis, [(i, i - 1) for i in range(1, n) if i - reach >= 0])
    total = take(me).astype(F32)
    if right is not None:
        total = total + right.astype(F32) + left.astype(F32)
    return total


def spread_reduce(vec, axis):
    n = lax.axis_size(axis)
    me = lax.axis_index(axis)
    total = lax.dynamic_index_in_dim(vec, me, 0, keepdims=False)
    for k in range(1, n):
        block = lax.dynamic_index_in_dim(vec, (me + k) % n, 0, keepdims=False)
        total = total + lax.ppermute(block, axis, [(i, (i + k) % n) for i in range(n)])
    return total


def forward_layer(x, lp, geo):
    slots = gather_slots(x)
    kept = None
    for k in range(len(slots)):
        kept = pre_slot(k, len(slots), slots[k], lp, geo["tables"], kept)
    n1, n2, q, k, v, g, slope = kept
    flat = lambda a: a.reshape(-1, SUB, a.shape[-1])
    o, lse = attend(geo["order"], geo["low"], flat(q), flat(k), flat(v), geo["start_cols"])
    o_slots = o.reshape(q.shape)
    make = lambda slot, half, addend, dtype: (post_slot(slot, o_slots, g, lp, half, addend, dtype),)
    summed, _ = reduce_slots(make)
    out_biases = lp["out_bias"].astype(F32)
    result = x.astype(F32) + summed + out_biases[0] + out_biases[1]
    saved = dict(slots=slots, n1=n1, n2=n2, q=flat(q), k=flat(k), v=flat(v), g=g, slope=slope, o=o, lse=lse)
    return result.astype(BF), saved


def backward_layer(e, lp, saved, geo):
    slots = gather_slots(e)
    kept = None
    for k in range(len(slots)):
        kept = bpre_slot(k, len(slots), slots[k], saved["slope"], lp, kept)
    e_all, do, df, bin_parts = kept
    flat = lambda a: a.reshape(-1, SUB, a.shape[-1])
    tables = [flat(t) for t in geo["tables"]]
    dqkv, bqkv_grad = attend_back(geo["order"], geo["low"], saved["q"], saved["k"], saved["v"], flat(do),
                                  saved["o"], saved["lse"], geo["start_rows"], tables)
    dqkv_slots = dqkv.reshape(len(slots), -1, dqkv.shape[-1])
    make = lambda slot, half, addend, dtype: bpost_slot(
        slot, saved["slots"][slot], dqkv_slots, df, lp, half, addend, dtype)
    u, extras = reduce_slots(make)
    col_sums = sum(item[0] for item in extras)
    x_rows, e_rows = saved["slots"][0].astype(F32), e.astype(F32)
    normal, inverse_std = norm_rows(x_rows)
    mean_grad = jnp.mean(u, axis=-1, keepdims=True)
    mean_cross = jnp.mean(u * normal, axis=-1, keepdims=True)
    dx = e_rows + (u - mean_grad - normal * mean_cross) * inverse_std
    rows2 = lambda a: a.reshape(-1, a.shape[-1])
    wgrad = lambda a, b: dot_tn(rows2(a), rows2(b)).astype(BF)
    grads = dict(
        w_out=wgrad(saved["o"], e_all),
        w_fc2=wgrad(saved["g"], e_all),
        w_in=wgrad(saved["n2"], df),
        w_qkv=wgrad(saved["n1"], dqkv),
    )
    small = jnp.concatenate([col_sums, jnp.sum(e_rows, axis=0, keepdims=True)], axis=0)
    bias_grads = jnp.concatenate([bqkv_grad[0], jnp.sum(bin_parts, axis=(0, 1))])
    return dx.astype(BF), grads, small, bias_grads


NAMES = ("w_qkv", "w_out", "w_in", "w_fc2")


def reduce_weights(grads, is_first):
    out = {}
    n = lax.axis_size("dp")
    for name in NAMES:
        g = grads[name]
        parts = g.reshape(n, 2, g.shape[0] // n // 2, g.shape[1])
        give = jnp.where(is_first, parts[:, 1], parts[:, 0])
        keep = jnp.where(is_first, parts[:, 0], parts[:, 1])
        both = (keep.astype(F32) + swap(give).astype(F32)).astype(BF)
        out[name] = line_reduce(both, "dp").astype(BF)
    return out


def column_order(a, direction):
    shape = a.shape
    heads = shape[-1] // (3 * HEAD_DIM)
    dims = (heads, 3) if direction > 0 else (3, heads)
    split = a.reshape(*shape[:-1], *dims, HEAD_DIM)
    return jnp.swapaxes(split, -2, -3).reshape(shape)


def body(ends, segments, ln_gain, ln_bias, w_qkv, b_qkv, w_out, w_in, b_in, w_fc2, out_bias):
    is_first = lax.axis_index("pipe") == 0
    me = lax.axis_index("tensor")
    n_tensor = lax.axis_size("tensor")
    choose = lambda a, b: jnp.where(is_first, a, b)
    shares = ends[0]
    rows, d = shares.shape[1:]

    keep = choose(shares[0], shares[1])
    got = swap(choose(shares[1], shares[0]))
    x0 = choose(keep, got)
    e1 = choose(got, keep)

    own = dict(ln_gain=ln_gain[0], ln_bias=ln_bias[0], w_qkv=column_order(w_qkv[0], 1),
               b_qkv=column_order(b_qkv, 1), w_out=w_out[0], w_in=w_in[0], b_in=b_in, w_fc2=w_fc2[0],
               out_bias=out_bias[0])
    small_names = ("ln_gain", "ln_bias", "b_qkv", "b_in", "out_bias")
    packed = jnp.concatenate([own[s].reshape(-1) for s in small_names]).reshape(-1, LANES)
    other_packed = swap(packed).reshape(-1)
    other = {name: swap(own[name]) for name in NAMES}
    at = 0
    for s in small_names:
        other[s] = other_packed[at:at + own[s].size].reshape(own[s].shape)
        at += own[s].size
    layer0 = {name: choose(own[name], other[name]) for name in own}
    layer1 = {name: choose(other[name], own[name]) for name in own}

    segment_row = choose(segments[0], segments[1])
    length = segment_row.shape[0]
    places = jnp.arange(length, dtype=jnp.int32)
    begins = jnp.concatenate([jnp.ones((1,), dtype=jnp.bool_), segment_row[1:] != segment_row[:-1]])
    starts = lax.cummax(jnp.where(begins, places, 0), axis=0)
    slot_index = jnp.arange(n_tensor, dtype=jnp.int32) ^ me
    by_slot = jnp.take((places - starts).reshape(n_tensor, rows), slot_index, axis=0)
    lane = jnp.arange(LANES, dtype=jnp.int32) % HEAD_DIM
    half_rot = ROT // 2
    frequency = jnp.power(10000.0, -2.0 * (lane % half_rot).astype(F32) / ROT)
    angles = by_slot.astype(F32)[:, :, None] * frequency
    sines = jnp.sin(angles)
    tables = (jnp.where(lane < ROT, jnp.cos(angles), 1.0),
              jnp.where(lane < half_rot, -sines, 0.0),
              jnp.where(jnp.logical_and(lane >= half_rot, lane < ROT), sines, 0.0))
    per = rows // SUB
    subs = jnp.arange(length // SUB, dtype=jnp.int32)
    geo = dict(
        tables=tables,
        order=(((subs // per) ^ me) * per + subs % per).astype(jnp.int32),
        low=(starts.reshape(-1, TILE)[:, 0] // TILE).astype(jnp.int32),
        start_cols=jnp.broadcast_to(starts[:, None], (length, LANES)),
        start_rows=starts.reshape(-1, 1, TILE),
    )

    h, saved0 = forward_layer(x0, layer0, geo)
    y1, saved1 = forward_layer(h, layer1, geo)
    e0, grads1, small1, bias1 = backward_layer(e1, layer1, saved1, geo)
    half1 = reduce_weights(grads1, is_first)
    dx0, grads0, small0, bias0 = backward_layer(e0, layer0, saved0, geo)
    half0 = reduce_weights(grads0, is_first)

    got = swap(choose(y1, dx0))
    mine = choose(dx0, y1)
    boundary = jnp.stack([choose(mine, got), choose(got, mine)])[None]

    full = {}
    for name in NAMES:
        got = swap(choose(half1[name], half0[name]))
        mine = choose(half0[name], half1[name])
        full[name] = jnp.concatenate([choose(mine, got), choose(got, mine)], axis=0).astype(F32)

    n_dp = lax.axis_size("dp")
    small = choose(small0, small1) + swap(choose(small1, small0))
    bias = choose(bias0, bias1) + swap(choose(bias1, bias0))
    small = jnp.moveaxis(small.reshape(small.shape[0], n_tensor, -1), 1, 0)
    small = spread_reduce(small, "tensor")
    small = jnp.moveaxis(small.reshape(small.shape[0], n_dp, -1), 1, 0)
    n_qkv = b_qkv.size
    bias = jnp.concatenate([bias[:n_qkv].reshape(n_dp, -1), bias[n_qkv:].reshape(n_dp, -1)], axis=1)
    back = column_order(bias_qkv_whole(bias, n_qkv, n_dp), -1).reshape(n_dp, -1)
    bias = jnp.concatenate([back, bias[:, n_qkv // n_dp:]], axis=1)
    line = jnp.concatenate([small.reshape(n_dp, -1), bias], axis=1)
    line = spread_reduce(line, "dp")
    n_small = small.shape[1] * small.shape[2]
    sums = line[:n_small].reshape(small.shape[1:])
    bias = line[n_small:]
    g_b_qkv, g_b_in = bias[:n_qkv // n_dp], bias[n_qkv // n_dp:]
    g_gain, g_bias = sums[None, 0:2], sums[None, 2:4]
    g_out_bias = jnp.stack([sums[4], sums[4]])[None]
    return (
        boundary,
        g_gain,
        g_bias,
        column_order(full["w_qkv"], -1)[None],
        g_b_qkv[None],
        full["w_out"][None],
        full["w_in"][None],
        g_b_in[None],
        full["w_fc2"][None],
        g_out_bias,
    )


def bias_qkv_whole(bias, n_qkv, n_dp):
    return bias[:, :n_qkv // n_dp].reshape(1, n_qkv)


def solution(mesh):
    placed = (
        P("pipe", "dp", "tensor", None),
        P("dp", None),
        P("pipe", None, None),
        P("pipe", None, None),
        P("pipe", None, "tensor"),
        P("pipe", "tensor"),
        P("pipe", "tensor", None),
        P("pipe", None, "tensor"),
        P("pipe", "tensor"),
        P("pipe", "tensor", None),
        P("pipe", None, None),
    )
    return jax.shard_map(
        body,
        mesh=mesh,
        in_specs=placed,
        out_specs=(
            P("pipe", "dp", "tensor", None),
            P("pipe", None, ("tensor", "dp")),
            P("pipe", None, ("tensor", "dp")),
            P("pipe", "dp", "tensor"),
            P("pipe", ("tensor", "dp")),
            P("pipe", ("tensor", "dp"), None),
            P("pipe", "dp", "tensor"),
            P("pipe", ("tensor", "dp")),
            P("pipe", ("tensor", "dp"), None),
            P("pipe", None, ("tensor", "dp")),
        ),
        check_vma=False,
    )
```

time: 2130 us -> 787 us (0.37)
  waiting for transfers between devices: 997 us -> 94.4 us
  matrix products: 542 us -> 28 us
  Pallas kernels: 0 us -> 335 us
  local copies, waits for them, and re-layouts: 361 us -> 41.7 us
  starting transfers between devices: 9.68 us -> 180 us
  other arithmetic: 179 us -> 90.5 us
    reduce_scatter x13 -> x0, waiting for transfers between devices: 610 us -> none  [the longest x3 206 us: forward_section(): lax.psum_scatter(jnp.dot(mixed, out_weight, preferred_element_type=jnp.fl...]
    dot_general x99 -> x8, matrix products: 542 us -> 28 us  [dot_tn(): return lax.dot_general(a, b, TN, preferred_element_type=F32)]
    pallas_call x0 -> x36, Pallas kernels: none -> 335 us  [the longest x16 102 us: slot_call(): pl.pallas_call(functools.partial(kernel, n_alias), grid=grid, in_specs=sp...]
    all_gather x9 -> x0, waiting for transfers between devices: 232 us -> none  [the longest x3 117 us: forward_section(): lax.all_gather(one_share, 'tensor', axis=0, tiled=True)]
    dynamic_update_slice x36 -> x0, local copies, waits for them, and re-layouts: 201 us -> none  [attend_forward(): lax.map(one_block, (jnp.arange(blocks, dtype=jnp.int32), queries.reshape(...]
    ppermute x4 -> x107, starting transfers between devices: 7.76 us -> 180 us  [the longest x24 105 us: line_reduce(): lax.ppermute(up, axis, [(i, i + 1) for i in range(n - 1) if i + reach <=...]
    unnamed x32 -> x0, waiting for transfers between devices: 149 us -> none
    ppermute x4 -> x107, waiting for transfers between devices: 6.55 us -> 94.4 us  [the longest x32 70.3 us: across(): return lax.ppermute(x, 'tensor', [(i, i ^ k) for i in range(n)])]
  transfers between devices with their start and end apart: 31 -> 107, of which waited for: 23 -> 23; matrix products, arithmetic and copies ran while one was open for 46% -> 19% of each run, Pallas kernels for 0% -> 29%
where the time goes in v1:
time: 787 us; the launch traced here: 773 us
  Pallas kernels  335 us (43%)
  starting transfers between devices  180 us (23%)
  waiting for transfers between devices  94.4 us (12%)
  other arithmetic  90.5 us (11%)
  local copies, waits for them, and re-layouts  41.7 us (5%)
  matrix products  28 us (4%)
    ppermute x24, starting transfers between devices, line_reduce(): lax.ppermute(up, axis, [(i, i + 1) for i in range(n - 1) if i + reach <=...  105 us
    pallas_call x16, Pallas kernels, slot_call(): pl.pallas_call(functools.partial(kernel, n_alias), grid=grid, in_specs=sp...  102 us
    pallas_call x2, Pallas kernels, attend(): pl.pallas_call(attend_kernel, grid=(1,), in_specs=[SMEM_SPEC, SMEM_SPEC]...  80.8 us
    ppermute x32, waiting for transfers between devices, across(): return lax.ppermute(x, 'tensor', [(i, i ^ k) for i in range(n)])  70.3 us
    pallas_call x2, Pallas kernels, attend_back(): pl.pallas_call(attend_back_kernel, grid=(1,), in_specs=[SMEM_SPEC, SMEM_S...  60.8 us
    pallas_call x8, Pallas kernels, bpost_slot(): pl.pallas_call(functools.partial(bpost_kernel, half, ck), grid=(d // ck,)...  51.3 us
    pallas_call x8, Pallas kernels, post_slot(): pl.pallas_call(functools.partial(post_kernel, half), grid=(d // ck,), in_...  39.9 us
    ppermute x32, starting transfers between devices, across(): return lax.ppermute(x, 'tensor', [(i, i ^ k) for i in range(n)])  39.3 us
  transfers between devices with their start and end apart: 107, of which 23 were waited for; matrix products, arithmetic and copies ran while one was open for 19% of the time, Pallas kernels for 29%

profile of v1, /device:TPU:0, one launch (start us, length us, event | category | flops | bytes accessed | tf_op | source)
XLA Modules:
  0.0 773.0 jit_solution(14813655454970640046)
XLA Ops:
  22.4 16.6 %collective-permute-done.1.x_ref = bf16[384,1024]{1,0:T(8,128)(2,1)} collective-permute-done((bf16[384,1024]{1,0:T(8,128)(2,1)S(1)}, bf16[384,1024]{1,0:T(8,128)(2,1)}, u32[]{:S(2)}, u32[]{:S(2)}) %collective-permute-start.1) | collective-permute-done | bytes 786464 | tf_op jit(solution)/shard_map/ppermute | solution.py:443
  45.6 13.9 %collective-permute-done.3.x_ref = bf16[384,1024]{1,0:T(8,128)(2,1)} collective-permute-done((bf16[384,1024]{1,0:T(8,128)(2,1)S(1)}, bf16[384,1024]{1,0:T(8,128)(2,1)}, u32[]{:S(2)}, u32[]{:S(2)}) %collective-permute-start.3) | collective-permute-done | bytes 786464 | tf_op jit(solution)/shard_map/ppermute | solution.py:443
  72.9 7.3 shard_map.186
  80.1 7.3 shard_map.187
  87.4 7.4 shard_map.188
  94.7 7.8 %shard_map.189 = (bf16[4,384,1024]{2,1,0:T(8,128)(2,1)}, bf16[4,384,1024]{2,1,0:T(8,128)(2,1)}, bf16[4,384,256]{2,1,0:T(8,128)(2,1)}, bf16[4,384,256]{2,1,0:T(8,...) custom-call(bf16[384,1024]{1,0:T(8,128)(2,1)} %copy-done.44, ...), custom_call_target="tpu_custom_call", output_to_operand_aliasing={{0}: (10, {}), {1}: (11, {}), {2}: (12, {}), {3}: (13, {}),... | custom-call | tf_op jit(solution)/shard_map/pallas_call | solution.py:104
  103.7 40.4 %shard_map.190 = (bf16[12,128,256]{2,1,0:T(8,128)(2,1)}, f32[1536,128]{1,0:T(8,128)}) custom-call(s32[12]{0:T(128)} %fusion.101.order_ref, s32[6]{0:T(128)} %and_select_fusion.2.low_ref, bf16[12,128,256]{2,1,0:T(8,128)(2,1)} %bitcast.467, bf16[12,128,256]{2,1,0:T(8,128)(2,1)} %bitcast.469, bf16[12,128,256]{2,1,0:T(8,128)(2,1)} %bitcast.471, ...), custom_call_target="tpu_custom_call" | custom-call | tf_op jit(solution)/shard_map/pallas_call | solution.py:332
  158.5 5.6 collective-permute-done.10.rest_0_
  164.1 5.0 shard_map.193
  171.1 5.1 shard_map.194
  188.1 8.1 %collective-permute-done.11 = bf16[384,1024]{1,0:T(8,128)(2,1)} collective-permute-done((bf16[384,1024]{1,0:T(8,128)(2,1)}, bf16[384,1024]{1,0:T(8,128)(2,1)}, u32[]{:S(2)}, u32[]{:S(2)}) %collective-permute-start.11) | collective-permute-done | bytes 786464 | tf_op jit(solution)/shard_map/ppermute | solution.py:443
  210.4 6.4 collective-permute-done.14.x_ref
  219.9 7.3 shard_map.195
  227.8 7.5 shard_map.196
  235.3 7.3 shard_map.197
  243.5 7.3 shard_map.198
  250.8 5.3 shard_map.199
  256.1 40.4 %shard_map.203 = (bf16[12,128,256]{2,1,0:T(8,128)(2,1)}, f32[1536,128]{1,0:T(8,128)}) custom-call(s32[12]{0:T(128)} %fusion.101.order_ref, s32[6]{0:T(128)} %and_select_fusion.2.low_ref, bf16[12,128,256]{2,1,0:T(8,128)(2,1)} %bitcast.461, bf16[12,128,256]{2,1,0:T(8,128)(2,1)} %bitcast.463, bf16[12,128,256]{2,1,0:T(8,128)(2,1)} %bitcast.465, ...), custom_call_target="tpu_custom_call" | custom-call | tf_op jit(solution)/shard_map/pallas_call | solution.py:332
  296.5 5.3 shard_map.200
  301.9 5.3 shard_map.201
  307.2 5.3 shard_map.202
  312.6 30.4 %shard_map.204 = (bf16[12,128,768]{2,1,0:T(8,128)(2,1)}, f32[1,768]{1,0:T(1,128)}) custom-call(s32[12]{0:T(128)} %fusion.101.order_ref, s32[6]{0:T(128)} %and_select_fusion.2.low_ref, bf16[12,128,256]{2,1,0:T(8,128)(2,1)} %bitcast.462, bf16[12,128,256]{2,1,0:T(8,128)(2,1)} %bitcast.464, bf16[12,128,256]{2,1,0:T(8,128)(2,1)} %bitcast.466, ...), custom_call_target="tpu_custom_call" | custom-call | tf_op jit(solution)/shard_map/pallas_call | solution.py:428
  343.0 6.4 shard_map.206
  390.3 5.4 collective-permute-start.71
  396.8 6.4 shard_map.205
  403.2 5.0 shard_map.218
  408.3 6.4 shard_map.207
  414.7 6.4 shard_map.208
  421.1 5.0 shard_map.220
  426.8 5.1 shard_map.221
  438.4 5.3 collective-permute-start.55
  475.2 5.3 shard_map.209
  493.4 5.5 shard_map.210
  498.9 5.4 shard_map.211
  505.2 5.5 shard_map.212
  510.8 6.7 bitcast_convert_fusion.1
  525.4 30.4 %shard_map.213 = (bf16[12,128,768]{2,1,0:T(8,128)(2,1)}, f32[1,768]{1,0:T(1,128)}) custom-call(s32[12]{0:T(128)} %fusion.101.order_ref, s32[6]{0:T(128)} %and_select_fusion.2.low_ref, bf16[12,128,256]{2,1,0:T(8,128)(2,1)} %bitcast.468, bf16[12,128,256]{2,1,0:T(8,128)(2,1)} %bitcast.470, bf16[12,128,256]{2,1,0:T(8,128)(2,1)} %bitcast.472, ...), custom_call_target="tpu_custom_call" | custom-call | tf_op jit(solution)/shard_map/pallas_call | solution.py:428
  566.0 6.5 shard_map.215
  579.2 6.4 shard_map.214
  589.4 6.5 shard_map.216
  597.3 6.3 shard_map.217
  605.2 12.0 %collective-permute-start.63 = (bf16[32,1024]{1,0:T(8,128)(2,1)}, bf16[32,1024]{1,0:T(8,128)(2,1)}, u32[]{:S(2)}, u32[]{:S(2)}) collective-permute-start(bf16[32,1024]{1,0:T(8,128)(2,1)} %get-tuple-element.346), channel_id=1, source_target_pairs={{0,1},{4,5},{8,9},{12,13},{16,17},{20,21},{24,25},{28,29}} | collective-permute-start | bytes 196616 | tf_op jit(solution)/shard_map/ppermute | solution.py:484
  669.8 11.6 %collective-permute-done.31 = bf16[384,1024]{1,0:T(8,128)(2,1)S(1)} collective-permute-done((bf16[384,1024]{1,0:T(8,128)(2,1)S(1)}, bf16[384,1024]{1,0:T(8,128)(2,1)S(1)}, u32[]{:S(2)}, u32[]{:S(2)}) %collective-permute-start.31) | collective-permute-done | bytes 786464 | tf_op jit(solution)/shard_map/ppermute | solution.py:443
  684.1 5.8 collective-permute-start.49
  689.9 5.1 collective-permute-start.93
  718.9 5.9 collective-permute-start.102
  739.4 8.7 %collective-permute-start.95 = (bf16[128,1024]{1,0:T(8,128)(2,1)}, bf16[128,1024]{1,0:T(8,128)(2,1)S(1)}, u32[]{:S(2)}, u32[]{:S(2)}) collective-permute-start(bf16[128,1024]{1,0:T(8,128)(2,1)} %get-tuple-element.303), channel_id=1, source_target_pairs={{0,1},{1,2},{2,3},{4,5},{5,6},{6,7},{8,9},{9,10},{10,11},{12,13},{... | collective-permute-start | bytes 786440 | tf_op jit(solution)/shard_map/ppermute | solution.py:484
  754.4 5.2 collective-permute-start.80
  (600 shorter events, 326.9 us)
Async XLA Ops:
  7.1 55.2 %collective-permute-start.6 = (bf16[1024,768]{1,0:T(8,128)(2,1)}, bf16[1024,768]{1,0:T(8,128)(2,1)}, u32[]{:S(2)}, u32[]{:S(2)}) collective-permute-start(bf16[1024,768]{1,0:T(8,128)(2,1)} %copy.153), channel_id=1, source_target_pairs={{0,16},{16,0},{1,17},{17,1},{2,18},{18,2},{3,19},{19,3},{4,20},{20... | collective-permute-start | bytes 4718600 | tf_op jit(solution)/shard_map/ppermute | solution.py:447
  7.6 61.2 %collective-permute-start.7 = (bf16[1024,1024]{1,0:T(8,128)(2,1)}, bf16[1024,1024]{1,0:T(8,128)(2,1)}, u32[]{:S(2)}, u32[]{:S(2)}) collective-permute-start(bf16[1024,1024]{1,0:T(8,128)(2,1)} %bitcast.500), channel_id=1, source_target_pairs={{0,16},{16,0},{1,17},{17,1},{2,18},{18,2},{3,19},{19,3},{4,20},{20... | collective-permute-start | bytes 6291464 | tf_op jit(solution)/shard_map/ppermute | solution.py:447
  7.7 136.5 %collective-permute-start.9 = (bf16[1024,1024]{1,0:T(8,128)(2,1)}, bf16[1024,1024]{1,0:T(8,128)(2,1)}, u32[]{:S(2)}, u32[]{:S(2)}) collective-permute-start(bf16[1024,1024]{1,0:T(8,128)(2,1)} %bitcast.501), channel_id=1, source_target_pairs={{0,16},{16,0},{1,17},{17,1},{2,18},{18,2},{3,19},{19,3},{4,20},{20... | collective-permute-start | bytes 6291464 | tf_op jit(solution)/shard_map/ppermute | solution.py:447
  15.8 27.2 %collective-permute-start.8 = (bf16[256,1024]{1,0:T(8,128)(2,1)}, bf16[256,1024]{1,0:T(8,128)(2,1)}, u32[]{:S(2)}, u32[]{:S(2)}) collective-permute-start(bf16[256,1024]{1,0:T(8,128)(2,1)} %bitcast.20), channel_id=1, source_target_pairs={{0,16},{16,0},{1,17},{17,1},{2,18},{18,2},{3,19},{19,3},{4,20},{20... | collective-permute-start | bytes 1572872 | tf_op jit(solution)/shard_map/ppermute | solution.py:447
  18.1 20.8 %collective-permute-start.1 = (bf16[384,1024]{1,0:T(8,128)(2,1)S(1)}, bf16[384,1024]{1,0:T(8,128)(2,1)}, u32[]{:S(2)}, u32[]{:S(2)}) collective-permute-start(bf16[384,1024]{1,0:T(8,128)(2,1)S(1)} %get-tuple-element.294.x_ref), channel_id=1, source_target_pairs={{0,4},{4,0},{8,12},{12,8},{1,5},{5,1},{9,13},{13,9},{2,6},{6,2},{1... | collective-permute-start | bytes 2359304 | tf_op jit(solution)/shard_map/ppermute | solution.py:443
  39.0 20.6 %collective-permute-start.3 = (bf16[384,1024]{1,0:T(8,128)(2,1)S(1)}, bf16[384,1024]{1,0:T(8,128)(2,1)}, u32[]{:S(2)}, u32[]{:S(2)}) collective-permute-start(bf16[384,1024]{1,0:T(8,128)(2,1)S(1)} %get-tuple-element.294.x_ref), channel_id=1, source_target_pairs={{0,8},{4,12},{8,0},{12,4},{1,9},{5,13},{9,1},{13,5},{2,10},{6,14},... | collective-permute-start | bytes 2359304 | tf_op jit(solution)/shard_map/ppermute | solution.py:443
  43.0 23.3 %collective-permute-start.2 = (bf16[192,1024]{1,0:T(8,128)(2,1)S(1)}, bf16[192,1024]{1,0:T(8,128)(2,1)S(1)}, u32[]{:S(2)}, u32[]{:S(2)}) collective-permute-start(bf16[192,1024]{1,0:T(8,128)(2,1)S(1)} %slice.307), channel_id=1, source_target_pairs={{0,8},{4,12},{8,0},{12,4},{1,9},{5,13},{9,1},{13,5},{2,10},{6,14},... | collective-permute-start | bytes 1179656 | tf_op jit(solution)/shard_map/ppermute | solution.py:443
  157.4 23.5 %collective-permute-start.18 = (bf16[384,1024]{1,0:T(8,128)(2,1)S(1)}, bf16[384,1024]{1,0:T(8,128)(2,1)S(1)}, u32[]{:S(2)}, u32[]{:S(2)}) collective-permute-start(bf16[384,1024]{1,0:T(8,128)(2,1)S(1)} %get-tuple-element.275.e_ref), channel_id=1, source_target_pairs={{0,4},{4,0},{8,12},{12,8},{1,5},{5,1},{9,13},{13,9},{2,6},{6,2},{1... | collective-permute-start | bytes 2359304 | tf_op jit(solution)/shard_map/ppermute | solution.py:443
  157.9 23.9 %collective-permute-start.20 = (bf16[384,1024]{1,0:T(8,128)(2,1)S(1)}, bf16[384,1024]{1,0:T(8,128)(2,1)S(1)}, u32[]{:S(2)}, u32[]{:S(2)}) collective-permute-start(bf16[384,1024]{1,0:T(8,128)(2,1)S(1)} %get-tuple-element.275.e_ref), channel_id=1, source_target_pairs={{0,8},{4,12},{8,0},{12,4},{1,9},{5,13},{9,1},{13,5},{2,10},{6,14},... | collective-permute-start | bytes 2359304 | tf_op jit(solution)/shard_map/ppermute | solution.py:443
  169.2 27.1 %collective-permute-start.11 = (bf16[384,1024]{1,0:T(8,128)(2,1)}, bf16[384,1024]{1,0:T(8,128)(2,1)}, u32[]{:S(2)}, u32[]{:S(2)}) collective-permute-start(bf16[384,1024]{1,0:T(8,128)(2,1)} %shard_map.193), channel_id=1, source_target_pairs={{0,4},{4,0},{8,12},{12,8},{1,5},{5,1},{9,13},{13,9},{2,6},{6,2},{1... | collective-permute-start | bytes 2359304 | tf_op jit(solution)/shard_map/ppermute | solution.py:443
  176.2 21.6 %collective-permute-start.13 = (bf16[384,1024]{1,0:T(8,128)(2,1)}, bf16[384,1024]{1,0:T(8,128)(2,1)}, u32[]{:S(2)}, u32[]{:S(2)}) collective-permute-start(bf16[384,1024]{1,0:T(8,128)(2,1)} %shard_map.194), channel_id=1, source_target_pairs={{0,8},{4,12},{8,0},{12,4},{1,9},{5,13},{9,1},{13,5},{2,10},{6,14},... | collective-permute-start | bytes 2359304 | tf_op jit(solution)/shard_map/ppermute | solution.py:443
  180.9 28.1 %collective-permute-start.19 = (bf16[192,1024]{1,0:T(8,128)(2,1)S(1)}, bf16[192,1024]{1,0:T(8,128)(2,1)S(1)}, u32[]{:S(2)}, u32[]{:S(2)}) collective-permute-start(bf16[192,1024]{1,0:T(8,128)(2,1)S(1)} %slice.320), channel_id=1, source_target_pairs={{0,8},{4,12},{8,0},{12,4},{1,9},{5,13},{9,1},{13,5},{2,10},{6,14},... | collective-permute-start | bytes 1179656 | tf_op jit(solution)/shard_map/ppermute | solution.py:443
  181.9 27.1 %collective-permute-start.21 = (bf16[192,1024]{1,0:T(8,128)(2,1)S(1)}, bf16[192,1024]{1,0:T(8,128)(2,1)S(1)}, u32[]{:S(2)}, u32[]{:S(2)}) collective-permute-start(bf16[192,1024]{1,0:T(8,128)(2,1)S(1)} %slice.321), channel_id=1, source_target_pairs={{0,4},{4,0},{8,12},{12,8},{1,5},{5,1},{9,13},{13,9},{2,6},{6,2},{1... | collective-permute-start | bytes 1179656 | tf_op jit(solution)/shard_map/ppermute | solution.py:443
  216.9 25.7 %collective-permute-start.15 = (bf16[192,1024]{1,0:T(8,128)(2,1)S(1)}, bf16[192,1024]{1,0:T(8,128)(2,1)S(1)}, u32[]{:S(2)}, u32[]{:S(2)}) collective-permute-start(bf16[192,1024]{1,0:T(8,128)(2,1)S(1)} %slice.318), channel_id=1, source_target_pairs={{0,8},{4,12},{8,0},{12,4},{1,9},{5,13},{9,1},{13,5},{2,10},{6,14},... | collective-permute-start | bytes 1179656 | tf_op jit(solution)/shard_map/ppermute | solution.py:443
  218.8 23.7 %collective-permute-start.17 = (bf16[192,1024]{1,0:T(8,128)(2,1)S(1)}, bf16[192,1024]{1,0:T(8,128)(2,1)S(1)}, u32[]{:S(2)}, u32[]{:S(2)}) collective-permute-start(bf16[192,1024]{1,0:T(8,128)(2,1)S(1)} %slice.319), channel_id=1, source_target_pairs={{0,4},{4,0},{8,12},{12,8},{1,5},{5,1},{9,13},{13,9},{2,6},{6,2},{1... | collective-permute-start | bytes 1179656 | tf_op jit(solution)/shard_map/ppermute | solution.py:443
  351.5 37.6 %collective-permute-start.22 = (bf16[192,1024]{1,0:T(8,128)(2,1)}, bf16[192,1024]{1,0:T(8,128)(2,1)}, u32[]{:S(2)}, u32[]{:S(2)}) collective-permute-start(bf16[192,1024]{1,0:T(8,128)(2,1)} %get-tuple-element.334), channel_id=1, source_target_pairs={{0,8},{4,12},{8,0},{12,4},{1,9},{5,13},{9,1},{13,5},{2,10},{6,14},... | collective-permute-start | bytes 1179656 | tf_op jit(solution)/shard_map/ppermute | solution.py:443
  352.4 37.9 %collective-permute-start.24 = (bf16[192,1024]{1,0:T(8,128)(2,1)}, bf16[192,1024]{1,0:T(8,128)(2,1)}, u32[]{:S(2)}, u32[]{:S(2)}) collective-permute-start(bf16[192,1024]{1,0:T(8,128)(2,1)} %get-tuple-element.335), channel_id=1, source_target_pairs={{0,4},{4,0},{8,12},{12,8},{1,5},{5,1},{9,13},{13,9},{2,6},{6,2},{1... | collective-permute-start | bytes 1179656 | tf_op jit(solution)/shard_map/ppermute | solution.py:443
  363.1 17.9 %collective-permute-start.69 = (bf16[4,32,1024]{2,1,0:T(8,128)(2,1)S(1)}, bf16[4,32,1024]{2,1,0:T(8,128)(2,1)}, u32[]{:S(2)}, u32[]{:S(2)}) collective-permute-start(bf16[4,32,1024]{2,1,0:T(8,128)(2,1)S(1)} %select_bitcast_fusion.13), channel_id=1, source_target_pairs={{0,16},{16,0},{1,17},{17,1},{2,18},{18,2},{3,19},{19,3},{4,20},{20... | collective-permute-start | bytes 786440 | tf_op jit(solution)/shard_map/ppermute | solution.py:447
  375.0 61.0 %collective-permute-start.54 = (bf16[4,128,768]{1,2,0:T(8,128)(2,1)}, bf16[4,128,768]{1,2,0:T(8,128)(2,1)}, u32[]{:S(2)}, u32[]{:S(2)}) collective-permute-start(bf16[4,128,768]{1,2,0:T(8,128)(2,1)} %select_bitcast_fusion.4), channel_id=1, source_target_pairs={{0,16},{16,0},{1,17},{17,1},{2,18},{18,2},{3,19},{19,3},{4,20},{20... | collective-permute-start | bytes 2359304 | tf_op jit(solution)/shard_map/ppermute | solution.py:447
  386.1 34.9 %collective-permute-start.34 = (bf16[192,1024]{1,0:T(8,128)(2,1)S(1)}, bf16[192,1024]{1,0:T(8,128)(2,1)}, u32[]{:S(2)}, u32[]{:S(2)}) collective-permute-start(bf16[192,1024]{1,0:T(8,128)(2,1)S(1)} %get-tuple-element.329), channel_id=1, source_target_pairs={{0,8},{4,12},{8,0},{12,4},{1,9},{5,13},{9,1},{13,5},{2,10},{6,14},... | collective-permute-start | bytes 1179656 | tf_op jit(solution)/shard_map/ppermute | solution.py:443
  388.1 38.2 %collective-permute-start.36 = (bf16[192,1024]{1,0:T(8,128)(2,1)S(1)}, bf16[192,1024]{1,0:T(8,128)(2,1)}, u32[]{:S(2)}, u32[]{:S(2)}) collective-permute-start(bf16[192,1024]{1,0:T(8,128)(2,1)S(1)} %get-tuple-element.330), channel_id=1, source_target_pairs={{0,4},{4,0},{8,12},{12,8},{1,5},{5,1},{9,13},{13,9},{2,6},{6,2},{1... | collective-permute-start | bytes 1179656 | tf_op jit(solution)/shard_map/ppermute | solution.py:443
  389.0 42.8 %collective-permute-start.73 = (bf16[32,1024]{1,0:T(8,128)(2,1)S(1)}, bf16[32,1024]{1,0:T(8,128)(2,1)}, u32[]{:S(2)}, u32[]{:S(2)}) collective-permute-start(bf16[32,1024]{1,0:T(8,128)(2,1)S(1)} %get-tuple-element.343), channel_id=1, source_target_pairs={{3,2},{7,6},{11,10},{15,14},{19,18},{23,22},{27,26},{31,30}} | collective-permute-start | bytes 196616 | tf_op jit(solution)/shard_map/ppermute | solution.py:485
  390.3 42.6 %collective-permute-start.71 = (bf16[32,1024]{1,0:T(8,128)(2,1)S(1)}, bf16[32,1024]{1,0:T(8,128)(2,1)}, u32[]{:S(2)}, u32[]{:S(2)}) collective-permute-start(bf16[32,1024]{1,0:T(8,128)(2,1)S(1)} %fusion.78), channel_id=1, source_target_pairs={{0,1},{1,2},{4,5},{5,6},{8,9},{9,10},{12,13},{13,14},{16,17},{17,1... | collective-permute-start | bytes 196616 | tf_op jit(solution)/shard_map/ppermute | solution.py:484
  421.1 26.5 %collective-permute-start.99 = (bf16[4,128,1024]{2,1,0:T(8,128)(2,1)}, bf16[4,128,1024]{2,1,0:T(8,128)(2,1)}, u32[]{:S(2)}, u32[]{:S(2)}) collective-permute-start(bf16[4,128,1024]{2,1,0:T(8,128)(2,1)} %select_bitcast_fusion), channel_id=1, source_target_pairs={{0,16},{16,0},{1,17},{17,1},{2,18},{18,2},{3,19},{19,3},{4,20},{20... | collective-permute-start | bytes 3145736 | tf_op jit(solution)/shard_map/ppermute | solution.py:447
  426.2 27.7 %collective-permute-start.84 = (bf16[4,128,1024]{2,1,0:T(8,128)(2,1)}, bf16[4,128,1024]{2,1,0:T(8,128)(2,1)S(1)}, u32[]{:S(2)}, u32[]{:S(2)}) collective-permute-start(bf16[4,128,1024]{2,1,0:T(8,128)(2,1)} %select_bitcast_fusion.2), channel_id=1, source_target_pairs={{0,16},{16,0},{1,17},{17,1},{2,18},{18,2},{3,19},{19,3},{4,20},{20... | collective-permute-start | bytes 3145736 | tf_op jit(solution)/shard_map/ppermute | solution.py:447
  431.8 27.1 %collective-permute-start.23 = (bf16[384,1024]{1,0:T(8,128)(2,1)}, bf16[384,1024]{1,0:T(8,128)(2,1)S(1)}, u32[]{:S(2)}, u32[]{:S(2)}) collective-permute-start(bf16[384,1024]{1,0:T(8,128)(2,1)} %get-tuple-element.192), channel_id=1, source_target_pairs={{0,4},{4,0},{8,12},{12,8},{1,5},{5,1},{9,13},{13,9},{2,6},{6,2},{1... | collective-permute-start | bytes 2359304 | tf_op jit(solution)/shard_map/ppermute | solution.py:443
  432.9 26.8 %collective-permute-start.25 = (bf16[384,1024]{1,0:T(8,128)(2,1)}, bf16[384,1024]{1,0:T(8,128)(2,1)S(1)}, u32[]{:S(2)}, u32[]{:S(2)}) collective-permute-start(bf16[384,1024]{1,0:T(8,128)(2,1)} %get-tuple-element.193), channel_id=1, source_target_pairs={{0,8},{4,12},{8,0},{12,4},{1,9},{5,13},{9,1},{13,5},{2,10},{6,14},... | collective-permute-start | bytes 2359304 | tf_op jit(solution)/shard_map/ppermute | solution.py:443
  446.8 24.2 %collective-permute-start.58 = (bf16[128,768]{0,1:T(8,128)(2,1)S(1)}, bf16[128,768]{0,1:T(8,128)(2,1)S(1)}, u32[]{:S(2)}, u32[]{:S(2)}) collective-permute-start(bf16[128,768]{0,1:T(8,128)(2,1)S(1)} %get-tuple-element.324), channel_id=1, source_target_pairs={{3,2},{7,6},{11,10},{15,14},{19,18},{23,22},{27,26},{31,30}} | collective-permute-start | bytes 589832 | tf_op jit(solution)/shard_map/ppermute | solution.py:485
  447.5 24.4 %collective-permute-start.56 = (bf16[128,768]{0,1:T(8,128)(2,1)S(1)}, bf16[128,768]{0,1:T(8,128)(2,1)S(1)}, u32[]{:S(2)}, u32[]{:S(2)}) collective-permute-start(bf16[128,768]{0,1:T(8,128)(2,1)S(1)} %fusion.66), channel_id=1, source_target_pairs={{0,1},{1,2},{4,5},{5,6},{8,9},{9,10},{12,13},{13,14},{16,17},{17,1... | collective-permute-start | bytes 589832 | tf_op jit(solution)/shard_map/ppermute | solution.py:484
  463.4 20.6 %collective-permute-start.88 = (bf16[128,1024]{1,0:T(8,128)(2,1)S(1)}, bf16[128,1024]{1,0:T(8,128)(2,1)S(1)}, u32[]{:S(2)}, u32[]{:S(2)}) collective-permute-start(bf16[128,1024]{1,0:T(8,128)(2,1)S(1)} %get-tuple-element.310), channel_id=1, source_target_pairs={{3,2},{7,6},{11,10},{15,14},{19,18},{23,22},{27,26},{31,30}} | collective-permute-start | bytes 786440 | tf_op jit(solution)/shard_map/ppermute | solution.py:485
  471.0 17.5 %collective-permute-start.26 = (bf16[384,1024]{1,0:T(8,128)(2,1)S(1)}, bf16[384,1024]{1,0:T(8,128)(2,1)S(1)}, u32[]{:S(2)}, u32[]{:S(2)}) collective-permute-start(bf16[384,1024]{1,0:T(8,128)(2,1)S(1)} %get-tuple-element.277.e_ref), channel_id=1, source_target_pairs={{0,4},{4,0},{8,12},{12,8},{1,5},{5,1},{9,13},{13,9},{2,6},{6,2},{1... | collective-permute-start | bytes 2359304 | tf_op jit(solution)/shard_map/ppermute | solution.py:443
  472.0 17.8 %collective-permute-start.28 = (bf16[384,1024]{1,0:T(8,128)(2,1)S(1)}, bf16[384,1024]{1,0:T(8,128)(2,1)S(1)}, u32[]{:S(2)}, u32[]{:S(2)}) collective-permute-start(bf16[384,1024]{1,0:T(8,128)(2,1)S(1)} %get-tuple-element.277.e_ref), channel_id=1, source_target_pairs={{0,8},{4,12},{8,0},{12,4},{1,9},{5,13},{9,1},{13,5},{2,10},{6,14},... | collective-permute-start | bytes 2359304 | tf_op jit(solution)/shard_map/ppermute | solution.py:443
  480.6 164.7 %collective-permute-start.72 = (bf16[32,1024]{1,0:T(8,128)(2,1)}, bf16[32,1024]{1,0:T(8,128)(2,1)}, u32[]{:S(2)}, u32[]{:S(2)}) collective-permute-start(bf16[32,1024]{1,0:T(8,128)(2,1)} %get-tuple-element.340), channel_id=1, source_target_pairs={{0,1},{1,2},{2,3},{4,5},{5,6},{6,7},{8,9},{9,10},{10,11},{12,13},{... | collective-permute-start | bytes 196616 | tf_op jit(solution)/shard_map/ppermute | solution.py:484
  488.5 157.8 %collective-permute-start.75 = (bf16[32,1024]{1,0:T(8,128)(2,1)S(1)}, bf16[32,1024]{1,0:T(8,128)(2,1)}, u32[]{:S(2)}, u32[]{:S(2)}) collective-permute-start(bf16[32,1024]{1,0:T(8,128)(2,1)S(1)} %fusion.77), channel_id=1, source_target_pairs={{1,0},{2,1},{3,2},{5,4},{6,5},{7,6},{9,8},{10,9},{11,10},{13,12},{... | collective-permute-start | bytes 196616 | tf_op jit(solution)/shard_map/ppermute | solution.py:485
  525.3 62.8 %collective-permute-start.62 = (bf16[4,32,1024]{2,1,0:T(8,128)(2,1)}, bf16[4,32,1024]{2,1,0:T(8,128)(2,1)}, u32[]{:S(2)}, u32[]{:S(2)}) collective-permute-start(bf16[4,32,1024]{2,1,0:T(8,128)(2,1)} %select_bitcast_fusion.14), channel_id=1, source_target_pairs={{0,16},{16,0},{1,17},{17,1},{2,18},{18,2},{3,19},{19,3},{4,20},{20... | collective-permute-start | bytes 786440 | tf_op jit(solution)/shard_map/ppermute | solution.py:447
  645.2 38.8 %collective-permute-start.35 = (bf16[384,1024]{1,0:T(8,128)(2,1)}, bf16[384,1024]{1,0:T(8,128)(2,1)S(1)}, u32[]{:S(2)}, u32[]{:S(2)}) collective-permute-start(bf16[384,1024]{1,0:T(8,128)(2,1)} %shard_map.220), channel_id=1, source_target_pairs={{0,4},{4,0},{8,12},{12,8},{1,5},{5,1},{9,13},{13,9},{2,6},{6,2},{1... | collective-permute-start | bytes 2359304 | tf_op jit(solution)/shard_map/ppermute | solution.py:443
  646.2 43.7 %collective-permute-start.37 = (bf16[384,1024]{1,0:T(8,128)(2,1)}, bf16[384,1024]{1,0:T(8,128)(2,1)S(1)}, u32[]{:S(2)}, u32[]{:S(2)}) collective-permute-start(bf16[384,1024]{1,0:T(8,128)(2,1)} %shard_map.221), channel_id=1, source_target_pairs={{0,8},{4,12},{8,0},{12,4},{1,9},{5,13},{9,1},{13,5},{2,10},{6,14},... | collective-permute-start | bytes 2359304 | tf_op jit(solution)/shard_map/ppermute | solution.py:443
  661.9 19.5 %collective-permute-start.31 = (bf16[384,1024]{1,0:T(8,128)(2,1)S(1)}, bf16[384,1024]{1,0:T(8,128)(2,1)S(1)}, u32[]{:S(2)}, u32[]{:S(2)}) collective-permute-start(bf16[384,1024]{1,0:T(8,128)(2,1)S(1)} %copy-done.89), channel_id=1, source_target_pairs={{0,4},{4,0},{8,12},{12,8},{1,5},{5,1},{9,13},{13,9},{2,6},{6,2},{1... | collective-permute-start | bytes 2359304 | tf_op jit(solution)/shard_map/ppermute | solution.py:443
  662.9 19.7 %collective-permute-start.33 = (bf16[384,1024]{1,0:T(8,128)(2,1)S(1)}, bf16[384,1024]{1,0:T(8,128)(2,1)S(1)}, u32[]{:S(2)}, u32[]{:S(2)}) collective-permute-start(bf16[384,1024]{1,0:T(8,128)(2,1)S(1)} %copy-done.90), channel_id=1, source_target_pairs={{0,8},{4,12},{8,0},{12,4},{1,9},{5,13},{9,1},{13,5},{2,10},{6,14},... | collective-permute-start | bytes 2359304 | tf_op jit(solution)/shard_map/ppermute | solution.py:443
  664.3 45.8 %collective-permute-start.57 = (bf16[128,768]{0,1:T(8,128)(2,1)S(1)}, bf16[128,768]{0,1:T(8,128)(2,1)S(1)}, u32[]{:S(2)}, u32[]{:S(2)}) collective-permute-start(bf16[128,768]{0,1:T(8,128)(2,1)S(1)} %copy-done.66), channel_id=1, source_target_pairs={{0,1},{1,2},{2,3},{4,5},{5,6},{6,7},{8,9},{9,10},{10,11},{12,13},{... | collective-permute-start | bytes 589832 | tf_op jit(solution)/shard_map/ppermute | solution.py:484
  681.3 37.6 %collective-permute-start.60 = (bf16[128,768]{0,1:T(8,128)(2,1)S(1)}, bf16[128,768]{0,1:T(8,128)(2,1)S(1)}, u32[]{:S(2)}, u32[]{:S(2)}) collective-permute-start(bf16[128,768]{0,1:T(8,128)(2,1)S(1)} %copy-done.65), channel_id=1, source_target_pairs={{1,0},{2,1},{3,2},{5,4},{6,5},{7,6},{9,8},{10,9},{11,10},{13,12},{... | collective-permute-start | bytes 589832 | tf_op jit(solution)/shard_map/ppermute | solution.py:485
  709.4 19.9 %collective-permute-start.81 = (bf16[128,1024]{1,0:T(8,128)(2,1)S(1)}, bf16[128,1024]{1,0:T(8,128)(2,1)S(1)}, u32[]{:S(2)}, u32[]{:S(2)}) collective-permute-start(bf16[128,1024]{1,0:T(8,128)(2,1)S(1)} %get-tuple-element.314), channel_id=1, source_target_pairs={{3,2},{7,6},{11,10},{15,14},{19,18},{23,22},{27,26},{31,30}} | collective-permute-start | bytes 786440 | tf_op jit(solution)/shard_map/ppermute | solution.py:485
  712.2 18.4 %collective-permute-start.79 = (bf16[128,1024]{1,0:T(8,128)(2,1)S(1)}, bf16[128,1024]{1,0:T(8,128)(2,1)S(1)}, u32[]{:S(2)}, u32[]{:S(2)}) collective-permute-start(bf16[128,1024]{1,0:T(8,128)(2,1)S(1)} %fusion.58), channel_id=1, source_target_pairs={{0,1},{1,2},{4,5},{5,6},{8,9},{9,10},{12,13},{13,14},{16,17},{17,1... | collective-permute-start | bytes 786440 | tf_op jit(solution)/shard_map/ppermute | solution.py:484
  718.9 34.2 %collective-permute-start.102 = (bf16[128,1024]{1,0:T(8,128)(2,1)}, bf16[128,1024]{1,0:T(8,128)(2,1)}, u32[]{:S(2)}, u32[]{:S(2)}) collective-permute-start(bf16[128,1024]{1,0:T(8,128)(2,1)} %get-tuple-element.299), channel_id=1, source_target_pairs={{0,1},{1,2},{2,3},{4,5},{5,6},{6,7},{8,9},{9,10},{10,11},{12,13},{... | collective-permute-start | bytes 786440 | tf_op jit(solution)/shard_map/ppermute | solution.py:484
  724.8 37.6 %collective-permute-start.87 = (bf16[128,1024]{1,0:T(8,128)(2,1)}, bf16[128,1024]{1,0:T(8,128)(2,1)S(1)}, u32[]{:S(2)}, u32[]{:S(2)}) collective-permute-start(bf16[128,1024]{1,0:T(8,128)(2,1)} %get-tuple-element.307), channel_id=1, source_target_pairs={{0,1},{1,2},{2,3},{4,5},{5,6},{6,7},{8,9},{9,10},{10,11},{12,13},{... | collective-permute-start | bytes 786440 | tf_op jit(solution)/shard_map/ppermute | solution.py:484
  728.1 21.1 %collective-permute-start.38 = (bf16[384,1024]{1,0:T(8,128)(2,1)}, bf16[384,1024]{1,0:T(8,128)(2,1)}, u32[]{:S(2)}, u32[]{:S(2)}) collective-permute-start(bf16[384,1024]{1,0:T(8,128)(2,1)} %get-tuple-element.278), channel_id=1, source_target_pairs={{0,16},{16,0},{1,17},{17,1},{2,18},{18,2},{3,19},{19,3},{4,20},{20... | collective-permute-start | bytes 2359304 | tf_op jit(solution)/shard_map/ppermute | solution.py:447
  736.9 17.5 %collective-permute-start.105 = (bf16[128,1024]{1,0:T(8,128)(2,1)}, bf16[128,1024]{1,0:T(8,128)(2,1)S(1)}, u32[]{:S(2)}, u32[]{:S(2)}) collective-permute-start(bf16[128,1024]{1,0:T(8,128)(2,1)} %fusion.39), channel_id=1, source_target_pairs={{1,0},{2,1},{3,2},{5,4},{6,5},{7,6},{9,8},{10,9},{11,10},{13,12},{... | collective-permute-start | bytes 786440 | tf_op jit(solution)/shard_map/ppermute | solution.py:485
  739.4 20.2 %collective-permute-start.95 = (bf16[128,1024]{1,0:T(8,128)(2,1)}, bf16[128,1024]{1,0:T(8,128)(2,1)S(1)}, u32[]{:S(2)}, u32[]{:S(2)}) collective-permute-start(bf16[128,1024]{1,0:T(8,128)(2,1)} %get-tuple-element.303), channel_id=1, source_target_pairs={{0,1},{1,2},{2,3},{4,5},{5,6},{6,7},{8,9},{9,10},{10,11},{12,13},{... | collective-permute-start | bytes 786440 | tf_op jit(solution)/shard_map/ppermute | solution.py:484
  (150 other events, 2063.7 us)

commit v2 on v1

v2 whole, which is shorter than its diff:
```python
import functools
import math

import jax
import jax.numpy as jnp
from jax import lax
from jax.experimental import pallas as pl
from jax.experimental.pallas import tpu as pltpu
from jax.sharding import PartitionSpec as P

HEAD_DIM = 64
ROT = 16
EPSILON = 1e-05
MASKED = -1e30
TILE = 256
CHUNK = 512
SUB = 128
LANES = 128
BF = jnp.bfloat16
F32 = jnp.float32

VM = pltpu.VMEM
NT = (((1,), (1,)), ((), ()))
TN = (((0,), (0,)), ((), ()))


def dot_nn(a, b):
    return jnp.dot(a, b, preferred_element_type=F32)


def dot_nt(a, b):
    return lax.dot_general(a, b, NT, preferred_element_type=F32)


def dot_tn(a, b):
    return lax.dot_general(a, b, TN, preferred_element_type=F32)


def whole(shape):
    return pl.BlockSpec(shape, lambda *_: (0,) * len(shape))


SMEM_SPEC = pl.BlockSpec(memory_space=pltpu.SMEM)
ANY_SPEC = pl.BlockSpec(memory_space=pl.ANY)
PARAMS = pltpu.CompilerParams(vmem_limit_bytes=56 * 1024 * 1024)


def cost(flops, moved):
    return pl.CostEstimate(flops=int(flops), bytes_accessed=int(moved), transcendentals=0)


def norm_rows(rows):
    centre = jnp.mean(rows, axis=-1, keepdims=True)
    shifted = rows - centre
    inverse_std = lax.rsqrt(jnp.mean(shifted * shifted, axis=-1, keepdims=True) + EPSILON)
    return shifted * inverse_std, inverse_std


def turn(values, tables, direction):
    cos_t, sin_a, sin_b = tables
    width = values.shape[-1]
    times = width // LANES
    wide = lambda t: jnp.concatenate([t] * times, axis=1)
    ahead = pltpu.roll(values, width - ROT // 2, 1)
    behind = pltpu.roll(values, ROT // 2, 1)
    return values * wide(cos_t) + direction * (ahead * wide(sin_a) + behind * wide(sin_b))


SLOTS = (1, 2, 0, 3)
OWN, NEAR, FAR, ENDS = (1, 2), (2, 0), (1, 3), (2, 1)


def stacked(refs):
    parts = [r[...] for r in refs]
    return parts[0] if len(parts) == 1 else jnp.concatenate(parts, axis=0)


def pre_kernel(n_x, n_alias, *refs):
    x_refs = refs[:n_x]
    (gain_ref, bias_ref, wqkv_ref, bqkv_ref, win_ref, bin_ref, cos_ref, sa_ref, sb_ref) = refs[n_x:n_x + 9]
    n1_ref, n2_ref, q_ref, k_ref, v_ref, g_ref, slope_ref, n2_keep = refs[n_x + 9 + n_alias:]

    @pl.when(pl.program_id(0) == 0)
    def _():
        normal, _ = norm_rows(stacked(x_refs).astype(F32))
        gains = gain_ref[...].astype(F32)
        biases = bias_ref[...].astype(F32)
        n1 = (normal * gains[0:1] + biases[0:1]).astype(BF)
        n2 = (normal * gains[1:2] + biases[1:2]).astype(BF)
        n1_ref[...] = n1.reshape(n1_ref.shape)
        n2_ref[...] = n2.reshape(n2_ref.shape)
        n2_keep[...] = n2
        flat = lambda r: r[...].reshape(n1.shape[0], LANES)
        tables = (flat(cos_ref), flat(sa_ref), flat(sb_ref))
        wide = q_ref.shape[-1]
        scale = 1.0 / math.sqrt(HEAD_DIM)
        bq = bqkv_ref[...].astype(F32)
        part = lambda i: dot_nn(n1, wqkv_ref[:, i * wide:(i + 1) * wide]) + bq[:, i * wide:(i + 1) * wide]
        q = (turn(part(0), tables, 1.0).astype(BF).astype(F32) * scale).astype(BF)
        q_ref[...] = q.reshape(q_ref.shape)
        k_ref[...] = turn(part(1), tables, 1.0).astype(BF).reshape(k_ref.shape)
        v_ref[...] = part(2).astype(BF).reshape(v_ref.shape)

    f = dot_nn(n2_keep[...], win_ref[...]) + bin_ref[...].astype(F32)
    phi = 0.5 * (1.0 + lax.erf(f * (1.0 / math.sqrt(2.0))))
    density = jnp.exp(-0.5 * f * f) * (1.0 / math.sqrt(2.0 * math.pi))
    g_ref[...] = (f * phi).astype(BF).reshape(g_ref.shape)
    slope_ref[...] = (phi + f * density).astype(BF).reshape(slope_ref.shape)


def group_call(kernel, args, in_specs, outs, kept, grid, scratch, price):
    n_alias = 0 if kept is None else len(outs)
    specs = list(in_specs)
    operands = list(args)
    aliases = {}
    if kept is not None:
        for i, buf in enumerate(kept):
            aliases[len(operands)] = i
            operands.append(buf)
            specs.append(ANY_SPEC)
    return pl.pallas_call(
        functools.partial(kernel, n_alias),
        grid=grid,
        in_specs=specs,
        out_specs=[pl.BlockSpec(block, index) for _, _, block, index in outs],
        out_shape=[jax.ShapeDtypeStruct(shape, dtype) for shape, dtype, _, _ in outs],
        input_output_aliases=aliases,
        scratch_shapes=scratch,
        compiler_params=PARAMS,
        cost_estimate=price,
    )(*operands)


def pre_group(group, xs, lp, tables, kept):
    size, at = group
    d = xs[0].shape[1]
    slots, rows = len(SLOTS), tables[0].shape[1]
    total = size * rows
    wide = lp["w_qkv"].shape[1]
    units = lp["w_in"].shape[1]
    cols = wide // 3
    ck = min(CHUNK, units)
    first = lambda j: (at, 0, 0)
    moving = lambda j: (at, 0, j)
    outs = [((slots, rows, d), BF, (size, rows, d), first)] * 2
    outs += [((slots, rows, cols), BF, (size, rows, cols), first)] * 3
    outs += [((slots, rows, units), BF, (size, rows, ck), moving)] * 2
    in_specs = [whole(x.shape) for x in xs]
    in_specs += [whole((2, d)), whole((2, d)), whole((d, wide)), whole((1, wide)),
                 pl.BlockSpec((d, ck), lambda j: (0, j)), pl.BlockSpec((1, ck), lambda j: (0, j))]
    in_specs += [pl.BlockSpec((size, rows, LANES), first)] * 3
    args = [*xs, lp["ln_gain"], lp["ln_bias"], lp["w_qkv"], lp["b_qkv"], lp["w_in"], lp["b_in"], *tables]
    return group_call(functools.partial(pre_kernel, len(xs)), args, in_specs, outs, kept, (units // ck,),
                      [VM((total, d), BF)],
                      cost(2 * total * d * (wide + units), 2 * d * (wide + units) + 10 * total * d))


def share(part, addend_refs, outs):
    if len(outs) == 3:
        own, far_a, far_b = outs
        rows, half = own.shape[0], far_a.shape[0]
        own[...] = part[:rows]
        far_a[...] = part[rows:rows + half].astype(BF)
        far_b[...] = part[rows + half:].astype(BF)
        return
    one, two = outs
    from_two, from_one = addend_refs
    rows, half = one.shape[0], from_two.shape[0]
    one[:half, :] = part[:half].astype(BF)
    one[half:, :] = (part[half:rows] + from_two[...].astype(F32)).astype(BF)
    two[:half, :] = (part[rows:rows + half] + from_one[...].astype(F32)).astype(BF)
    two[half:, :] = part[rows + half:].astype(BF)


def share_specs(group, rows, d, ck):
    col = lambda j: (0, j)
    if group == ENDS:
        shapes = [((rows, d), F32), ((rows // 2, d), BF), ((rows // 2, d), BF)]
    else:
        shapes = [((rows, d), BF), ((rows, d), BF)]
    return [pl.BlockSpec((s[0], ck), col) for s, _ in shapes], [jax.ShapeDtypeStruct(s, t) for s, t in shapes]


def post_kernel(n_add, o_ref, g_ref, wout_ref, wfc_ref, *rest):
    total = o_ref.shape[0] * o_ref.shape[1]
    o = o_ref[...].reshape(total, o_ref.shape[-1])
    g = g_ref[...].reshape(total, g_ref.shape[-1])
    share(dot_nn(o, wout_ref[...]) + dot_nn(g, wfc_ref[...]), rest[:n_add], rest[n_add:])


def post_group(group, o_all, g_all, lp, addends):
    size, at = group
    _, rows, cols = o_all.shape
    units, d = lp["w_fc2"].shape
    ck = min(CHUNK, d)
    fixed = lambda j: (at, 0, 0)
    in_specs = [pl.BlockSpec((size, rows, cols), fixed), pl.BlockSpec((size, rows, units), fixed),
                pl.BlockSpec((cols, ck), lambda j: (0, j)), pl.BlockSpec((units, ck), lambda j: (0, j))]
    in_specs += [pl.BlockSpec((a.shape[0], ck), lambda j: (0, j)) for a in addends]
    out_specs, out_shape = share_specs(group, rows, d, ck)
    total = size * rows
    return pl.pallas_call(
        functools.partial(post_kernel, len(addends)),
        grid=(d // ck,),
        in_specs=in_specs,
        out_specs=out_specs,
        out_shape=out_shape,
        compiler_params=PARAMS,
        cost_estimate=cost(2 * total * d * (cols + units), 2 * d * (cols + units) + 5 * total * d),
    )(o_all, g_all, lp["w_out"], lp["w_fc2"], *addends)


def bpre_kernel(n_x, n_alias, *refs):
    e_refs = refs[:n_x]
    wout_ref, wfc_ref, slope_ref = refs[n_x:n_x + 3]
    eall_ref, do_ref, df_ref, sums_ref = refs[n_x + 3 + n_alias:]
    e = stacked(e_refs)

    @pl.when(pl.program_id(0) == 0)
    def _():
        eall_ref[...] = e.reshape(eall_ref.shape)
        do_ref[...] = dot_nt(e, wout_ref[...]).astype(BF).reshape(do_ref.shape)

    back = dot_nt(e, wfc_ref[...])
    df = (back * slope_ref[...].reshape(back.shape).astype(F32)).astype(BF)
    df_ref[...] = df.reshape(df_ref.shape)
    sums = jnp.sum(df.astype(F32).reshape(df_ref.shape), axis=1, keepdims=True)
    sums_ref[...] = sums


def bpre_group(group, es, slope_all, lp, kept):
    size, at = group
    d = es[0].shape[1]
    slots, rows, units = slope_all.shape
    cols = lp["w_out"].shape[0]
    ck = min(CHUNK, units)
    first = lambda j: (at, 0, 0)
    moving = lambda j: (at, 0, j)
    outs = [((slots, rows, d), BF, (size, rows, d), first), ((slots, rows, cols), BF, (size, rows, cols), first),
            ((slots, rows, units), BF, (size, rows, ck), moving), ((slots, 1, units), F32, (size, 1, ck), moving)]
    in_specs = [whole(e.shape) for e in es]
    in_specs += [whole((cols, d)), pl.BlockSpec((ck, d), lambda j: (j, 0)),
                 pl.BlockSpec((size, rows, ck), moving)]
    args = [*es, lp["w_out"], lp["w_fc2"], slope_all]
    total = size * rows
    return group_call(functools.partial(bpre_kernel, len(es)), args, in_specs, outs, kept, (units // ck,), [],
                      cost(2 * total * d * (cols + units), 2 * d * (cols + units) + 8 * total * d))


def bpost_kernel(n_x, n_add, ck, *refs):
    x_refs = refs[:n_x]
    gain_ref, dqkv_ref, df_ref, wqkv_ref, win_ref = refs[n_x:n_x + 5]
    addend_refs = refs[n_x + 5:n_x + 5 + n_add]
    outs = refs[n_x + 5 + n_add:-2]
    sums_ref, normal_keep = refs[-2:]
    j = pl.program_id(0)

    @pl.when(j == 0)
    def _():
        normal, _ = norm_rows(stacked(x_refs).astype(F32))
        for c in range(normal_keep.shape[0]):
            normal_keep[c] = normal[:, c * ck:(c + 1) * ck]

    normal = normal_keep[j]
    flat = lambda r: r[...].reshape(normal.shape[0], r.shape[-1])
    one = dot_nt(flat(dqkv_ref), wqkv_ref[...])
    two = dot_nt(flat(df_ref), win_ref[...])
    total = lambda v: jnp.sum(v, axis=0, keepdims=True)
    sums_ref[0:1, :] = total(one * normal)
    sums_ref[1:2, :] = total(two * normal)
    sums_ref[2:3, :] = total(one)
    sums_ref[3:4, :] = total(two)
    gains = gain_ref[...].astype(F32)
    share(one * gains[0:1] + two * gains[1:2], addend_refs, outs)


def bpost_group(group, xs, dqkv_all, df_all, lp, addends):
    size, at = group
    d = xs[0].shape[1]
    _, rows, wide = dqkv_all.shape
    units = df_all.shape[-1]
    ck = min(CHUNK, d)
    total = size * rows
    fixed = lambda j: (at, 0, 0)
    in_specs = [whole(x.shape) for x in xs]
    in_specs += [pl.BlockSpec((2, ck), lambda j: (0, j)),
                 pl.BlockSpec((size, rows, wide), fixed), pl.BlockSpec((size, rows, units), fixed),
                 pl.BlockSpec((ck, wide), lambda j: (j, 0)), pl.BlockSpec((ck, units), lambda j: (j, 0))]
    in_specs += [pl.BlockSpec((a.shape[0], ck), lambda j: (0, j)) for a in addends]
    out_specs, out_shape = share_specs(group, rows, d, ck)
    return pl.pallas_call(
        functools.partial(bpost_kernel, len(xs), len(addends), ck),
        grid=(d // ck,),
        in_specs=in_specs,
        out_specs=out_specs + [pl.BlockSpec((4, ck), lambda j: (0, j))],
        out_shape=out_shape + [jax.ShapeDtypeStruct((4, d), F32)],
        scratch_shapes=[VM((d // ck, total, ck), F32)],
        compiler_params=PARAMS,
        cost_estimate=cost(2 * total * d * (wide + units), 2 * d * (wide + units) + 7 * total * d),
    )(*xs, lp["ln_gain"], dqkv_all, df_all, lp["w_qkv"], lp["w_in"], *addends)


def wgrad_kernel(with_out, core_ref, *refs):
    first = core_ref[0] == 0
    if with_out:
        keep_ref, give_ref, whole_out = refs[-3:]
        pairs = list(refs[2:-3])
    else:
        keep_ref, give_ref = refs[-2:]
        pairs = list(refs[:-2])
    many, half, _ = keep_ref.shape

    def store(b, rows, cols, zero, one):
        keep_ref[b, rows, cols] = jnp.where(first, zero, one).astype(BF)
        give_ref[b, rows, cols] = jnp.where(first, one, zero).astype(BF)

    at = 0
    if with_out:
        o_ref, e_ref = refs[:2]
        cols = o_ref.shape[1]
        j = pl.program_id(0)

        @pl.when(j == 0)
        def _():
            whole_out[...] = dot_tn(o_ref[...], e_ref[...])

        groups = e_ref.shape[1] // cols
        few = half // groups
        for b in range(many):
            start = 2 * (j * many + b)
            zero, one = [whole_out[pl.ds(pl.multiple_of((start + h) * few, few), few), :] for h in range(2)]
            for c in range(groups):
                part = slice(c * cols, (c + 1) * cols)
                store(b, slice(c * few, (c + 1) * few), slice(0, cols), zero[:, part], one[:, part])
        at = cols
        pairs.append(e_ref)
    for a_ref, b_ref in zip(pairs[0::2], pairs[1::2]):
        wide = b_ref.shape[1]
        product = dot_tn(a_ref[...], b_ref[...])
        for b in range(many):
            low = 2 * b * half
            store(b, slice(None), slice(at, at + wide), product[low:low + half], product[low + half:low + 2 * half])
        at += wide


def wgrad_shapes(d, cols):
    n = lax.axis_size("dp")
    block = d // n
    lanes = max(block, LANES)
    many = lanes // block
    specs = [pl.BlockSpec((many, block // 2, cols), lambda j: (j, 0, 0))] * 2
    shapes = [jax.ShapeDtypeStruct((n, block // 2, cols), BF)] * 2
    return d // lanes, lanes, specs, shapes


def wgrad_early(core, o, e, n2, df, g):
    length, d = e.shape
    cols = o.shape[1] + df.shape[1] + d
    steps, lanes, specs, shapes = wgrad_shapes(d, cols)
    moving = pl.BlockSpec((length, lanes), lambda j: (0, j))
    return pl.pallas_call(
        functools.partial(wgrad_kernel, True),
        grid=(steps,),
        in_specs=[SMEM_SPEC, whole(o.shape), whole(e.shape), moving, whole(df.shape), moving],
        out_specs=specs,
        out_shape=shapes,
        scratch_shapes=[VM((o.shape[1], d), F32)],
        compiler_params=PARAMS,
        cost_estimate=cost(2 * length * d * cols, 2 * length * 4 * d + 2 * d * cols),
    )(core, o, e, n2, df, g)


def wgrad_late(core, n1, dqkv):
    length, d = n1.shape
    cols = dqkv.shape[1]
    steps, lanes, specs, shapes = wgrad_shapes(d, cols)
    return pl.pallas_call(
        functools.partial(wgrad_kernel, False),
        grid=(steps,),
        in_specs=[SMEM_SPEC, pl.BlockSpec((length, lanes), lambda j: (0, j)), whole(dqkv.shape)],
        out_specs=specs,
        out_shape=shapes,
        compiler_params=PARAMS,
        cost_estimate=cost(2 * length * d * cols, 2 * length * 2 * d + 2 * d * cols),
    )(core, n1, dqkv)


def head_lanes(shape):
    return lax.broadcasted_iota(jnp.int32, shape, len(shape) - 1) // HEAD_DIM


def attend_kernel(order_ref, low_ref, q_ref, k_ref, v_ref, start_ref, o_ref, lse_ref,
                  k_abs, v_turned, acc, qm, top, tot):
    subs, _, cols = q_ref.shape
    heads = cols // HEAD_DIM
    per = TILE // SUB
    blocks = subs // per
    for b in range(blocks):
        pair = [order_ref[b * per + u] for u in range(per)]
        k_abs[b * TILE:(b + 1) * TILE, :] = jnp.concatenate([k_ref[s] for s in pair], axis=0)
        v_turned[b] = jnp.transpose(jnp.concatenate([v_ref[s] for s in pair], axis=0))

    def one_query(qb, _):
        srcs = [order_ref[qb * per + u] for u in range(per)]
        q = jnp.concatenate([q_ref[s] for s in srcs], axis=0)
        base = qb * TILE
        starts = start_ref[qb]
        places = base + lax.broadcasted_iota(jnp.int32, (1, TILE), 1)
        group = head_lanes(q.shape)
        for h in range(heads):
            qm[h] = jnp.where(group == h, q, jnp.zeros_like(q))
        down = lax.broadcasted_iota(jnp.int32, (TILE, TILE), 0)

        def scores(kb):
            at = pl.multiple_of(kb * TILE, TILE)
            keys = k_abs[pl.ds(at, TILE), :]
            allowed = jnp.logical_and(down + at >= starts, down + at <= places)
            return [jnp.where(allowed, dot_nt(keys, qm[h]), MASKED) for h in range(heads)]

        found = scores(qb)
        for h in range(heads):
            lanes = slice(h * HEAD_DIM, (h + 1) * HEAD_DIM)
            m = jnp.max(found[h], axis=0, keepdims=True)
            p = jnp.exp(found[h] - m)
            top[h] = m
            tot[h] = jnp.sum(p, axis=0, keepdims=True)
            acc[lanes, :] = dot_nn(v_turned[qb, lanes, :], p.astype(BF))

        def one_key(kb, _):
            found = scores(kb)
            for h in range(heads):
                lanes = slice(h * HEAD_DIM, (h + 1) * HEAD_DIM)
                old = top[h]
                m = jnp.maximum(old, jnp.max(found[h], axis=0, keepdims=True))
                fade = jnp.exp(old - m)
                p = jnp.exp(found[h] - m)
                top[h] = m
                tot[h] = tot[h] * fade + jnp.sum(p, axis=0, keepdims=True)
                acc[lanes, :] = acc[lanes, :] * fade + dot_nn(v_turned[kb, lanes, :], p.astype(BF))
            return 0

        lax.fori_loop(low_ref[qb], qb, one_key, 0)
        for h in range(heads):
            lanes = slice(h * HEAD_DIM, (h + 1) * HEAD_DIM)
            acc[lanes, :] = acc[lanes, :] / tot[h]
            lse_ref[qb, h:h + 1, :] = top[h] + jnp.log(tot[h])
        out = jnp.transpose(acc[...]).astype(BF)
        for u in range(per):
            o_ref[srcs[u]] = out[u * SUB:(u + 1) * SUB]
        return 0

    lax.fori_loop(0, blocks, one_query, 0)


def attend(order, low, q, k, v, start_rows):
    subs, _, cols = q.shape
    length = subs * SUB
    heads = cols // HEAD_DIM
    blocks = length // TILE
    full = [whole(a.shape) for a in (q, k, v, start_rows)]
    return pl.pallas_call(
        attend_kernel,
        grid=(1,),
        in_specs=[SMEM_SPEC, SMEM_SPEC] + full,
        out_specs=[whole(q.shape), whole((blocks, 8, TILE))],
        out_shape=[jax.ShapeDtypeStruct(q.shape, BF), jax.ShapeDtypeStruct((blocks, 8, TILE), F32)],
        scratch_shapes=[VM((length, cols), BF), VM((blocks, cols, TILE), BF), VM((cols, TILE), F32),
                        VM((heads, TILE, cols), BF), VM((heads, 1, TILE), F32), VM((heads, 1, TILE), F32)],
        compiler_params=PARAMS,
        cost_estimate=cost(3 * length * length * cols, 5 * length * cols),
    )(order, low, q, k, v, start_rows)


def attend_back_kernel(order_ref, low_ref, q_ref, k_ref, v_ref, do_ref, o_ref, lse_ref, start_ref,
                       cos_ref, sa_ref, sb_ref, out_ref, sums_ref,
                       k_abs, v_abs, km, dk, dv, dq, qm, dom, stat):
    subs, _, cols = q_ref.shape
    heads = cols // HEAD_DIM
    per = TILE // SUB
    scale = 1.0 / math.sqrt(HEAD_DIM)
    for i in range(subs):
        src = order_ref[i]
        rows = slice(i * SUB, (i + 1) * SUB)
        key = k_ref[src]
        k_abs[rows, :] = key
        v_abs[rows, :] = v_ref[src]
        for h in range(heads):
            km[h, rows, :] = jnp.where(head_lanes(key.shape) == h, key, jnp.zeros_like(key))
        dk[rows, :] = jnp.zeros((SUB, cols), F32)
        dv[rows, :] = jnp.zeros((SUB, cols), F32)
    sums_ref[...] = jnp.zeros(sums_ref.shape, F32)

    def tables(src):
        return cos_ref[src], sa_ref[src], sb_ref[src]

    def emit(src, at, values):
        low = values.astype(BF)
        out_ref[src, :, at:at + cols] = low
        sums_ref[:, at:at + cols] += jnp.sum(low.astype(F32), axis=0, keepdims=True)

    def one_query(qb, _):
        base = pl.multiple_of(qb * TILE, TILE)
        srcs = [order_ref[qb * per + u] for u in range(per)]
        q = jnp.concatenate([q_ref[s] for s in srcs], axis=0)
        do = jnp.concatenate([do_ref[s] for s in srcs], axis=0)
        o = jnp.concatenate([o_ref[s] for s in srcs], axis=0)
        group = head_lanes(q.shape)
        logs = lse_ref[qb]
        inner = jnp.transpose(do.astype(F32) * o.astype(F32))
        for h in range(heads):
            qm[h] = jnp.where(group == h, q, jnp.zeros_like(q))
            dom[h] = jnp.where(group == h, do, jnp.zeros_like(do))
            stat[h, 0:1, :] = logs[h:h + 1, :]
            stat[h, 1:2, :] = jnp.sum(inner[h * HEAD_DIM:(h + 1) * HEAD_DIM, :], axis=0, keepdims=True)
        dq[...] = jnp.zeros((TILE, cols), F32)
        starts = start_ref[qb]
        places = base + lax.broadcasted_iota(jnp.int32, (1, TILE), 1)
        down = lax.broadcasted_iota(jnp.int32, (TILE, TILE), 0)

        def one_key(kb, _):
            at = pl.multiple_of(kb * TILE, TILE)
            keys = k_abs[pl.ds(at, TILE), :]
            vals = v_abs[pl.ds(at, TILE), :]
            allowed = jnp.logical_and(down + at >= starts, down + at <= places)
            dk_new = dv_new = dq_new = None
            more = lambda old, new: new if old is None else old + new
            for h in range(heads):
                s = dot_nt(keys, qm[h])
                p = jnp.exp(jnp.where(allowed, s - stat[h, 0:1, :], MASKED))
                dp = dot_nt(vals, dom[h])
                ds = (p * (dp - stat[h, 1:2, :])).astype(BF)
                dv_new = more(dv_new, dot_nn(p.astype(BF), dom[h]))
                dk_new = more(dk_new, dot_nn(ds, qm[h]))
                dq_new = more(dq_new, dot_tn(ds, km[h, pl.ds(at, TILE), :]))
            dv[pl.ds(at, TILE), :] += dv_new
            dk[pl.ds(at, TILE), :] += dk_new
            dq[...] += dq_new
            return 0

        lax.fori_loop(low_ref[qb], qb + 1, one_key, 0)
        for u in range(per):
            emit(srcs[u], 0, turn(dq[u * SUB:(u + 1) * SUB, :] * scale, tables(srcs[u]), -1.0))
        return 0

    lax.fori_loop(0, subs // per, one_query, 0)
    for i in range(subs):
        src = order_ref[i]
        rows = slice(i * SUB, (i + 1) * SUB)
        emit(src, cols, turn(dk[rows, :], tables(src), -1.0))
        emit(src, 2 * cols, dv[rows, :])


def attend_back(order, low, q, k, v, do, o, lse, start_rows, tables):
    subs, _, cols = q.shape
    length = subs * SUB
    heads = cols // HEAD_DIM
    args = (q, k, v, do, o, lse, start_rows, *tables)
    return pl.pallas_call(
        attend_back_kernel,
        grid=(1,),
        in_specs=[SMEM_SPEC, SMEM_SPEC] + [whole(a.shape) for a in args],
        out_specs=[whole((subs, SUB, 3 * cols)), whole((1, 3 * cols))],
        out_shape=[jax.ShapeDtypeStruct((subs, SUB, 3 * cols), BF), jax.ShapeDtypeStruct((1, 3 * cols), F32)],
        scratch_shapes=[VM((length, cols), BF), VM((length, cols), BF), VM((heads, length, cols), BF),
                        VM((length, cols), F32), VM((length, cols), F32), VM((TILE, cols), F32),
                        VM((heads, TILE, cols), BF), VM((heads, TILE, cols), BF), VM((heads, 2, TILE), F32)],
        compiler_params=PARAMS,
        cost_estimate=cost(8 * length * length * cols, 16 * length * cols),
    )(order, low, *args)


def across(x, k):
    n = lax.axis_size("tensor")
    return lax.ppermute(x, "tensor", [(i, i ^ k) for i in range(n)])


def swap(x):
    return lax.ppermute(x, "pipe", [(0, 1), (1, 0)])


def gather_and_run(x, call, beside=None):
    half = x.shape[0] // 2
    one, two = across(x, 1), across(x, 2)
    kept = call(OWN, [x], None)
    one, two, kept = lax.optimization_barrier((one, two, kept))
    far_a = across(one[:half], 2)
    far_b = across(two[half:], 1)
    kept = call(NEAR, [one, two], kept)
    far_a, far_b, kept, beside = lax.optimization_barrier((far_a, far_b, kept, beside))
    kept = call(FAR, [far_a, far_b], kept)
    return (x, one, two, far_a, far_b), kept, beside


def add_rows(own, got_one, got_two):
    return own + got_one.astype(F32) + got_two.astype(F32)


def dp_reduce(blocks):
    n, rows, cols = blocks.shape
    return lax.psum_scatter(blocks.reshape(n * rows, cols), "dp", scatter_dimension=0, tiled=True)


def butterfly(vec, axis):
    n = lax.axis_size(axis)
    k = 1
    while k < n:
        vec = vec + lax.ppermute(vec, axis, [(i, i ^ k) for i in range(n)])
        k *= 2
    return vec


def flat(a):
    return a.reshape(-1, SUB, a.shape[-1])


NAMES = ("w_qkv", "w_out", "w_in", "w_fc2")


def rows2(a):
    return a.reshape(-1, a.shape[-1])


def forward_layer(x, lp, geo, beside=None):
    call = lambda group, xs, kept: pre_group(group, xs, lp, geo["tables"], kept)
    rows, kept, beside = gather_and_run(x, call, beside)
    n1, n2, q, k, v, g, slope = kept
    o, lse = attend(geo["order"], geo["low"], flat(q), flat(k), flat(v), geo["start_rows"])
    o_slots = o.reshape(q.shape)
    own, far_a, far_b = post_group(ENDS, o_slots, g, lp, [])
    from_one, from_two = across(far_a, 1), across(far_b, 2)
    one, two = post_group(NEAR, o_slots, g, lp, [from_two, from_one])
    summed = add_rows(own, across(one, 1), across(two, 2))
    out_biases = lp["out_bias"].astype(F32)
    result = x.astype(F32) + summed + out_biases[0] + out_biases[1]
    saved = dict(rows=rows, n1=n1, n2=n2, q=flat(q), k=flat(k), v=flat(v), g=g, slope=slope, o=o, lse=lse)
    return result.astype(BF), saved, beside


def over_chip(pair):
    return (pair[0].astype(F32) + swap(pair[1]).astype(F32)).astype(BF)


def backward_layer(e, lp, saved, geo, core, last):
    call = lambda group, es, kept: bpre_group(group, es, saved["slope"], lp, kept)
    _, (e_all, do, df, bin_parts), _ = gather_and_run(e, call)
    early = wgrad_early(core, rows2(saved["o"]), rows2(e_all), rows2(saved["n2"]), rows2(df), rows2(saved["g"]))
    if last:
        early, do = lax.optimization_barrier((over_chip(early), do))
        early = dp_reduce(early)
    dqkv, bqkv_grad = attend_back(geo["order"], geo["low"], saved["q"], saved["k"], saved["v"], flat(do),
                                  saved["o"], saved["lse"], geo["start_rows"], geo["flat_tables"])
    x, x_one, x_two, x_far_a, x_far_b = saved["rows"]
    dqkv_slots = dqkv.reshape(*df.shape[:2], dqkv.shape[-1])
    own, far_a, far_b, sums_a = bpost_group(ENDS, [x, x_far_a, x_far_b], dqkv_slots, df, lp, [])
    from_one, from_two = across(far_a, 1), across(far_b, 2)
    late = wgrad_late(core, rows2(saved["n1"]), rows2(dqkv))
    late, from_one, from_two = lax.optimization_barrier((late, from_one, from_two))
    one, two, sums_b = bpost_group(NEAR, [x_one, x_two], dqkv_slots, df, lp, [from_two, from_one])
    got_one, got_two = across(one, 1), across(two, 2)
    if not last:
        early, got_one, got_two = lax.optimization_barrier((early, got_one, got_two))
        early = dp_reduce(over_chip(early))
    u = add_rows(own, got_one, got_two)
    late = dp_reduce(over_chip(late))
    x_rows, e_rows = x.astype(F32), e.astype(F32)
    normal, inverse_std = norm_rows(x_rows)
    mean_grad = jnp.mean(u, axis=-1, keepdims=True)
    mean_cross = jnp.mean(u * normal, axis=-1, keepdims=True)
    dx = e_rows + (u - mean_grad - normal * mean_cross) * inverse_std
    small = jnp.concatenate([sums_a + sums_b, jnp.sum(e_rows, axis=0, keepdims=True)], axis=0)
    bias_grads = jnp.concatenate([bqkv_grad[0], jnp.sum(bin_parts, axis=(0, 1))])
    return dx.astype(BF), (early, late), small, bias_grads


def unpack_out(g, rows, d):
    groups = d // rows
    return jnp.swapaxes(g.reshape(groups, -1, rows), 0, 1).reshape(-1, d)


def column_order(a, direction):
    shape = a.shape
    heads = shape[-1] // (3 * HEAD_DIM)
    dims = (heads, 3) if direction > 0 else (3, heads)
    split = a.reshape(*shape[:-1], *dims, HEAD_DIM)
    return jnp.swapaxes(split, -2, -3).reshape(shape)


def body(ends, segments, ln_gain, ln_bias, w_qkv, b_qkv, w_out, w_in, b_in, w_fc2, out_bias):
    is_first = lax.axis_index("pipe") == 0
    me = lax.axis_index("tensor")
    n_tensor = lax.axis_size("tensor")
    choose = lambda a, b: jnp.where(is_first, a, b)
    shares = ends[0]
    rows, d = shares.shape[1:]

    got = swap(shares)
    x0 = choose(shares[0], got[1])
    e1 = choose(got[0], shares[1])

    own = dict(ln_gain=ln_gain[0], ln_bias=ln_bias[0], w_qkv=column_order(w_qkv[0], 1),
               b_qkv=column_order(b_qkv, 1), w_out=w_out[0], w_in=w_in[0], b_in=b_in, w_fc2=w_fc2[0],
               out_bias=out_bias[0])
    small_names = ("ln_gain", "ln_bias", "b_qkv", "b_in", "out_bias")
    packed = jnp.concatenate([own[s].reshape(-1) for s in small_names]).reshape(-1, LANES)
    other_packed = swap(packed).reshape(-1)
    other = {name: swap(own[name]) for name in NAMES}
    at = 0
    for s in small_names:
        other[s] = other_packed[at:at + own[s].size].reshape(own[s].shape)
        at += own[s].size
    layer0 = {name: choose(own[name], other[name]) for name in own}
    layer1 = {name: choose(other[name], own[name]) for name in own}

    segment_row = choose(segments[0], segments[1])
    length = segment_row.shape[0]
    places = jnp.arange(length, dtype=jnp.int32)
    begins = jnp.concatenate([jnp.ones((1,), dtype=jnp.bool_), segment_row[1:] != segment_row[:-1]])
    starts = lax.cummax(jnp.where(begins, places, 0), axis=0)
    slot_index = jnp.array(SLOTS, dtype=jnp.int32) ^ me
    by_slot = jnp.take((places - starts).reshape(n_tensor, rows), slot_index, axis=0)
    x0, by_slot = lax.optimization_barrier((x0, by_slot))
    lane = jnp.arange(LANES, dtype=jnp.int32) % HEAD_DIM
    half_rot = ROT // 2
    frequency = jnp.power(10000.0, -2.0 * (lane % half_rot).astype(F32) / ROT)
    angles = by_slot.astype(F32)[:, :, None] * frequency
    sines = jnp.sin(angles)
    tables = (jnp.where(lane < ROT, jnp.cos(angles), 1.0),
              jnp.where(lane < half_rot, -sines, 0.0),
              jnp.where(jnp.logical_and(lane >= half_rot, lane < ROT), sines, 0.0))
    per = rows // SUB
    subs = jnp.arange(length // SUB, dtype=jnp.int32)
    place_of = jnp.array([SLOTS.index(k) for k in range(n_tensor)], dtype=jnp.int32)
    tables = lax.optimization_barrier(tables)
    geo = dict(
        tables=tables,
        flat_tables=[flat(t) for t in tables],
        order=(place_of[(subs // per) ^ me] * per + subs % per).astype(jnp.int32),
        low=(starts.reshape(-1, TILE)[:, 0] // TILE).astype(jnp.int32),
        start_rows=starts.reshape(-1, 1, TILE),
    )

    core = lax.axis_index("pipe").astype(jnp.int32).reshape(1)
    h, saved0, _ = forward_layer(x0, layer0, geo)
    y1, saved1, e1 = forward_layer(h, layer1, geo, e1)
    e0, half1, small1, bias1 = backward_layer(e1, layer1, saved1, geo, core, False)
    dx0, half0, small0, bias0 = backward_layer(e0, layer0, saved0, geo, core, True)

    got = swap(choose(y1, dx0))
    mine = choose(dx0, y1)
    boundary = jnp.stack([choose(mine, got), choose(got, mine)])[None]

    full = []
    for one, zero in zip(half1, half0):
        got = swap(choose(one, zero))
        mine = choose(zero, one)
        full.append((choose(mine, got).astype(F32), choose(got, mine).astype(F32)))
    early, g_qkv = full
    n_out, n_in = w_out.shape[1], w_in.shape[2]
    join = lambda f: jnp.concatenate([f(early[0]), f(early[1])], axis=0)
    g_out = join(lambda a: unpack_out(a[:, :n_out], n_out, d))
    g_in = join(lambda a: a[:, n_out:n_out + n_in])
    g_fc2 = join(lambda a: a[:, n_out + n_in:])
    g_qkv = jnp.concatenate(g_qkv, axis=0)

    n_dp = lax.axis_size("dp")
    small = choose(small0, small1) + swap(choose(small1, small0))
    bias = choose(bias0, bias1) + swap(choose(bias1, bias0))
    at = small.size
    line = butterfly(jnp.concatenate([small.reshape(-1), bias]), "dp")
    small, bias = line[:at].reshape(small.shape), line[at:]
    small = butterfly(small, "tensor").reshape(small.shape[0], n_tensor * n_dp, -1)
    where = lax.axis_index("dp")
    pick = lambda a, i: lax.dynamic_index_in_dim(a, i, -2, keepdims=False)
    sums = pick(small, me * n_dp + where)
    n_qkv = b_qkv.size
    g_b_qkv = pick(column_order(bias[None, :n_qkv], -1).reshape(n_dp, -1), where)
    g_b_in = pick(bias[n_qkv:].reshape(n_dp, -1), where)
    g_gain, g_bias = sums[None, 0:2], sums[None, 2:4]
    g_out_bias = jnp.stack([sums[4], sums[4]])[None]
    return (
        boundary,
        g_gain,
        g_bias,
        column_order(g_qkv, -1)[None],
        g_b_qkv[None],
        g_out[None],
        g_in[None],
        g_b_in[None],
        g_fc2[None],
        g_out_bias,
    )


def solution(mesh):
    placed = (
        P("pipe", "dp", "tensor", None),
        P("dp", None),
        P("pipe", None, None),
        P("pipe", None, None),
        P("pipe", None, "tensor"),
        P("pipe", "tensor"),
        P("pipe", "tensor", None),
        P("pipe", None, "tensor"),
        P("pipe", "tensor"),
        P("pipe", "tensor", None),
        P("pipe", None, None),
    )
    return jax.shard_map(
        body,
        mesh=mesh,
        in_specs=placed,
        out_specs=(
            P("pipe", "dp", "tensor", None),
            P("pipe", None, ("tensor", "dp")),
            P("pipe", None, ("tensor", "dp")),
            P("pipe", "dp", "tensor"),
            P("pipe", ("tensor", "dp")),
            P("pipe", ("tensor", "dp"), None),
            P("pipe", "dp", "tensor"),
            P("pipe", ("tensor", "dp")),
            P("pipe", ("tensor", "dp"), None),
            P("pipe", None, ("tensor", "dp")),
        ),
        check_vma=False,
    )
```

time: 787 us -> 547 us (0.70)
  starting transfers between devices: 180 us -> 66.4 us
  Pallas kernels: 335 us -> 247 us
  waiting for transfers between devices: 94.4 us -> 134 us
  other arithmetic: 90.5 us -> 54.1 us
  matrix products: 28 us -> 0 us
  local copies, waits for them, and re-layouts: 41.7 us -> 20.6 us
  between operations: 3.48 us -> 15.2 us
    ppermute x54 -> x4, starting transfers between devices: 137 us -> 29.4 us  [butterfly(): vec = vec + lax.ppermute(vec, axis, [(i, i ^ k) for i in range(n)])]
    pallas_call x2, Pallas kernels: 80.8 us -> 24.8 us  [attend(): pl.pallas_call(attend_kernel, grid=(1,), in_specs=[SMEM_SPEC, SMEM_SPEC]...]
    reduce_scatter x0 -> x2, waiting for transfers between devices: none -> 41.4 us  [dp_reduce(): lax.psum_scatter(blocks.reshape(n * rows, cols), 'dp', scatter_dimension=...]
    dot_general x8 -> x0, matrix products: 28 us -> none  [dot_tn(): return lax.dot_general(a, b, TN, preferred_element_type=F32)]
    pallas_call x32 -> x24, Pallas kernels: 193 us -> 172 us  [the longest x12 76 us: group_call(): pl.pallas_call(functools.partial(kernel, n_alias), grid=grid, in_specs=sp...]
    ppermute x54 -> x4, waiting for transfers between devices: 23.6 us -> 5.55 us  [butterfly(): vec = vec + lax.ppermute(vec, axis, [(i, i ^ k) for i in range(n)])]
    convert_element_type x35 -> x5, other arithmetic: 28.3 us -> 12.3 us  [the longest x4 12.1 us: over_chip(): return (pair[0].astype(F32) + swap(pair[1]).astype(F32)).astype(BF)]
    ppermute x21 -> x15, waiting for transfers between devices: 0.48 us -> 13.1 us  [swap(): return lax.ppermute(x, 'pipe', [(0, 1), (1, 0)])]
  transfers between devices with their start and end apart: 107 -> 55, of which waited for: 23 -> 29; matrix products, arithmetic and copies ran while one was open for 19% -> 12% of each run, Pallas kernels for 29% -> 28%
where the time goes in v2:
time: 547 us; the launch traced here: 537 us
  Pallas kernels  247 us (45%)
  waiting for transfers between devices  134 us (24%)
  starting transfers between devices  66.4 us (12%)
  other arithmetic  54.1 us (10%)
  local copies, waits for them, and re-layouts  20.6 us (4%)
  between operations  15.2 us (3%)
    pallas_call x12, Pallas kernels, group_call(): pl.pallas_call(functools.partial(kernel, n_alias), grid=grid, in_specs=sp...  76 us
    ppermute x32, waiting for transfers between devices, across(): return lax.ppermute(x, 'tensor', [(i, i ^ k) for i in range(n)])  73.3 us
    pallas_call x2, Pallas kernels, attend_back(): pl.pallas_call(attend_back_kernel, grid=(1,), in_specs=[SMEM_SPEC, SMEM_S...  50.2 us
    reduce_scatter x2, waiting for transfers between devices, dp_reduce(): lax.psum_scatter(blocks.reshape(n * rows, cols), 'dp', scatter_dimension=...  41.4 us
    pallas_call x4, Pallas kernels, bpost_group(): pl.pallas_call(functools.partial(bpost_kernel, len(xs), len(addends), ck)...  34.4 us
    ppermute x32, starting transfers between devices, across(): return lax.ppermute(x, 'tensor', [(i, i ^ k) for i in range(n)])  34.3 us
    ppermute x4, starting transfers between devices, butterfly(): vec = vec + lax.ppermute(vec, axis, [(i, i ^ k) for i in range(n)])  29.4 us
    pallas_call x2, Pallas kernels, wgrad_early(): pl.pallas_call(functools.partial(wgrad_kernel, True), grid=(steps,), in_s...  26.4 us
  transfers between devices with their start and end apart: 55, of which 29 were waited for; matrix products, arithmetic and copies ran while one was open for 12% of the time, Pallas kernels for 28%

profile of v2, /device:TPU:0, one launch (start us, length us, event | category | flops | bytes accessed | tf_op | source)
XLA Modules:
  0.0 537.3 jit_solution(16652432033519391580)
XLA Ops:
  23.0 2.8 collective-permute-done.8
  33.0 4.5 fusion.24
  37.5 3.9 broadcast_select_fusion.4
  41.4 3.9 broadcast_select_fusion.1
  45.3 6.5 %shard_map.204 = (bf16[4,384,1024]{2,1,0:T(8,128)(2,1)}, bf16[4,384,1024]{2,1,0:T(8,128)(2,1)}, bf16[4,384,256]{2,1,0:T(8,128)(2,1)}, bf16[4,384,256]{2,1,0:T(8,...) custom-call(bf16[384,1024]{1,0:T(8,128)(2,1)} %copy-done.1, ...), custom_call_target="tpu_custom_call" | custom-call | flops 1409286144 | bytes 7602176 | tf_op jit(solution)/shard_map/pallas_call | solution.py:121
  53.3 3.9 broadcast_select_fusion
  57.1 9.9 %shard_map.205 = (bf16[4,384,1024]{2,1,0:T(8,128)(2,1)}, bf16[4,384,1024]{2,1,0:T(8,128)(2,1)}, bf16[4,384,256]{2,1,0:T(8,128)(2,1)}, bf16[4,384,256]{2,1,0:T(8,...) custom-call(bf16[384,1024]{1,0:T(8,128)(2,1)} %copy-done.12, ...), custom_call_target="tpu_custom_call", output_to_operand_aliasing={{0}: (11, {}), {1}: (12, {}), {2}: (13, {}), {3}: (14, {}),... | custom-call | flops 2818572288 | bytes 11534336 | tf_op jit(solution)/shard_map/pallas_call | solution.py:121
  67.9 6.6 %shard_map.206 = (bf16[4,384,1024]{2,1,0:T(8,128)(2,1)}, bf16[4,384,1024]{2,1,0:T(8,128)(2,1)}, bf16[4,384,256]{2,1,0:T(8,128)(2,1)}, bf16[4,384,256]{2,1,0:T(8,...) custom-call(bf16[192,1024]{1,0:T(8,128)(2,1)} %copy-done.26, ...), custom_call_target="tpu_custom_call", output_to_operand_aliasing={{0}: (11, {}), {1}: (12, {}), {2}: (13, {}), {3}: (14, {}),... | custom-call | flops 1409286144 | bytes 7602176 | tf_op jit(solution)/shard_map/pallas_call | solution.py:121
  74.5 12.4 %shard_map.207 = (bf16[12,128,256]{2,1,0:T(8,128)(2,1)}, f32[6,8,256]{2,1,0:T(8,128)}) custom-call(s32[12]{0:T(128)} %fusion.37.order_ref, s32[6]{0:T(128)} %and_select_fusion.2.low_ref, bf16[12,128,256]{2,1,0:T(8,128)(2,1)} %bitcast.177, bf16[12,128,256]{2,1,0:T(8,128)(2,1)} %bitcast.179, bf16[12,128,256]{2,1,0:T(8,128)(2,1)} %bitcast.181, ...), custom_call_target="tpu_custom_call" | custom-call | flops 1811939328 | bytes 1966080 | tf_op jit(solution)/shard_map/pallas_call | solution.py:461
  86.9 5.3 shard_map.208
  95.0 7.3 %collective-permute-done.10.rest_0_ = bf16[192,1024]{1,0:T(8,128)(2,1)S(1)} collective-permute-done((bf16[192,1024]{1,0:T(8,128)(2,1)}, bf16[192,1024]{1,0:T(8,128)(2,1)S(1)}, u32[]{:S(2)}, u32[]{:S(2)}) %collective-permute-start.10) | collective-permute-done | bytes 393248 | tf_op jit(solution)/shard_map/ppermute | solution.py:574
  104.4 5.7 %shard_map.209 = (bf16[384,1024]{1,0:T(8,128)(2,1)}, bf16[384,1024]{1,0:T(8,128)(2,1)}) custom-call(bf16[4,384,256]{2,1,0:T(8,128)(2,1)} %bitcast.223, bf16[4,384,1024]{2,1,0:T(8,128)(2,1)} %get-tuple-element.237.g_ref, bf16[256,1024]{1,0:T(8,128)(2,1)} %get-tuple-element.442.wout_ref.refs_1_.refs_2_, ...), custom_call_target="tpu_custom_call" | custom-call | flops 2013265920 | bytes 6553600 | tf_op jit(solution)/shard_map/pallas_call | solution.py:202
  113.5 14.3 %collective-permute-done.12 = bf16[384,1024]{1,0:T(8,128)(2,1)S(1)} collective-permute-done((bf16[384,1024]{1,0:T(8,128)(2,1)}, bf16[384,1024]{1,0:T(8,128)(2,1)S(1)}, u32[]{:S(2)}, u32[]{:S(2)}) %collective-permute-start.12) | collective-permute-done | bytes 786464 | tf_op jit(solution)/shard_map/ppermute | solution.py:574
  131.8 6.2 %shard_map.210 = (bf16[4,384,1024]{2,1,0:T(8,128)(2,1)}, bf16[4,384,1024]{2,1,0:T(8,128)(2,1)}, bf16[4,384,256]{2,1,0:T(8,128)(2,1)}, bf16[4,384,256]{2,1,0:T(8,...) custom-call(bf16[384,1024]{1,0:T(8,128)(2,1)} %copy-done.4, ...), custom_call_target="tpu_custom_call" | custom-call | flops 1409286144 | bytes 7602176 | tf_op jit(solution)/shard_map/pallas_call | solution.py:121
  138.1 8.1 %collective-permute-done.14.refs_0_ = bf16[384,1024]{1,0:T(8,128)(2,1)S(1)} collective-permute-done((bf16[384,1024]{1,0:T(8,128)(2,1)S(1)}, bf16[384,1024]{1,0:T(8,128)(2,1)S(1)}, u32[]{:S(2)}, u32[]{:S(2)}) %collective-permute-start.14) | collective-permute-done | bytes 786464 | tf_op jit(solution)/shard_map/ppermute | solution.py:574
  151.1 10.3 %shard_map.211 = (bf16[4,384,1024]{2,1,0:T(8,128)(2,1)}, bf16[4,384,1024]{2,1,0:T(8,128)(2,1)}, bf16[4,384,256]{2,1,0:T(8,128)(2,1)}, bf16[4,384,256]{2,1,0:T(8,...) custom-call(bf16[384,1024]{1,0:T(8,128)(2,1)} %copy-done.14, ...), custom_call_target="tpu_custom_call", output_to_operand_aliasing={{0}: (11, {}), {1}: (12, {}), {2}: (13, {}), {3}: (14, {}),... | custom-call | flops 2818572288 | bytes 11534336 | tf_op jit(solution)/shard_map/pallas_call | solution.py:121
  162.6 6.3 %shard_map.212 = (bf16[4,384,1024]{2,1,0:T(8,128)(2,1)}, bf16[4,384,1024]{2,1,0:T(8,128)(2,1)}, bf16[4,384,256]{2,1,0:T(8,128)(2,1)}, bf16[4,384,256]{2,1,0:T(8,...) custom-call(bf16[192,1024]{1,0:T(8,128)(2,1)} %copy-done.28, ...), custom_call_target="tpu_custom_call", output_to_operand_aliasing={{0}: (11, {}), {1}: (12, {}), {2}: (13, {}), {3}: (14, {}),... | custom-call | flops 1409286144 | bytes 7602176 | tf_op jit(solution)/shard_map/pallas_call | solution.py:121
  168.9 4.4 shard_map.213
  173.3 5.1 collective-permute-done.18.refs_0_
  181.3 12.4 %shard_map.216 = (bf16[12,128,256]{2,1,0:T(8,128)(2,1)}, f32[6,8,256]{2,1,0:T(8,128)}) custom-call(s32[12]{0:T(128)} %fusion.37.order_ref, s32[6]{0:T(128)} %and_select_fusion.2.low_ref, bf16[12,128,256]{2,1,0:T(8,128)(2,1)} %bitcast.183, bf16[12,128,256]{2,1,0:T(8,128)(2,1)} %bitcast.185, bf16[12,128,256]{2,1,0:T(8,128)(2,1)} %bitcast.187, ...), custom_call_target="tpu_custom_call" | custom-call | flops 1811939328 | bytes 1966080 | tf_op jit(solution)/shard_map/pallas_call | solution.py:461
  193.8 6.3 %shard_map.214 = (bf16[4,384,1024]{2,1,0:T(8,128)(2,1)}, bf16[4,384,256]{2,1,0:T(8,128)(2,1)}, bf16[4,384,1024]{2,1,0:T(8,128)(2,1)}, f32[4,1,1024]{2,1,0:T(1,128)}) custom-call(bf16[384,1024]{1,0:T(8,128)(2,1)} %copy-done.21, bf16[384,1024]{1,0:T(8,128)(2,1)} %copy-done.22, ...), custom_call_target="tpu_custom_call", output_to_operand_aliasing={{0}: (5, {}), {1}: (6, {}), {2}: (7, {}), {3}: (8, {})} | custom-call | flops 2013265920 | bytes 8912896 | tf_op jit(solution)/shard_map/pallas_call | solution.py:121
  200.9 4.4 shard_map.215
  205.4 25.1 %shard_map.217 = (bf16[12,128,768]{2,1,0:T(8,128)(2,1)}, f32[1,768]{1,0:T(1,128)}) custom-call(s32[12]{0:T(128)} %fusion.37.order_ref, s32[6]{0:T(128)} %and_select_fusion.2.low_ref, bf16[12,128,256]{2,1,0:T(8,128)(2,1)} %bitcast.184, bf16[12,128,256]{2,1,0:T(8,128)(2,1)} %bitcast.186, bf16[12,128,256]{2,1,0:T(8,128)(2,1)} %bitcast.188, ...), custom_call_target="tpu_custom_call" | custom-call | flops 4831838208 | bytes 6291456 | tf_op jit(solution)/shard_map/pallas_call | solution.py:558
  230.5 8.5 %shard_map.218 = (f32[384,1024]{1,0:T(8,128)}, bf16[192,1024]{1,0:T(8,128)(2,1)}, bf16[192,1024]{1,0:T(8,128)(2,1)}, f32[4,1024]{1,0:T(4,128)}) custom-call(bf16[384,1024]{1,0:T(8,128)(2,1)} %copy-done.4, bf16[192,1024]{1,0:T(8,128)(2,1)} %copy-done.28, bf16[192,1024]{1,0:T(8,128)(2,1)} %copy-done.29, ...), custom_call_target="tpu_custom_call" | custom-call | flops 2818572288 | bytes 9175040 | tf_op jit(solution)/shard_map/pallas_call | solution.py:291
  241.6 6.6 %shard_map.220 = (bf16[4,128,768]{2,1,0:T(8,128)(2,1)}, bf16[4,128,768]{2,1,0:T(8,128)(2,1)}) custom-call(s32[1]{0:T(128)} %bitcast.38.core_ref, bf16[1536,1024]{1,0:T(8,128)(2,1)} %bitcast.162, bf16[1536,768]{1,0:T(8,128)(2,1)} %bitcast.173), custom_call_target="tpu_custom_call" | custom-call | flops 2415919104 | bytes 7864320 | tf_op jit(solution)/shard_map/pallas_call | solution.py:377
  249.1 8.6 %shard_map.221 = (bf16[384,1024]{1,0:T(8,128)(2,1)}, bf16[384,1024]{1,0:T(8,128)(2,1)}, f32[4,1024]{1,0:T(4,128)}) custom-call(bf16[384,1024]{1,0:T(8,128)(2,1)} %copy-done.14, bf16[384,1024]{1,0:T(8,128)(2,1)} %copy-done.15, bf16[2,1024]{1,0:T(2,128)(2,1)} %get-tuple-element.472.refs_1_.refs_2_.refs_3_, bf16[4,384,768]{2,1,0:T(8,128)(2,1)} %bitcast.174, ...), custom_call_target="tpu_custom_call" | custom-call | flops 2818572288 | bytes 9175040 | tf_op jit(solution)/shard_map/pallas_call | solution.py:291
  260.3 13.3 %shard_map.219 = (bf16[4,128,2304]{2,1,0:T(8,128)(2,1)}, bf16[4,128,2304]{2,1,0:T(8,128)(2,1)}) custom-call(s32[1]{0:T(128)} %bitcast.38.core_ref, bf16[1536,256]{1,0:T(8,128)(2,1)} %bitcast.225, bf16[1536,1024]{1,0:T(8,128)(2,1)} %bitcast.165, bf16[1536,1024]{1,0:T(8,128)(2,1)} %bitcast.163, bf16[1536,1024]{1,0:T(8,128)(2,1)} %bitcast.151, ...), custom_call_target="tpu_custom_call" | custom-call | flops 7247757312 | bytes 17301504 | tf_op jit(solution)/shard_map/pallas_call | solution.py:361
  280.5 4.4 shard_map.222
  284.9 10.9 %collective-permute-done.26.refs_0_ = bf16[384,1024]{1,0:T(8,128)(2,1)S(1)} collective-permute-done((bf16[384,1024]{1,0:T(8,128)(2,1)S(1)}, bf16[384,1024]{1,0:T(8,128)(2,1)S(1)}, u32[]{:S(2)}, u32[]{:S(2)}) %collective-permute-start.26) | collective-permute-done | bytes 786464 | tf_op jit(solution)/shard_map/ppermute | solution.py:574
  296.9 6.3 %shard_map.223 = (bf16[4,384,1024]{2,1,0:T(8,128)(2,1)}, bf16[4,384,256]{2,1,0:T(8,128)(2,1)}, bf16[4,384,1024]{2,1,0:T(8,128)(2,1)}, f32[4,1,1024]{2,1,0:T(1,128)}) custom-call(bf16[384,1024]{1,0:T(8,128)(2,1)} %copy-done.23, bf16[384,1024]{1,0:T(8,128)(2,1)} %copy-done.24, ...), custom_call_target="tpu_custom_call", output_to_operand_aliasing={{0}: (5, {}), {1}: (6, {}), {2}: (7, {}), {3}: (8, {})} | custom-call | flops 2013265920 | bytes 8912896 | tf_op jit(solution)/shard_map/pallas_call | solution.py:121
  305.4 4.4 shard_map.224
  309.8 13.1 %shard_map.225 = (bf16[4,128,2304]{2,1,0:T(8,128)(2,1)}, bf16[4,128,2304]{2,1,0:T(8,128)(2,1)}) custom-call(s32[1]{0:T(128)} %bitcast.38.core_ref, bf16[1536,256]{1,0:T(8,128)(2,1)} %bitcast.224, bf16[1536,1024]{1,0:T(8,128)(2,1)} %bitcast.166, bf16[1536,1024]{1,0:T(8,128)(2,1)} %bitcast.160, bf16[1536,1024]{1,0:T(8,128)(2,1)} %bitcast.152, ...), custom_call_target="tpu_custom_call" | custom-call | flops 7247757312 | bytes 17301504 | tf_op jit(solution)/shard_map/pallas_call | solution.py:361
  323.5 5.8 %collective-permute-done.47 = bf16[4,128,768]{2,1,0:T(8,128)(2,1)S(1)} collective-permute-done((bf16[4,128,768]{2,1,0:T(8,128)(2,1)S(1)}, bf16[4,128,768]{2,1,0:T(8,128)(2,1)S(1)}, u32[]{:S(2)}, u32[]{:S(2)}) %collective-permute-start.47) | collective-permute-done | bytes 786464 | tf_op jit(solution)/shard_map/ppermute | solution.py:578
  330.6 4.4 add_convert_fusion.1
  334.9 25.1 %shard_map.226 = (bf16[12,128,768]{2,1,0:T(8,128)(2,1)}, f32[1,768]{1,0:T(1,128)}) custom-call(s32[12]{0:T(128)} %fusion.37.order_ref, s32[6]{0:T(128)} %and_select_fusion.2.low_ref, bf16[12,128,256]{2,1,0:T(8,128)(2,1)} %bitcast.178, bf16[12,128,256]{2,1,0:T(8,128)(2,1)} %bitcast.180, bf16[12,128,256]{2,1,0:T(8,128)(2,1)} %bitcast.182, ...), custom_call_target="tpu_custom_call" | custom-call | flops 4831838208 | bytes 6291456 | tf_op jit(solution)/shard_map/pallas_call | solution.py:558
  360.1 8.4 %shard_map.227 = (f32[384,1024]{1,0:T(8,128)}, bf16[192,1024]{1,0:T(8,128)(2,1)}, bf16[192,1024]{1,0:T(8,128)(2,1)}, f32[4,1024]{1,0:T(4,128)}) custom-call(bf16[384,1024]{1,0:T(8,128)(2,1)} %copy-done.1, bf16[192,1024]{1,0:T(8,128)(2,1)} %copy-done.26, bf16[192,1024]{1,0:T(8,128)(2,1)} %copy-done.27, ...), custom_call_target="tpu_custom_call" | custom-call | flops 2818572288 | bytes 9175040 | tf_op jit(solution)/shard_map/pallas_call | solution.py:291
  370.4 6.5 %shard_map.228 = (bf16[4,128,768]{2,1,0:T(8,128)(2,1)}, bf16[4,128,768]{2,1,0:T(8,128)(2,1)}) custom-call(s32[1]{0:T(128)} %bitcast.38.core_ref, bf16[1536,1024]{1,0:T(8,128)(2,1)} %bitcast.159, bf16[1536,768]{1,0:T(8,128)(2,1)} %bitcast.170), custom_call_target="tpu_custom_call" | custom-call | flops 2415919104 | bytes 7864320 | tf_op jit(solution)/shard_map/pallas_call | solution.py:377
  376.9 3.2 collective-permute-done.31.refs_8_
  385.4 4.4 add_convert_fusion
  390.4 5.6 %shard_map.230 = (f32[384,1024]{1,0:T(8,128)}, bf16[192,1024]{1,0:T(8,128)(2,1)}, bf16[192,1024]{1,0:T(8,128)(2,1)}) custom-call(bf16[4,384,256]{2,1,0:T(8,128)(2,1)} %bitcast.226, bf16[4,384,1024]{2,1,0:T(8,128)(2,1)} %get-tuple-element.308.g_ref, bf16[256,1024]{1,0:T(8,128)(2,1)} %get-tuple-element.441.refs_1_.refs_2_.wout_ref, ...), custom_call_target="tpu_custom_call" | custom-call | flops 2013265920 | bytes 6553600 | tf_op jit(solution)/shard_map/pallas_call | solution.py:202
  398.5 8.8 %collective-permute-done.35.rest_0_ = bf16[192,1024]{1,0:T(8,128)(2,1)S(1)} collective-permute-done((bf16[192,1024]{1,0:T(8,128)(2,1)}, bf16[192,1024]{1,0:T(8,128)(2,1)S(1)}, u32[]{:S(2)}, u32[]{:S(2)}) %collective-permute-start.35) | collective-permute-done | bytes 393248 | tf_op jit(solution)/shard_map/ppermute | solution.py:574
  409.0 5.6 %shard_map.231 = (bf16[384,1024]{1,0:T(8,128)(2,1)}, bf16[384,1024]{1,0:T(8,128)(2,1)}) custom-call(bf16[4,384,256]{2,1,0:T(8,128)(2,1)} %bitcast.227, bf16[4,384,1024]{2,1,0:T(8,128)(2,1)} %get-tuple-element.308.g_ref, bf16[256,1024]{1,0:T(8,128)(2,1)} %get-tuple-element.441.refs_1_.refs_2_.wout_ref, ...), custom_call_target="tpu_custom_call" | custom-call | flops 2013265920 | bytes 6553600 | tf_op jit(solution)/shard_map/pallas_call | solution.py:202
  417.1 8.8 %shard_map.229 = (bf16[384,1024]{1,0:T(8,128)(2,1)}, bf16[384,1024]{1,0:T(8,128)(2,1)}, f32[4,1024]{1,0:T(4,128)}) custom-call(bf16[384,1024]{1,0:T(8,128)(2,1)} %copy-done.12, bf16[384,1024]{1,0:T(8,128)(2,1)} %copy-done.13, bf16[2,1024]{1,0:T(2,128)(2,1)} %get-tuple-element.471.refs_1_.refs_2_.refs_3_, bf16[4,384,768]{2,1,0:T(8,128)(2,1)} %bitcast.171, ...), custom_call_target="tpu_custom_call" | custom-call | flops 2818572288 | bytes 9175040 | tf_op jit(solution)/shard_map/pallas_call | solution.py:291
  430.1 17.5 %collective-permute-start.42 = (f32[6912]{0:T(1024)S(1)}, f32[6912]{0:T(1024)S(1)}, u32[]{:S(2)}, u32[]{:S(2)}) collective-permute-start(f32[6912]{0:T(1024)S(1)} %pad_maximum_fusion.3), channel_id=1, source_target_pairs={{0,1},{1,0},{2,3},{3,2},{4,5},{5,4},{6,7},{7,6},{8,9},{9,8},{10,11... | collective-permute-start | bytes 82952 | tf_op jit(solution)/shard_map/ppermute | solution.py:607
  447.7 2.7 collective-permute-done.33
  453.6 4.9 broadcast_select_fusion.6
  458.6 8.9 %collective-permute-start.43 = (f32[6912]{0:T(1024)S(1)}, f32[6912]{0:T(1024)S(1)}, u32[]{:S(2)}, u32[]{:S(2)}) collective-permute-start(f32[6912]{0:T(1024)S(1)} %fusion.46), channel_id=1, source_target_pairs={{0,2},{1,3},{2,0},{3,1},{4,6},{5,7},{6,4},{7,5},{8,10},{9,11},{10,... | collective-permute-start | bytes 82952 | tf_op jit(solution)/shard_map/ppermute | solution.py:607
  482.4 41.4 %reduce-scatter.9.cloned.1.call-done = bf16[128,2304]{1,0:T(8,128)(2,1)} async-done(((bf16[512,2304]{1,0:T(8,128)(2,1)}), bf16[128,2304]{1,0:T(8,128)(2,1)}) %reduce-scatter.9.cloned.1.call-update) | async-done | bytes 589840 | tf_op jit(solution)/shard_map/reduce_scatter | solution.py:600
  (357 shorter events, 108.4 us)
Async XLA Ops:
  7.2 460.3 %reduce-scatter.15.cloned.1.call-start = ((), (), s32[]{:S(2)}) async-start(), calls=%async_computation.7 | async-start | bytes 983040
  7.2 19.6 %collective-permute-start = (bf16[2,384,1024]{2,1,0:T(8,128)(2,1)}, bf16[2,384,1024]{2,1,0:T(8,128)(2,1)}, u32[]{:S(2)}, u32[]{:S(2)}) collective-permute-start(bf16[2,384,1024]{2,1,0:T(8,128)(2,1)} %bitcast.196), channel_id=1, source_target_pairs={{0,16},{16,0},{1,17},{17,1},{2,18},{18,2},{3,19},{19,3},{4,20},{20... | collective-permute-start | bytes 4718600 | tf_op jit(solution)/shard_map/ppermute | solution.py:578
  12.0 9.0 %collective-permute-start.3 = (bf16[62,128]{1,0:T(8,128)(2,1)S(1)}, bf16[62,128]{1,0:T(8,128)(2,1)S(1)}, u32[]{:S(2)}, u32[]{:S(2)}) collective-permute-start(bf16[62,128]{1,0:T(8,128)(2,1)S(1)} %bitcast.221), channel_id=1, source_target_pairs={{0,16},{16,0},{1,17},{17,1},{2,18},{18,2},{3,19},{19,3},{4,20},{20... | collective-permute-start | bytes 47624 | tf_op jit(solution)/shard_map/ppermute | solution.py:578
  15.6 21.9 %collective-permute-start.4 = (bf16[1024,768]{1,0:T(8,128)(2,1)}, bf16[1024,768]{1,0:T(8,128)(2,1)}, u32[]{:S(2)}, u32[]{:S(2)}) collective-permute-start(bf16[1024,768]{1,0:T(8,128)(2,1)} %copy.114), channel_id=1, source_target_pairs={{0,16},{16,0},{1,17},{17,1},{2,18},{18,2},{3,19},{19,3},{4,20},{20... | collective-permute-start | bytes 4718600 | tf_op jit(solution)/shard_map/ppermute | solution.py:578
  16.1 25.3 %collective-permute-start.5 = (bf16[1024,1024]{1,0:T(8,128)(2,1)}, bf16[1024,1024]{1,0:T(8,128)(2,1)}, u32[]{:S(2)}, u32[]{:S(2)}) collective-permute-start(bf16[1024,1024]{1,0:T(8,128)(2,1)} %bitcast.194), channel_id=1, source_target_pairs={{0,16},{16,0},{1,17},{17,1},{2,18},{18,2},{3,19},{19,3},{4,20},{20... | collective-permute-start | bytes 6291464 | tf_op jit(solution)/shard_map/ppermute | solution.py:578
  16.1 37.2 %collective-permute-start.9 = (bf16[1024,1024]{1,0:T(8,128)(2,1)}, bf16[1024,1024]{1,0:T(8,128)(2,1)}, u32[]{:S(2)}, u32[]{:S(2)}) collective-permute-start(bf16[1024,1024]{1,0:T(8,128)(2,1)} %bitcast.195), channel_id=1, source_target_pairs={{0,16},{16,0},{1,17},{17,1},{2,18},{18,2},{3,19},{19,3},{4,20},{20... | collective-permute-start | bytes 6291464 | tf_op jit(solution)/shard_map/ppermute | solution.py:578
  28.8 22.9 %collective-permute-start.1 = (bf16[384,1024]{1,0:T(8,128)(2,1)S(1)}, bf16[384,1024]{1,0:T(8,128)(2,1)S(1)}, u32[]{:S(2)}, u32[]{:S(2)}) collective-permute-start(bf16[384,1024]{1,0:T(8,128)(2,1)S(1)} %get-tuple-element.196.refs_0_), channel_id=1, source_target_pairs={{0,4},{4,0},{8,12},{12,8},{1,5},{5,1},{9,13},{13,9},{2,6},{6,2},{1... | collective-permute-start | bytes 2359304 | tf_op jit(solution)/shard_map/ppermute | solution.py:574
  31.5 20.3 %collective-permute-start.2 = (bf16[384,1024]{1,0:T(8,128)(2,1)S(1)}, bf16[384,1024]{1,0:T(8,128)(2,1)S(1)}, u32[]{:S(2)}, u32[]{:S(2)}) collective-permute-start(bf16[384,1024]{1,0:T(8,128)(2,1)S(1)} %get-tuple-element.196.refs_0_), channel_id=1, source_target_pairs={{0,8},{4,12},{8,0},{12,4},{1,9},{5,13},{9,1},{13,5},{2,10},{6,14},... | collective-permute-start | bytes 2359304 | tf_op jit(solution)/shard_map/ppermute | solution.py:574
  51.9 15.2 %collective-permute-start.6 = (bf16[192,1024]{1,0:T(8,128)(2,1)S(1)}, bf16[192,1024]{1,0:T(8,128)(2,1)S(1)}, u32[]{:S(2)}, u32[]{:S(2)}) collective-permute-start(bf16[192,1024]{1,0:T(8,128)(2,1)S(1)} %slice.162), channel_id=1, source_target_pairs={{0,8},{4,12},{8,0},{12,4},{1,9},{5,13},{9,1},{13,5},{2,10},{6,14},... | collective-permute-start | bytes 1179656 | tf_op jit(solution)/shard_map/ppermute | solution.py:574
  52.7 14.3 %collective-permute-start.7 = (bf16[192,1024]{1,0:T(8,128)(2,1)S(1)}, bf16[192,1024]{1,0:T(8,128)(2,1)S(1)}, u32[]{:S(2)}, u32[]{:S(2)}) collective-permute-start(bf16[192,1024]{1,0:T(8,128)(2,1)S(1)} %slice.163), channel_id=1, source_target_pairs={{0,4},{4,0},{8,12},{12,8},{1,5},{5,1},{9,13},{13,9},{2,6},{6,2},{1... | collective-permute-start | bytes 1179656 | tf_op jit(solution)/shard_map/ppermute | solution.py:574
  92.2 10.1 %collective-permute-start.10 = (bf16[192,1024]{1,0:T(8,128)(2,1)}, bf16[192,1024]{1,0:T(8,128)(2,1)S(1)}, u32[]{:S(2)}, u32[]{:S(2)}) collective-permute-start(bf16[192,1024]{1,0:T(8,128)(2,1)} %get-tuple-element.239), channel_id=1, source_target_pairs={{0,8},{4,12},{8,0},{12,4},{1,9},{5,13},{9,1},{13,5},{2,10},{6,14},... | collective-permute-start | bytes 1179656 | tf_op jit(solution)/shard_map/ppermute | solution.py:574
  93.5 10.2 %collective-permute-start.11 = (bf16[192,1024]{1,0:T(8,128)(2,1)}, bf16[192,1024]{1,0:T(8,128)(2,1)S(1)}, u32[]{:S(2)}, u32[]{:S(2)}) collective-permute-start(bf16[192,1024]{1,0:T(8,128)(2,1)} %get-tuple-element.240), channel_id=1, source_target_pairs={{0,4},{4,0},{8,12},{12,8},{1,5},{5,1},{9,13},{13,9},{2,6},{6,2},{1... | collective-permute-start | bytes 1179656 | tf_op jit(solution)/shard_map/ppermute | solution.py:574
  110.1 17.7 %collective-permute-start.12 = (bf16[384,1024]{1,0:T(8,128)(2,1)}, bf16[384,1024]{1,0:T(8,128)(2,1)S(1)}, u32[]{:S(2)}, u32[]{:S(2)}) collective-permute-start(bf16[384,1024]{1,0:T(8,128)(2,1)} %get-tuple-element.241), channel_id=1, source_target_pairs={{0,4},{4,0},{8,12},{12,8},{1,5},{5,1},{9,13},{13,9},{2,6},{6,2},{1... | collective-permute-start | bytes 2359304 | tf_op jit(solution)/shard_map/ppermute | solution.py:574
  111.6 17.4 %collective-permute-start.13 = (bf16[384,1024]{1,0:T(8,128)(2,1)}, bf16[384,1024]{1,0:T(8,128)(2,1)S(1)}, u32[]{:S(2)}, u32[]{:S(2)}) collective-permute-start(bf16[384,1024]{1,0:T(8,128)(2,1)} %get-tuple-element.242), channel_id=1, source_target_pairs={{0,8},{4,12},{8,0},{12,4},{1,9},{5,13},{9,1},{13,5},{2,10},{6,14},... | collective-permute-start | bytes 2359304 | tf_op jit(solution)/shard_map/ppermute | solution.py:574
  129.9 16.3 %collective-permute-start.14 = (bf16[384,1024]{1,0:T(8,128)(2,1)S(1)}, bf16[384,1024]{1,0:T(8,128)(2,1)S(1)}, u32[]{:S(2)}, u32[]{:S(2)}) collective-permute-start(bf16[384,1024]{1,0:T(8,128)(2,1)S(1)} %get-tuple-element.422.refs_0_), channel_id=1, source_target_pairs={{0,4},{4,0},{8,12},{12,8},{1,5},{5,1},{9,13},{13,9},{2,6},{6,2},{1... | collective-permute-start | bytes 2359304 | tf_op jit(solution)/shard_map/ppermute | solution.py:574
  130.5 17.5 %collective-permute-start.15 = (bf16[384,1024]{1,0:T(8,128)(2,1)S(1)}, bf16[384,1024]{1,0:T(8,128)(2,1)S(1)}, u32[]{:S(2)}, u32[]{:S(2)}) collective-permute-start(bf16[384,1024]{1,0:T(8,128)(2,1)S(1)} %get-tuple-element.422.refs_0_), channel_id=1, source_target_pairs={{0,8},{4,12},{8,0},{12,4},{1,9},{5,13},{9,1},{13,5},{2,10},{6,14},... | collective-permute-start | bytes 2359304 | tf_op jit(solution)/shard_map/ppermute | solution.py:574
  148.0 13.4 %collective-permute-start.16 = (bf16[192,1024]{1,0:T(8,128)(2,1)S(1)}, bf16[192,1024]{1,0:T(8,128)(2,1)S(1)}, u32[]{:S(2)}, u32[]{:S(2)}) collective-permute-start(bf16[192,1024]{1,0:T(8,128)(2,1)S(1)} %slice.167), channel_id=1, source_target_pairs={{0,8},{4,12},{8,0},{12,4},{1,9},{5,13},{9,1},{13,5},{2,10},{6,14},... | collective-permute-start | bytes 1179656 | tf_op jit(solution)/shard_map/ppermute | solution.py:574
  149.5 11.8 %collective-permute-start.17 = (bf16[192,1024]{1,0:T(8,128)(2,1)S(1)}, bf16[192,1024]{1,0:T(8,128)(2,1)S(1)}, u32[]{:S(2)}, u32[]{:S(2)}) collective-permute-start(bf16[192,1024]{1,0:T(8,128)(2,1)S(1)} %slice.168), channel_id=1, source_target_pairs={{0,4},{4,0},{8,12},{12,8},{1,5},{5,1},{9,13},{13,9},{2,6},{6,2},{1... | collective-permute-start | bytes 1179656 | tf_op jit(solution)/shard_map/ppermute | solution.py:574
  161.4 17.0 %collective-permute-start.18 = (bf16[384,1024]{1,0:T(8,128)(2,1)S(1)}, bf16[384,1024]{1,0:T(8,128)(2,1)S(1)}, u32[]{:S(2)}, u32[]{:S(2)}) collective-permute-start(bf16[384,1024]{1,0:T(8,128)(2,1)S(1)} %get-tuple-element.266.refs_0_), channel_id=1, source_target_pairs={{0,4},{4,0},{8,12},{12,8},{1,5},{5,1},{9,13},{13,9},{2,6},{6,2},{1... | collective-permute-start | bytes 2359304 | tf_op jit(solution)/shard_map/ppermute | solution.py:574
  162.0 17.4 %collective-permute-start.19 = (bf16[384,1024]{1,0:T(8,128)(2,1)S(1)}, bf16[384,1024]{1,0:T(8,128)(2,1)S(1)}, u32[]{:S(2)}, u32[]{:S(2)}) collective-permute-start(bf16[384,1024]{1,0:T(8,128)(2,1)S(1)} %get-tuple-element.266.refs_0_), channel_id=1, source_target_pairs={{0,8},{4,12},{8,0},{12,4},{1,9},{5,13},{9,1},{13,5},{2,10},{6,14},... | collective-permute-start | bytes 2359304 | tf_op jit(solution)/shard_map/ppermute | solution.py:574
  179.4 20.6 %collective-permute-start.20 = (bf16[192,1024]{1,0:T(8,128)(2,1)S(1)}, bf16[192,1024]{1,0:T(8,128)(2,1)S(1)}, u32[]{:S(2)}, u32[]{:S(2)}) collective-permute-start(bf16[192,1024]{1,0:T(8,128)(2,1)S(1)} %slice.171), channel_id=1, source_target_pairs={{0,8},{4,12},{8,0},{12,4},{1,9},{5,13},{9,1},{13,5},{2,10},{6,14},... | collective-permute-start | bytes 1179656 | tf_op jit(solution)/shard_map/ppermute | solution.py:574
  180.2 19.8 %collective-permute-start.21 = (bf16[192,1024]{1,0:T(8,128)(2,1)S(1)}, bf16[192,1024]{1,0:T(8,128)(2,1)S(1)}, u32[]{:S(2)}, u32[]{:S(2)}) collective-permute-start(bf16[192,1024]{1,0:T(8,128)(2,1)S(1)} %slice.172), channel_id=1, source_target_pairs={{0,4},{4,0},{8,12},{12,8},{1,5},{5,1},{9,13},{13,9},{2,6},{6,2},{1... | collective-permute-start | bytes 1179656 | tf_op jit(solution)/shard_map/ppermute | solution.py:574
  239.0 9.2 %collective-permute-start.22 = (bf16[192,1024]{1,0:T(8,128)(2,1)}, bf16[192,1024]{1,0:T(8,128)(2,1)S(1)}, u32[]{:S(2)}, u32[]{:S(2)}) collective-permute-start(bf16[192,1024]{1,0:T(8,128)(2,1)} %get-tuple-element.314), channel_id=1, source_target_pairs={{0,4},{4,0},{8,12},{12,8},{1,5},{5,1},{9,13},{13,9},{2,6},{6,2},{1... | collective-permute-start | bytes 1179656 | tf_op jit(solution)/shard_map/ppermute | solution.py:574
  239.9 8.3 %collective-permute-start.23 = (bf16[192,1024]{1,0:T(8,128)(2,1)}, bf16[192,1024]{1,0:T(8,128)(2,1)S(1)}, u32[]{:S(2)}, u32[]{:S(2)}) collective-permute-start(bf16[192,1024]{1,0:T(8,128)(2,1)} %get-tuple-element.315), channel_id=1, source_target_pairs={{0,8},{4,12},{8,0},{12,4},{1,9},{5,13},{9,1},{13,5},{2,10},{6,14},... | collective-permute-start | bytes 1179656 | tf_op jit(solution)/shard_map/ppermute | solution.py:574
  257.7 17.6 %collective-permute-start.24 = (bf16[384,1024]{1,0:T(8,128)(2,1)}, bf16[384,1024]{1,0:T(8,128)(2,1)S(1)}, u32[]{:S(2)}, u32[]{:S(2)}) collective-permute-start(bf16[384,1024]{1,0:T(8,128)(2,1)} %get-tuple-element.318), channel_id=1, source_target_pairs={{0,4},{4,0},{8,12},{12,8},{1,5},{5,1},{9,13},{13,9},{2,6},{6,2},{1... | collective-permute-start | bytes 2359304 | tf_op jit(solution)/shard_map/ppermute | solution.py:574
  259.2 18.3 %collective-permute-start.25 = (bf16[384,1024]{1,0:T(8,128)(2,1)}, bf16[384,1024]{1,0:T(8,128)(2,1)S(1)}, u32[]{:S(2)}, u32[]{:S(2)}) collective-permute-start(bf16[384,1024]{1,0:T(8,128)(2,1)} %get-tuple-element.319), channel_id=1, source_target_pairs={{0,8},{4,12},{8,0},{12,4},{1,9},{5,13},{9,1},{13,5},{2,10},{6,14},... | collective-permute-start | bytes 2359304 | tf_op jit(solution)/shard_map/ppermute | solution.py:574
  279.5 16.3 %collective-permute-start.26 = (bf16[384,1024]{1,0:T(8,128)(2,1)S(1)}, bf16[384,1024]{1,0:T(8,128)(2,1)S(1)}, u32[]{:S(2)}, u32[]{:S(2)}) collective-permute-start(bf16[384,1024]{1,0:T(8,128)(2,1)S(1)} %get-tuple-element.417.refs_0_), channel_id=1, source_target_pairs={{0,4},{4,0},{8,12},{12,8},{1,5},{5,1},{9,13},{13,9},{2,6},{6,2},{1... | collective-permute-start | bytes 2359304 | tf_op jit(solution)/shard_map/ppermute | solution.py:574
  279.8 16.0 %collective-permute-start.27 = (bf16[384,1024]{1,0:T(8,128)(2,1)S(1)}, bf16[384,1024]{1,0:T(8,128)(2,1)S(1)}, u32[]{:S(2)}, u32[]{:S(2)}) collective-permute-start(bf16[384,1024]{1,0:T(8,128)(2,1)S(1)} %get-tuple-element.417.refs_0_), channel_id=1, source_target_pairs={{0,8},{4,12},{8,0},{12,4},{1,9},{5,13},{9,1},{13,5},{2,10},{6,14},... | collective-permute-start | bytes 2359304 | tf_op jit(solution)/shard_map/ppermute | solution.py:574
  295.8 7.8 %collective-permute-start.28 = (bf16[192,1024]{1,0:T(8,128)(2,1)S(1)}, bf16[192,1024]{1,0:T(8,128)(2,1)S(1)}, u32[]{:S(2)}, u32[]{:S(2)}) collective-permute-start(bf16[192,1024]{1,0:T(8,128)(2,1)S(1)} %slice.173), channel_id=1, source_target_pairs={{0,8},{4,12},{8,0},{12,4},{1,9},{5,13},{9,1},{13,5},{2,10},{6,14},... | collective-permute-start | bytes 1179656 | tf_op jit(solution)/shard_map/ppermute | solution.py:574
  296.8 7.8 %collective-permute-start.29 = (bf16[192,1024]{1,0:T(8,128)(2,1)S(1)}, bf16[192,1024]{1,0:T(8,128)(2,1)S(1)}, u32[]{:S(2)}, u32[]{:S(2)}) collective-permute-start(bf16[192,1024]{1,0:T(8,128)(2,1)S(1)} %slice.174), channel_id=1, source_target_pairs={{0,4},{4,0},{8,12},{12,8},{1,5},{5,1},{9,13},{13,9},{2,6},{6,2},{1... | collective-permute-start | bytes 1179656 | tf_op jit(solution)/shard_map/ppermute | solution.py:574
  322.9 7.6 %collective-permute-start.30 = (bf16[4,128,2304]{2,1,0:T(8,128)(2,1)}, bf16[4,128,2304]{2,1,0:T(8,128)(2,1)}, u32[]{:S(2)}, u32[]{:S(2)}) collective-permute-start(bf16[4,128,2304]{2,1,0:T(8,128)(2,1)} %get-tuple-element.347), channel_id=1, source_target_pairs={{0,16},{16,0},{1,17},{17,1},{2,18},{18,2},{3,19},{19,3},{4,20},{20... | collective-permute-start | bytes 7077896 | tf_op jit(solution)/shard_map/ppermute | solution.py:578
  322.9 6.4 %collective-permute-start.47 = (bf16[4,128,768]{2,1,0:T(8,128)(2,1)S(1)}, bf16[4,128,768]{2,1,0:T(8,128)(2,1)S(1)}, u32[]{:S(2)}, u32[]{:S(2)}) collective-permute-start(bf16[4,128,768]{2,1,0:T(8,128)(2,1)S(1)} %copy-done.55), channel_id=1, source_target_pairs={{0,16},{16,0},{1,17},{17,1},{2,18},{18,2},{3,19},{19,3},{4,20},{20... | collective-permute-start | bytes 2359304 | tf_op jit(solution)/shard_map/ppermute | solution.py:578
  323.4 61.9 %collective-permute-start.49 = (bf16[4,128,2304]{2,1,0:T(8,128)(2,1)}, bf16[4,128,2304]{2,1,0:T(8,128)(2,1)}, u32[]{:S(2)}, u32[]{:S(2)}) collective-permute-start(bf16[4,128,2304]{2,1,0:T(8,128)(2,1)} %get-tuple-element.381), channel_id=1, source_target_pairs={{0,16},{16,0},{1,17},{17,1},{2,18},{18,2},{3,19},{19,3},{4,20},{20... | collective-permute-start | bytes 7077896 | tf_op jit(solution)/shard_map/ppermute | solution.py:578
  330.5 150.6 %reduce-scatter.13.cloned.1.call-start = ((), (), s32[]{:S(2)}) async-start(), calls=%async_computation.6 | async-start | bytes 983040
  368.5 11.6 %collective-permute-start.31 = (bf16[192,1024]{1,0:T(8,128)(2,1)}, bf16[192,1024]{1,0:T(8,128)(2,1)S(1)}, u32[]{:S(2)}, u32[]{:S(2)}) collective-permute-start(bf16[192,1024]{1,0:T(8,128)(2,1)} %get-tuple-element.356), channel_id=1, source_target_pairs={{0,4},{4,0},{8,12},{12,8},{1,5},{5,1},{9,13},{13,9},{2,6},{6,2},{1... | collective-permute-start | bytes 1179656 | tf_op jit(solution)/shard_map/ppermute | solution.py:574
  369.3 11.3 %collective-permute-start.32 = (bf16[192,1024]{1,0:T(8,128)(2,1)}, bf16[192,1024]{1,0:T(8,128)(2,1)S(1)}, u32[]{:S(2)}, u32[]{:S(2)}) collective-permute-start(bf16[192,1024]{1,0:T(8,128)(2,1)} %get-tuple-element.357), channel_id=1, source_target_pairs={{0,8},{4,12},{8,0},{12,4},{1,9},{5,13},{9,1},{13,5},{2,10},{6,14},... | collective-permute-start | bytes 1179656 | tf_op jit(solution)/shard_map/ppermute | solution.py:574
  385.3 97.1 %reduce-scatter.11.cloned.1.call-start = ((), (), s32[]{:S(2)}) async-start(), calls=%async_computation.5 | async-start | bytes 2949120 | tf_op jit(solution)/shard_map/reduce_scatter | solution.py:600
  389.8 134.0 %reduce-scatter.9.cloned.1.call-start = ((), (), s32[]{:S(2)}) async-start(), calls=%async_computation.4 | async-start | bytes 2949120 | tf_op jit(solution)/shard_map/reduce_scatter | solution.py:600
  395.9 11.4 %collective-permute-start.35 = (bf16[192,1024]{1,0:T(8,128)(2,1)}, bf16[192,1024]{1,0:T(8,128)(2,1)S(1)}, u32[]{:S(2)}, u32[]{:S(2)}) collective-permute-start(bf16[192,1024]{1,0:T(8,128)(2,1)} %get-tuple-element.363), channel_id=1, source_target_pairs={{0,8},{4,12},{8,0},{12,4},{1,9},{5,13},{9,1},{13,5},{2,10},{6,14},... | collective-permute-start | bytes 1179656 | tf_op jit(solution)/shard_map/ppermute | solution.py:574
  397.1 11.1 %collective-permute-start.36 = (bf16[192,1024]{1,0:T(8,128)(2,1)}, bf16[192,1024]{1,0:T(8,128)(2,1)S(1)}, u32[]{:S(2)}, u32[]{:S(2)}) collective-permute-start(bf16[192,1024]{1,0:T(8,128)(2,1)} %get-tuple-element.364), channel_id=1, source_target_pairs={{0,4},{4,0},{8,12},{12,8},{1,5},{5,1},{9,13},{13,9},{2,6},{6,2},{1... | collective-permute-start | bytes 1179656 | tf_op jit(solution)/shard_map/ppermute | solution.py:574
  414.6 39.0 %collective-permute-start.37 = (bf16[384,1024]{1,0:T(8,128)(2,1)}, bf16[384,1024]{1,0:T(8,128)(2,1)}, u32[]{:S(2)}, u32[]{:S(2)}) collective-permute-start(bf16[384,1024]{1,0:T(8,128)(2,1)} %get-tuple-element.365), channel_id=1, source_target_pairs={{0,4},{4,0},{8,12},{12,8},{1,5},{5,1},{9,13},{13,9},{2,6},{6,2},{1... | collective-permute-start | bytes 2359304 | tf_op jit(solution)/shard_map/ppermute | solution.py:574
  415.9 37.7 %collective-permute-start.38 = (bf16[384,1024]{1,0:T(8,128)(2,1)}, bf16[384,1024]{1,0:T(8,128)(2,1)}, u32[]{:S(2)}, u32[]{:S(2)}) collective-permute-start(bf16[384,1024]{1,0:T(8,128)(2,1)} %get-tuple-element.366), channel_id=1, source_target_pairs={{0,8},{4,12},{8,0},{12,4},{1,9},{5,13},{9,1},{13,5},{2,10},{6,14},... | collective-permute-start | bytes 2359304 | tf_op jit(solution)/shard_map/ppermute | solution.py:574
  425.9 24.5 %collective-permute-start.33 = (bf16[384,1024]{1,0:T(8,128)(2,1)}, bf16[384,1024]{1,0:T(8,128)(2,1)}, u32[]{:S(2)}, u32[]{:S(2)}) collective-permute-start(bf16[384,1024]{1,0:T(8,128)(2,1)} %get-tuple-element.360), channel_id=1, source_target_pairs={{0,4},{4,0},{8,12},{12,8},{1,5},{5,1},{9,13},{13,9},{2,6},{6,2},{1... | collective-permute-start | bytes 2359304 | tf_op jit(solution)/shard_map/ppermute | solution.py:574
  426.7 24.7 %collective-permute-start.34 = (bf16[384,1024]{1,0:T(8,128)(2,1)}, bf16[384,1024]{1,0:T(8,128)(2,1)}, u32[]{:S(2)}, u32[]{:S(2)}) collective-permute-start(bf16[384,1024]{1,0:T(8,128)(2,1)} %get-tuple-element.361), channel_id=1, source_target_pairs={{0,8},{4,12},{8,0},{12,4},{1,9},{5,13},{9,1},{13,5},{2,10},{6,14},... | collective-permute-start | bytes 2359304 | tf_op jit(solution)/shard_map/ppermute | solution.py:574
  430.1 28.4 %collective-permute-start.42 = (f32[6912]{0:T(1024)S(1)}, f32[6912]{0:T(1024)S(1)}, u32[]{:S(2)}, u32[]{:S(2)}) collective-permute-start(f32[6912]{0:T(1024)S(1)} %pad_maximum_fusion.3), channel_id=1, source_target_pairs={{0,1},{1,0},{2,3},{3,2},{4,5},{5,4},{6,7},{7,6},{8,9},{9,8},{10,11... | collective-permute-start | bytes 82952 | tf_op jit(solution)/shard_map/ppermute | solution.py:607
  458.6 21.1 %collective-permute-start.39 = (bf16[384,1024]{1,0:T(8,128)(2,1)}, bf16[384,1024]{1,0:T(8,128)(2,1)S(1)}, u32[]{:S(2)}, u32[]{:S(2)}) collective-permute-start(bf16[384,1024]{1,0:T(8,128)(2,1)} %get-tuple-element.418), channel_id=1, source_target_pairs={{0,16},{16,0},{1,17},{17,1},{2,18},{18,2},{3,19},{19,3},{4,20},{20... | collective-permute-start | bytes 2359304 | tf_op jit(solution)/shard_map/ppermute | solution.py:578
  458.6 11.9 %collective-permute-start.43 = (f32[6912]{0:T(1024)S(1)}, f32[6912]{0:T(1024)S(1)}, u32[]{:S(2)}, u32[]{:S(2)}) collective-permute-start(f32[6912]{0:T(1024)S(1)} %fusion.46), channel_id=1, source_target_pairs={{0,2},{1,3},{2,0},{3,1},{4,6},{5,7},{6,4},{7,5},{8,10},{9,11},{10,... | collective-permute-start | bytes 82952 | tf_op jit(solution)/shard_map/ppermute | solution.py:607
  482.3 42.7 %collective-permute-start.48 = (bf16[128,768]{0,1:T(8,128)(2,1)S(1)}, bf16[128,768]{0,1:T(8,128)(2,1)S(1)}, u32[]{:S(2)}, u32[]{:S(2)}) collective-permute-start(bf16[128,768]{0,1:T(8,128)(2,1)S(1)} %broadcast_select_fusion.14), channel_id=1, source_target_pairs={{0,16},{16,0},{1,17},{17,1},{2,18},{18,2},{3,19},{19,3},{4,20},{20... | collective-permute-start | bytes 589832 | tf_op jit(solution)/shard_map/ppermute | solution.py:578
  (67 other events, 638.8 us)
Sparse Core Ops, SparseCore 0:
  330.6 32.1 reduce-scatter.14
  385.4 37.8 reduce-scatter.12
  425.6 47.8 reduce-scatter.10
  475.6 48.0 reduce-scatter.8

commit v3 on v2

--- a/solution.py
+++ b/solution.py
@@ -578,7 +578,7 @@
     return lax.ppermute(x, "pipe", [(0, 1), (1, 0)])
 
 
-def gather_and_run(x, call, beside=None):
+def gather_and_run(x, call, beside=None, near=None):
     half = x.shape[0] // 2
     one, two = across(x, 1), across(x, 2)
     kept = call(OWN, [x], None)
@@ -586,6 +586,8 @@
     far_a = across(one[:half], 2)
     far_b = across(two[half:], 1)
     kept = call(NEAR, [one, two], kept)
+    if near is not None:
+        kept = near(kept)
     far_a, far_b, kept, beside = lax.optimization_barrier((far_a, far_b, kept, beside))
     kept = call(FAR, [far_a, far_b], kept)
     return (x, one, two, far_a, far_b), kept, beside
@@ -620,56 +622,87 @@
     return a.reshape(-1, a.shape[-1])
 
 
+def tie(*values):
+    return lax.optimization_barrier(values)
+
+
 def forward_layer(x, lp, geo, beside=None):
     call = lambda group, xs, kept: pre_group(group, xs, lp, geo["tables"], kept)
     rows, kept, beside = gather_and_run(x, call, beside)
     n1, n2, q, k, v, g, slope = kept
     o, lse = attend(geo["order"], geo["low"], flat(q), flat(k), flat(v), geo["start_rows"])
-    o_slots = o.reshape(q.shape)
+    saved = dict(rows=rows, n1=n1, n2=n2, q=flat(q), k=flat(k), v=flat(v), g=g, slope=slope, o=o, lse=lse)
+    return saved, beside
+
+
+def branches(saved, lp):
+    g = saved["g"]
+    o_slots = saved["o"].reshape(*g.shape[:2], -1)
     own, far_a, far_b = post_group(ENDS, o_slots, g, lp, [])
     from_one, from_two = across(far_a, 1), across(far_b, 2)
     one, two = post_group(NEAR, o_slots, g, lp, [from_two, from_one])
-    summed = add_rows(own, across(one, 1), across(two, 2))
+    return own, one, two
+
+
+def layer_result(saved, lp, own, got_one, got_two):
     out_biases = lp["out_bias"].astype(F32)
-    result = x.astype(F32) + summed + out_biases[0] + out_biases[1]
-    saved = dict(rows=rows, n1=n1, n2=n2, q=flat(q), k=flat(k), v=flat(v), g=g, slope=slope, o=o, lse=lse)
-    return result.astype(BF), saved, beside
+    summed = add_rows(own, got_one, got_two)
+    return (saved["rows"][0].astype(F32) + summed + out_biases[0] + out_biases[1]).astype(BF)
 
 
 def over_chip(pair):
     return (pair[0].astype(F32) + swap(pair[1]).astype(F32)).astype(BF)
 
 
-def backward_layer(e, lp, saved, geo, core, last):
+def input_grad(e, x, u):
+    x_rows, e_rows = x.astype(F32), e.astype(F32)
+    normal, inverse_std = norm_rows(x_rows)
+    mean_grad = jnp.mean(u, axis=-1, keepdims=True)
+    mean_cross = jnp.mean(u * normal, axis=-1, keepdims=True)
+    return (e_rows + (u - mean_grad - normal * mean_cross) * inverse_std).astype(BF)
+
+
+def back_attention(saved, do, geo):
+    return attend_back(geo["order"], geo["low"], saved["q"], saved["k"], saved["v"], flat(do),
+                       saved["o"], saved["lse"], geo["start_rows"], geo["flat_tables"])
+
+
+def backward_layer(e, lp, saved, geo, core, before=None, after=None, near=None, ending=None):
+    last = ending is not None
     call = lambda group, es, kept: bpre_group(group, es, saved["slope"], lp, kept)
-    _, (e_all, do, df, bin_parts), _ = gather_and_run(e, call)
+    _, kept, _ = gather_and_run(e, call, near=near)
+    e_all, do, df, bin_parts = kept
     early = wgrad_early(core, rows2(saved["o"]), rows2(e_all), rows2(saved["n2"]), rows2(df), rows2(saved["g"]))
+    if before is not None:
+        do = before(do)
     if last:
-        early, do = lax.optimization_barrier((over_chip(early), do))
+        early, do = tie(over_chip(early), do)
         early = dp_reduce(early)
-    dqkv, bqkv_grad = attend_back(geo["order"], geo["low"], saved["q"], saved["k"], saved["v"], flat(do),
-                                  saved["o"], saved["lse"], geo["start_rows"], geo["flat_tables"])
+    dqkv, bqkv_grad = back_attention(saved, do, geo)
+    if after is not None:
+        dqkv = after(dqkv)
     x, x_one, x_two, x_far_a, x_far_b = saved["rows"]
     dqkv_slots = dqkv.reshape(*df.shape[:2], dqkv.shape[-1])
     own, far_a, far_b, sums_a = bpost_group(ENDS, [x, x_far_a, x_far_b], dqkv_slots, df, lp, [])
     from_one, from_two = across(far_a, 1), across(far_b, 2)
     late = wgrad_late(core, rows2(saved["n1"]), rows2(dqkv))
-    late, from_one, from_two = lax.optimization_barrier((late, from_one, from_two))
+    late, from_one, from_two = tie(late, from_one, from_two)
     one, two, sums_b = bpost_group(NEAR, [x_one, x_two], dqkv_slots, df, lp, [from_two, from_one])
     got_one, got_two = across(one, 1), across(two, 2)
-    if not last:
-        early, got_one, got_two = lax.optimization_barrier((early, got_one, got_two))
+    late = over_chip(late)
+    small = jnp.concatenate([sums_a + sums_b, jnp.sum(e.astype(F32), axis=0, keepdims=True)], axis=0)
+    bias_grads = jnp.concatenate([bqkv_grad[0], jnp.sum(bin_parts, axis=(0, 1))])
+    small = (small, bias_grads)
+    if last:
+        early, late = tie(early, late)
+        small = ending(small)
+        small, got_one, got_two = tie(small, got_one, got_two)
+    else:
+        early, got_one, got_two = tie(early, got_one, got_two)
         early = dp_reduce(over_chip(early))
-    u = add_rows(own, got_one, got_two)
-    late = dp_reduce(over_chip(late))
-    x_rows, e_rows = x.astype(F32), e.astype(F32)
-    normal, inverse_std = norm_rows(x_rows)
-    mean_grad = jnp.mean(u, axis=-1, keepdims=True)
-    mean_cross = jnp.mean(u * normal, axis=-1, keepdims=True)
-    dx = e_rows + (u - mean_grad - normal * mean_cross) * inverse_std
-    small = jnp.concatenate([sums_a + sums_b, jnp.sum(e_rows, axis=0, keepdims=True)], axis=0)
-    bias_grads = jnp.concatenate([bqkv_grad[0], jnp.sum(bin_parts, axis=(0, 1))])
-    return dx.astype(BF), (early, late), small, bias_grads
+    late = dp_reduce(late)
+    dx = input_grad(e, x, add_rows(own, got_one, got_two))
+    return dx, early, late, small
 
 
 def unpack_out(g, rows, d):
@@ -700,6 +733,7 @@
     own = dict(ln_gain=ln_gain[0], ln_bias=ln_bias[0], w_qkv=column_order(w_qkv[0], 1),
                b_qkv=column_order(b_qkv, 1), w_out=w_out[0], w_in=w_in[0], b_in=b_in, w_fc2=w_fc2[0],
                out_bias=out_bias[0])
+    own, x0, e1 = tie(own, x0, e1)
     small_names = ("ln_gain", "ln_bias", "b_qkv", "b_in", "out_bias")
     packed = jnp.concatenate([own[s].reshape(-1) for s in small_names]).reshape(-1, LANES)
     other_packed = swap(packed).reshape(-1)
@@ -740,21 +774,56 @@
     )
 
     core = lax.axis_index("pipe").astype(jnp.int32).reshape(1)
-    h, saved0, _ = forward_layer(x0, layer0, geo)
-    y1, saved1, e1 = forward_layer(h, layer1, geo, e1)
-    e0, half1, small1, bias1 = backward_layer(e1, layer1, saved1, geo, core, False)
-    dx0, half0, small0, bias0 = backward_layer(e0, layer0, saved0, geo, core, True)
-
-    got = swap(choose(y1, dx0))
-    mine = choose(dx0, y1)
-    boundary = jnp.stack([choose(mine, got), choose(got, mine)])[None]
-
-    full = []
-    for one, zero in zip(half1, half0):
-        got = swap(choose(one, zero))
-        mine = choose(zero, one)
-        full.append((choose(mine, got).astype(F32), choose(got, mine).astype(F32)))
-    early, g_qkv = full
+    saved0, _ = forward_layer(x0, layer0, geo)
+    own, one, two = branches(saved0, layer0)
+    h = layer_result(saved0, layer0, own, across(one, 1), across(two, 2))
+    saved1, e1 = forward_layer(h, layer1, geo, e1)
+
+    to_next = lambda a: lax.ppermute(a, "pipe", [(0, 1)])
+    to_first = lambda a: lax.ppermute(a, "pipe", [(1, 0)])
+    held = {}
+
+    def send_result(do):
+        own, one, two = branches(saved1, layer1)
+        one, two, do = tie(one, two, do)
+        held["y"] = own, across(one, 1), across(two, 2)
+        return do
+
+    def take_result(dqkv):
+        own, got_one, got_two = held["y"]
+        got_one, got_two, dqkv = tie(got_one, got_two, dqkv)
+        y1 = layer_result(saved1, layer1, own, got_one, got_two)
+        held["y1"] = y1, to_next(y1)
+        return dqkv
+
+    e0, early1, late1, small1 = backward_layer(e1, layer1, saved1, geo, core, send_result, take_result)
+
+    def take_late(kept):
+        held["late"], kept = tie(late1, kept)
+        return kept
+
+    def take_early(dqkv):
+        held["early"], dqkv = tie(early1, dqkv)
+        return dqkv
+
+    n_dp = lax.axis_size("dp")
+
+    def small_sums(small0):
+        mine = [choose(a, b) for a, b in zip(small0, small1)]
+        theirs = [choose(b, a) for a, b in zip(small0, small1)]
+        packed = lambda pair: jnp.concatenate([pair[0].reshape(-1), pair[1]])
+        return butterfly(packed(mine) + swap(packed(theirs)), "dp")
+
+    dx0, early0, late0, line = backward_layer(e0, layer0, saved0, geo, core, None, take_early, take_late, small_sums)
+
+    y1, y1_got = held["y1"]
+    boundary = jnp.stack([choose(dx0, y1_got), choose(to_first(dx0), y1)])[None]
+
+    def halves(one, zero):
+        from_first, from_second = to_next(one), to_first(zero)
+        return choose(zero, from_first).astype(F32), choose(from_second, one).astype(F32)
+
+    early, g_qkv = halves(held["early"], early0), halves(held["late"], late0)
     n_out, n_in = w_out.shape[1], w_in.shape[2]
     join = lambda f: jnp.concatenate([f(early[0]), f(early[1])], axis=0)
     g_out = join(lambda a: unpack_out(a[:, :n_out], n_out, d))
@@ -762,12 +831,8 @@
     g_fc2 = join(lambda a: a[:, n_out + n_in:])
     g_qkv = jnp.concatenate(g_qkv, axis=0)
 
-    n_dp = lax.axis_size("dp")
-    small = choose(small0, small1) + swap(choose(small1, small0))
-    bias = choose(bias0, bias1) + swap(choose(bias1, bias0))
-    at = small.size
-    line = butterfly(jnp.concatenate([small.reshape(-1), bias]), "dp")
-    small, bias = line[:at].reshape(small.shape), line[at:]
+    at = 5 * d
+    small, bias = line[:at].reshape(5, d), line[at:]
     small = butterfly(small, "tensor").reshape(small.shape[0], n_tensor * n_dp, -1)
     where = lax.axis_index("dp")
     pick = lambda a, i: lax.dynamic_index_in_dim(a, i, -2, keepdims=False)

time: 547 us -> 513 us (0.938)
  waiting for transfers between devices: 134 us -> 89.3 us
  Pallas kernels: 247 us -> 264 us
  starting transfers between devices: 66.4 us -> 53.7 us
    reduce_scatter x2, waiting for transfers between devices: 41.4 us -> 0.01 us  [dp_reduce(): lax.psum_scatter(blocks.reshape(n * rows, cols), 'dp', scatter_dimension=...]
    ppermute x4, starting transfers between devices: 29.4 us -> 4.93 us  [butterfly(): vec = vec + lax.ppermute(vec, axis, [(i, i ^ k) for i in range(n)])]
    ppermute x32, waiting for transfers between devices: 73.3 us -> 57.2 us  [across(): return lax.ppermute(x, 'tensor', [(i, i ^ k) for i in range(n)])]
    unnamed x6, waiting for transfers between devices: 0.57 us -> 14.4 us
    pallas_call x2, Pallas kernels: 50.2 us -> 60.3 us  [attend_back(): pl.pallas_call(attend_back_kernel, grid=(1,), in_specs=[SMEM_SPEC, SMEM_S...]
    ppermute x0 -> x6, starting transfers between devices: none -> 9.37 us  [the longest x3 5.51 us: body(): to_next = lambda a: lax.ppermute(a, 'pipe', [(0, 1)])]
    pallas_call x2, Pallas kernels: 24.8 us -> 30.3 us  [attend(): pl.pallas_call(attend_kernel, grid=(1,), in_specs=[SMEM_SPEC, SMEM_SPEC]...]
    select_n x15 -> x13, other arithmetic: 22.7 us -> 18.7 us  [body(): choose = lambda a, b: jnp.where(is_first, a, b)]
  transfers between devices with their start and end apart: 55 -> 57, of which waited for: 29 -> 26; matrix products, arithmetic and copies ran while one was open for 12% -> 13% of each run, Pallas kernels for 28% -> 41%
where the time goes in v3:
time: 513 us; the launch traced here: 504 us
  Pallas kernels  264 us (51%)
  waiting for transfers between devices  89.3 us (17%)
  other arithmetic  58.1 us (11%)
  starting transfers between devices  53.7 us (10%)
  local copies, waits for them, and re-layouts  23.5 us (5%)
  between operations  15.1 us (3%)
    pallas_call x12, Pallas kernels, group_call(): pl.pallas_call(functools.partial(kernel, n_alias), grid=grid, in_specs=sp...  76.8 us
    pallas_call x2, Pallas kernels, attend_back(): pl.pallas_call(attend_back_kernel, grid=(1,), in_specs=[SMEM_SPEC, SMEM_S...  60.3 us
    ppermute x32, waiting for transfers between devices, across(): return lax.ppermute(x, 'tensor', [(i, i ^ k) for i in range(n)])  57.2 us
    ppermute x32, starting transfers between devices, across(): return lax.ppermute(x, 'tensor', [(i, i ^ k) for i in range(n)])  37 us
    pallas_call x4, Pallas kernels, bpost_group(): pl.pallas_call(functools.partial(bpost_kernel, len(xs), len(addends), ck)...  34.8 us
    pallas_call x2, Pallas kernels, attend(): pl.pallas_call(attend_kernel, grid=(1,), in_specs=[SMEM_SPEC, SMEM_SPEC]...  30.3 us
    pallas_call x2, Pallas kernels, wgrad_early(): pl.pallas_call(functools.partial(wgrad_kernel, True), grid=(steps,), in_s...  26.7 us
    pallas_call x4, Pallas kernels, post_group(): pl.pallas_call(functools.partial(post_kernel, len(addends)), grid=(d // c...  22 us
  transfers between devices with their start and end apart: 57, of which 26 were waited for; matrix products, arithmetic and copies ran while one was open for 13% of the time, Pallas kernels for 41%

profile of v3, /device:TPU:0, one launch (start us, length us, event | category | flops | bytes accessed | tf_op | source)
XLA Modules:
  0.0 503.5 jit_solution(9685622301435067930)
XLA Ops:
  21.0 2.9 collective-permute-start.1
  26.0 4.5 fusion.24
  36.8 3.5 broadcast_select_fusion.4
  40.3 3.8 broadcast_select_fusion.1
  44.1 6.3 %shard_map.204 = (bf16[4,384,1024]{2,1,0:T(8,128)(2,1)}, bf16[4,384,1024]{2,1,0:T(8,128)(2,1)}, bf16[4,384,256]{2,1,0:T(8,128)(2,1)}, bf16[4,384,256]{2,1,0:T(8,...) custom-call(bf16[384,1024]{1,0:T(8,128)(2,1)} %copy-done.1, ...), custom_call_target="tpu_custom_call" | custom-call | flops 1409286144 | bytes 7602176 | tf_op jit(solution)/shard_map/pallas_call | solution.py:121
  56.1 9.9 %shard_map.205 = (bf16[4,384,1024]{2,1,0:T(8,128)(2,1)}, bf16[4,384,1024]{2,1,0:T(8,128)(2,1)}, bf16[4,384,256]{2,1,0:T(8,128)(2,1)}, bf16[4,384,256]{2,1,0:T(8,...) custom-call(bf16[384,1024]{1,0:T(8,128)(2,1)} %collective-permute-do, ...), custom_call_target="tpu_custom_call", output_to_operand_aliasing={{0}: (11, {}), {1}: (12, {}), {2}: (13, {}), {3}: (14, {}),... | custom-call | flops 2818572288 | bytes 11534336 | tf_op jit(solution)/shard_map/pallas_call | solution.py:121
  66.0 4.5 broadcast_select_fusion
  71.4 6.7 %shard_map.206 = (bf16[4,384,1024]{2,1,0:T(8,128)(2,1)}, bf16[4,384,1024]{2,1,0:T(8,128)(2,1)}, bf16[4,384,256]{2,1,0:T(8,128)(2,1)}, bf16[4,384,256]{2,1,0:T(8,...) custom-call(bf16[192,1024]{1,0:T(8,128)(2,1)} %copy-done.28, ...), custom_call_target="tpu_custom_call", output_to_operand_aliasing={{0}: (11, {}), {1}: (12, {}), {2}: (13, {}), {3}: (14, {}),... | custom-call | flops 1409286144 | bytes 7602176 | tf_op jit(solution)/shard_map/pallas_call | solution.py:121
  78.1 15.2 %shard_map.207 = (bf16[12,128,256]{2,1,0:T(8,128)(2,1)}, f32[6,8,256]{2,1,0:T(8,128)}) custom-call(s32[12]{0:T(128)} %fusion.37.order_ref, s32[6]{0:T(128)} %and_select_fusion.2.low_ref, bf16[12,128,256]{2,1,0:T(8,128)(2,1)} %bitcast.165, bf16[12,128,256]{2,1,0:T(8,128)(2,1)} %bitcast.167, bf16[12,128,256]{2,1,0:T(8,128)(2,1)} %bitcast.169, ...), custom_call_target="tpu_custom_call" | custom-call | flops 1811939328 | bytes 1966080 | tf_op jit(solution)/shard_map/pallas_call | solution.py:461
  93.2 5.3 %shard_map.208 = (f32[384,1024]{1,0:T(8,128)}, bf16[192,1024]{1,0:T(8,128)(2,1)}, bf16[192,1024]{1,0:T(8,128)(2,1)}) custom-call(bf16[4,384,256]{2,1,0:T(8,128)(2,1)} %bitcast.210, bf16[4,384,1024]{2,1,0:T(8,128)(2,1)} %get-tuple-element.274.g_ref, bf16[256,1024]{1,0:T(8,128)(2,1)} %get-tuple-element.485.wout_ref.refs_1_.refs_2_, ...), custom_call_target="tpu_custom_call" | custom-call | flops 2013265920 | bytes 6553600 | tf_op jit(solution)/shard_map/pallas_call | solution.py:202
  100.6 8.0 %collective-permute-done.10.rest_0_ = bf16[192,1024]{1,0:T(8,128)(2,1)S(1)} collective-permute-done((bf16[192,1024]{1,0:T(8,128)(2,1)}, bf16[192,1024]{1,0:T(8,128)(2,1)S(1)}, u32[]{:S(2)}, u32[]{:S(2)}) %collective-permute-start.10) | collective-permute-done | bytes 393248 | tf_op jit(solution)/shard_map/ppermute | solution.py:574
  110.0 5.7 %shard_map.209 = (bf16[384,1024]{1,0:T(8,128)(2,1)}, bf16[384,1024]{1,0:T(8,128)(2,1)}) custom-call(bf16[4,384,256]{2,1,0:T(8,128)(2,1)} %bitcast.211, bf16[4,384,1024]{2,1,0:T(8,128)(2,1)} %get-tuple-element.274.g_ref, bf16[256,1024]{1,0:T(8,128)(2,1)} %get-tuple-element.485.wout_ref.refs_1_.refs_2_, ...), custom_call_target="tpu_custom_call" | custom-call | flops 2013265920 | bytes 6553600 | tf_op jit(solution)/shard_map/pallas_call | solution.py:202
  118.5 14.9 %collective-permute-done.13 = bf16[384,1024]{1,0:T(8,128)(2,1)} collective-permute-done((bf16[384,1024]{1,0:T(8,128)(2,1)}, bf16[384,1024]{1,0:T(8,128)(2,1)}, u32[]{:S(2)}, u32[]{:S(2)}) %collective-permute-start.13) | collective-permute-done | bytes 786464 | tf_op jit(solution)/shard_map/ppermute | solution.py:574
  138.9 6.3 %shard_map.210 = (bf16[4,384,1024]{2,1,0:T(8,128)(2,1)}, bf16[4,384,1024]{2,1,0:T(8,128)(2,1)}, bf16[4,384,256]{2,1,0:T(8,128)(2,1)}, bf16[4,384,256]{2,1,0:T(8,...) custom-call(bf16[384,1024]{1,0:T(8,128)(2,1)} %copy-done.4, ...), custom_call_target="tpu_custom_call" | custom-call | flops 1409286144 | bytes 7602176 | tf_op jit(solution)/shard_map/pallas_call | solution.py:121
  145.2 7.1 %collective-permute-done.14.refs_0_ = bf16[384,1024]{1,0:T(8,128)(2,1)S(1)} collective-permute-done((bf16[384,1024]{1,0:T(8,128)(2,1)S(1)}, bf16[384,1024]{1,0:T(8,128)(2,1)S(1)}, u32[]{:S(2)}, u32[]{:S(2)}) %collective-permute-start.14) | collective-permute-done | bytes 786464 | tf_op jit(solution)/shard_map/ppermute | solution.py:574
  152.3 2.9 collective-permute-done.15.refs_1_
  157.3 10.1 %shard_map.211 = (bf16[4,384,1024]{2,1,0:T(8,128)(2,1)}, bf16[4,384,1024]{2,1,0:T(8,128)(2,1)}, bf16[4,384,256]{2,1,0:T(8,128)(2,1)}, bf16[4,384,256]{2,1,0:T(8,...) custom-call(bf16[384,1024]{1,0:T(8,128)(2,1)} %copy-done.14, ...), custom_call_target="tpu_custom_call", output_to_operand_aliasing={{0}: (11, {}), {1}: (12, {}), {2}: (13, {}), {3}: (14, {}),... | custom-call | flops 2818572288 | bytes 11534336 | tf_op jit(solution)/shard_map/pallas_call | solution.py:121
  169.7 6.3 %shard_map.212 = (bf16[4,384,1024]{2,1,0:T(8,128)(2,1)}, bf16[4,384,1024]{2,1,0:T(8,128)(2,1)}, bf16[4,384,256]{2,1,0:T(8,128)(2,1)}, bf16[4,384,256]{2,1,0:T(8,...) custom-call(bf16[192,1024]{1,0:T(8,128)(2,1)} %copy-done.30, ...), custom_call_target="tpu_custom_call", output_to_operand_aliasing={{0}: (11, {}), {1}: (12, {}), {2}: (13, {}), {3}: (14, {}),... | custom-call | flops 1409286144 | bytes 7602176 | tf_op jit(solution)/shard_map/pallas_call | solution.py:121
  176.0 15.2 %shard_map.213 = (bf16[12,128,256]{2,1,0:T(8,128)(2,1)}, f32[6,8,256]{2,1,0:T(8,128)}) custom-call(s32[12]{0:T(128)} %fusion.37.order_ref, s32[6]{0:T(128)} %and_select_fusion.2.low_ref, bf16[12,128,256]{2,1,0:T(8,128)(2,1)} %bitcast.171, bf16[12,128,256]{2,1,0:T(8,128)(2,1)} %bitcast.173, bf16[12,128,256]{2,1,0:T(8,128)(2,1)} %bitcast.175, ...), custom_call_target="tpu_custom_call" | custom-call | flops 1811939328 | bytes 1966080 | tf_op jit(solution)/shard_map/pallas_call | solution.py:461
  191.1 5.3 %shard_map.214 = (f32[384,1024]{1,0:T(8,128)}, bf16[192,1024]{1,0:T(8,128)(2,1)}, bf16[192,1024]{1,0:T(8,128)(2,1)}) custom-call(bf16[4,384,256]{2,1,0:T(8,128)(2,1)} %bitcast.213, bf16[4,384,1024]{2,1,0:T(8,128)(2,1)} %get-tuple-element.320.g_ref, bf16[256,1024]{1,0:T(8,128)(2,1)} %get-tuple-element.484.wout_ref.refs_1_.refs_2_, ...), custom_call_target="tpu_custom_call" | custom-call | flops 2013265920 | bytes 6553600 | tf_op jit(solution)/shard_map/pallas_call | solution.py:202
  198.3 4.4 shard_map.216
  207.2 5.6 %shard_map.215 = (bf16[384,1024]{1,0:T(8,128)(2,1)}, bf16[384,1024]{1,0:T(8,128)(2,1)}) custom-call(bf16[4,384,256]{2,1,0:T(8,128)(2,1)} %bitcast.214, bf16[4,384,1024]{2,1,0:T(8,128)(2,1)} %get-tuple-element.320.g_ref, bf16[256,1024]{1,0:T(8,128)(2,1)} %get-tuple-element.484.wout_ref.refs_1_.refs_2_, ...), custom_call_target="tpu_custom_call" | custom-call | flops 2013265920 | bytes 6553600 | tf_op jit(solution)/shard_map/pallas_call | solution.py:202
  212.9 6.4 %shard_map.217 = (bf16[4,384,1024]{2,1,0:T(8,128)(2,1)}, bf16[4,384,256]{2,1,0:T(8,128)(2,1)}, bf16[4,384,1024]{2,1,0:T(8,128)(2,1)}, f32[4,1,1024]{2,1,0:T(1,128)}) custom-call(bf16[384,1024]{1,0:T(8,128)(2,1)} %copy-done.23, bf16[384,1024]{1,0:T(8,128)(2,1)} %copy-done.24, ...), custom_call_target="tpu_custom_call", output_to_operand_aliasing={{0}: (5, {}), {1}: (6, {}), {2}: (7, {}), {3}: (8, {})} | custom-call | flops 2013265920 | bytes 8912896 | tf_op jit(solution)/shard_map/pallas_call | solution.py:121
  220.2 4.8 shard_map.218
  227.6 30.0 %shard_map.219 = (bf16[12,128,768]{2,1,0:T(8,128)(2,1)}, f32[1,768]{1,0:T(1,128)}) custom-call(s32[12]{0:T(128)} %fusion.37.order_ref, s32[6]{0:T(128)} %and_select_fusion.2.low_ref, bf16[12,128,256]{2,1,0:T(8,128)(2,1)} %bitcast.172, bf16[12,128,256]{2,1,0:T(8,128)(2,1)} %bitcast.174, bf16[12,128,256]{2,1,0:T(8,128)(2,1)} %bitcast.176, ...), custom_call_target="tpu_custom_call" | custom-call | flops 4831838208 | bytes 6291456 | tf_op jit(solution)/shard_map/pallas_call | solution.py:558
  257.7 8.9 %shard_map.220 = (f32[384,1024]{1,0:T(8,128)}, bf16[192,1024]{1,0:T(8,128)(2,1)}, bf16[192,1024]{1,0:T(8,128)(2,1)}, f32[4,1024]{1,0:T(4,128)}) custom-call(bf16[384,1024]{1,0:T(8,128)(2,1)} %copy-done.4, bf16[192,1024]{1,0:T(8,128)(2,1)} %copy-done.30, bf16[192,1024]{1,0:T(8,128)(2,1)} %copy-done.31, ...), custom_call_target="tpu_custom_call" | custom-call | flops 2818572288 | bytes 9175040 | tf_op jit(solution)/shard_map/pallas_call | solution.py:291
  268.2 6.5 %shard_map.222 = (bf16[4,128,768]{2,1,0:T(8,128)(2,1)}, bf16[4,128,768]{2,1,0:T(8,128)(2,1)}) custom-call(s32[1]{0:T(128)} %bitcast.39.core_ref, bf16[1536,1024]{1,0:T(8,128)(2,1)} %bitcast.150, bf16[1536,768]{1,0:T(8,128)(2,1)} %bitcast.161), custom_call_target="tpu_custom_call" | custom-call | flops 2415919104 | bytes 7864320 | tf_op jit(solution)/shard_map/pallas_call | solution.py:377
  276.0 8.6 %shard_map.223 = (bf16[384,1024]{1,0:T(8,128)(2,1)}, bf16[384,1024]{1,0:T(8,128)(2,1)}, f32[4,1024]{1,0:T(4,128)}) custom-call(bf16[384,1024]{1,0:T(8,128)(2,1)} %copy-done.14, bf16[384,1024]{1,0:T(8,128)(2,1)} %copy-done.15, bf16[2,1024]{1,0:T(2,128)(2,1)} %get-tuple-element.518.refs_1_.refs_2_.refs_3_, bf16[4,384,768]{2,1,0:T(8,128)(2,1)} %bitcast.162, ...), custom_call_target="tpu_custom_call" | custom-call | flops 2818572288 | bytes 9175040 | tf_op jit(solution)/shard_map/pallas_call | solution.py:291
  287.0 13.6 %shard_map.221 = (bf16[4,128,2304]{2,1,0:T(8,128)(2,1)}, bf16[4,128,2304]{2,1,0:T(8,128)(2,1)}) custom-call(s32[1]{0:T(128)} %bitcast.39.core_ref, bf16[1536,256]{1,0:T(8,128)(2,1)} %bitcast.215, bf16[1536,1024]{1,0:T(8,128)(2,1)} %bitcast.153, bf16[1536,1024]{1,0:T(8,128)(2,1)} %bitcast.151, bf16[1536,1024]{1,0:T(8,128)(2,1)} %bitcast.139, ...), custom_call_target="tpu_custom_call" | custom-call | flops 7247757312 | bytes 17301504 | tf_op jit(solution)/shard_map/pallas_call | solution.py:361
  301.7 4.3 collective-permute-done.35
  309.5 3.8 convert_reduce_fusion.2
  315.0 3.8 add_convert_fusion.1
  318.8 4.4 shard_map.224
  323.3 9.8 %collective-permute-done.31.refs_0_ = bf16[384,1024]{1,0:T(8,128)(2,1)S(1)} collective-permute-done((bf16[384,1024]{1,0:T(8,128)(2,1)S(1)}, bf16[384,1024]{1,0:T(8,128)(2,1)S(1)}, u32[]{:S(2)}, u32[]{:S(2)}) %collective-permute-start.31) | collective-permute-done | bytes 786464 | tf_op jit(solution)/shard_map/ppermute | solution.py:574
  336.2 6.8 %shard_map.225 = (bf16[4,384,1024]{2,1,0:T(8,128)(2,1)}, bf16[4,384,256]{2,1,0:T(8,128)(2,1)}, bf16[4,384,1024]{2,1,0:T(8,128)(2,1)}, f32[4,1,1024]{2,1,0:T(1,128)}) custom-call(bf16[384,1024]{1,0:T(8,128)(2,1)} %copy-done.25, bf16[384,1024]{1,0:T(8,128)(2,1)} %copy-done.26, ...), custom_call_target="tpu_custom_call", output_to_operand_aliasing={{0}: (5, {}), {1}: (6, {}), {2}: (7, {}), {3}: (8, {})} | custom-call | flops 2013265920 | bytes 8912896 | tf_op jit(solution)/shard_map/pallas_call | solution.py:121
  345.6 4.5 shard_map.226
  350.0 13.1 %shard_map.227 = (bf16[4,128,2304]{2,1,0:T(8,128)(2,1)}, bf16[4,128,2304]{2,1,0:T(8,128)(2,1)}) custom-call(s32[1]{0:T(128)} %bitcast.39.core_ref, bf16[1536,256]{1,0:T(8,128)(2,1)} %bitcast.212, bf16[1536,1024]{1,0:T(8,128)(2,1)} %bitcast.154, bf16[1536,1024]{1,0:T(8,128)(2,1)} %bitcast.148, bf16[1536,1024]{1,0:T(8,128)(2,1)} %bitcast.140, ...), custom_call_target="tpu_custom_call" | custom-call | flops 7247757312 | bytes 17301504 | tf_op jit(solution)/shard_map/pallas_call | solution.py:361
  363.1 4.7 collective-permute-done.36
  367.8 3.6 add_convert_fusion
  371.5 30.2 %shard_map.228 = (bf16[12,128,768]{2,1,0:T(8,128)(2,1)}, f32[1,768]{1,0:T(1,128)}) custom-call(s32[12]{0:T(128)} %fusion.37.order_ref, s32[6]{0:T(128)} %and_select_fusion.2.low_ref, bf16[12,128,256]{2,1,0:T(8,128)(2,1)} %bitcast.166, bf16[12,128,256]{2,1,0:T(8,128)(2,1)} %bitcast.168, bf16[12,128,256]{2,1,0:T(8,128)(2,1)} %bitcast.170, ...), custom_call_target="tpu_custom_call" | custom-call | flops 4831838208 | bytes 6291456 | tf_op jit(solution)/shard_map/pallas_call | solution.py:558
  401.8 8.4 %shard_map.229 = (f32[384,1024]{1,0:T(8,128)}, bf16[192,1024]{1,0:T(8,128)(2,1)}, bf16[192,1024]{1,0:T(8,128)(2,1)}, f32[4,1024]{1,0:T(4,128)}) custom-call(bf16[384,1024]{1,0:T(8,128)(2,1)} %copy-done.1, bf16[192,1024]{1,0:T(8,128)(2,1)} %copy-done.28, bf16[192,1024]{1,0:T(8,128)(2,1)} %copy-done.29, ...), custom_call_target="tpu_custom_call" | custom-call | flops 2818572288 | bytes 9175040 | tf_op jit(solution)/shard_map/pallas_call | solution.py:291
  412.7 6.6 %shard_map.230 = (bf16[4,128,768]{2,1,0:T(8,128)(2,1)}, bf16[4,128,768]{2,1,0:T(8,128)(2,1)}) custom-call(s32[1]{0:T(128)} %bitcast.39.core_ref, bf16[1536,1024]{1,0:T(8,128)(2,1)} %bitcast.147, bf16[1536,768]{1,0:T(8,128)(2,1)} %bitcast.158), custom_call_target="tpu_custom_call" | custom-call | flops 2415919104 | bytes 7864320 | tf_op jit(solution)/shard_map/pallas_call | solution.py:377
  423.5 8.8 %shard_map.231 = (bf16[384,1024]{1,0:T(8,128)(2,1)}, bf16[384,1024]{1,0:T(8,128)(2,1)}, f32[4,1024]{1,0:T(4,128)}) custom-call(bf16[384,1024]{1,0:T(8,128)(2,1)} %collective-permute-done.1.refs_0_, bf16[384,1024]{1,0:T(8,128)(2,1)} %copy-done.13, bf16[2,1024]{1,0:T(2,128)(2,1)} %get-tuple-element.517.refs_1_.refs_2_.refs_3_, bf16[4,384,768]{2,1,0:T(8,128)(2,1)} %bitcast.159, ...), custom_call_target="tpu_custom_call" | custom-call | flops 2818572288 | bytes 9175040 | tf_op jit(solution)/shard_map/pallas_call | solution.py:291
  439.7 2.6 collective-permute-start.41
  446.6 4.6 collective-permute-done.42
  453.7 3.4 select_bitcast_fusion.1
  464.6 2.8 collective-permute-done.47
  476.7 14.3 %reduce-scatter.15.cloned.1.call-done = bf16[128,768]{1,0:T(8,128)(2,1)} async-done(((bf16[512,768]{1,0:T(8,128)(2,1)}), bf16[128,768]{1,0:T(8,128)(2,1)}) %reduce-scatter.15.cloned.1.call-update) | async-done | bytes 196624
  (376 shorter events, 114.9 us)
Async XLA Ops:
  7.2 335.8 %reduce-scatter.13.cloned.1.call-start = ((), (), s32[]{:S(2)}) async-start(), calls=%async_computation.6 | async-start | bytes 983040
  7.2 10.8 %collective-permute-start = (bf16[2,384,1024]{2,1,0:T(8,128)(2,1)}, bf16[2,384,1024]{2,1,0:T(8,128)(2,1)}, u32[]{:S(2)}, u32[]{:S(2)}) collective-permute-start(bf16[2,384,1024]{2,1,0:T(8,128)(2,1)} %bitcast.184), channel_id=1, source_target_pairs={{0,16},{16,0},{1,17},{17,1},{2,18},{18,2},{3,19},{19,3},{4,20},{20... | collective-permute-start | bytes 4718600 | tf_op jit(solution)/shard_map/ppermute | solution.py:578
  20.9 9.6 %collective-permute-start.3 = (bf16[62,128]{1,0:T(8,128)(2,1)S(1)}, bf16[62,128]{1,0:T(8,128)(2,1)S(1)}, u32[]{:S(2)}, u32[]{:S(2)}) collective-permute-start(bf16[62,128]{1,0:T(8,128)(2,1)S(1)} %bitcast.209), channel_id=1, source_target_pairs={{0,16},{16,0},{1,17},{17,1},{2,18},{18,2},{3,19},{19,3},{4,20},{20... | collective-permute-start | bytes 47624 | tf_op jit(solution)/shard_map/ppermute | solution.py:578
  21.0 29.3 %collective-permute-start.1 = (bf16[384,1024]{1,0:T(8,128)(2,1)S(1)}, bf16[384,1024]{1,0:T(8,128)(2,1)}, u32[]{:S(2)}, u32[]{:S(2)}) collective-permute-start(bf16[384,1024]{1,0:T(8,128)(2,1)S(1)} %get-tuple-element.226.refs_0_), channel_id=1, source_target_pairs={{0,4},{4,0},{8,12},{12,8},{1,5},{5,1},{9,13},{13,9},{2,6},{6,2},{1... | collective-permute-start | bytes 2359304 | tf_op jit(solution)/shard_map/ppermute | solution.py:574
  25.5 11.3 %collective-permute-start.4 = (bf16[1024,768]{1,0:T(8,128)(2,1)}, bf16[1024,768]{1,0:T(8,128)(2,1)}, u32[]{:S(2)}, u32[]{:S(2)}) collective-permute-start(bf16[1024,768]{1,0:T(8,128)(2,1)} %copy.97), channel_id=1, source_target_pairs={{0,16},{16,0},{1,17},{17,1},{2,18},{18,2},{3,19},{19,3},{4,20},{20... | collective-permute-start | bytes 4718600 | tf_op jit(solution)/shard_map/ppermute | solution.py:578
  25.5 14.8 %collective-permute-start.5 = (bf16[1024,1024]{1,0:T(8,128)(2,1)}, bf16[1024,1024]{1,0:T(8,128)(2,1)}, u32[]{:S(2)}, u32[]{:S(2)}) collective-permute-start(bf16[1024,1024]{1,0:T(8,128)(2,1)} %bitcast.182), channel_id=1, source_target_pairs={{0,16},{16,0},{1,17},{17,1},{2,18},{18,2},{3,19},{19,3},{4,20},{20... | collective-permute-start | bytes 6291464 | tf_op jit(solution)/shard_map/ppermute | solution.py:578
  30.5 35.5 %collective-permute-start.9 = (bf16[1024,1024]{1,0:T(8,128)(2,1)}, bf16[1024,1024]{1,0:T(8,128)(2,1)}, u32[]{:S(2)}, u32[]{:S(2)}) collective-permute-start(bf16[1024,1024]{1,0:T(8,128)(2,1)} %bitcast.6), channel_id=1, source_target_pairs={{0,16},{16,0},{1,17},{17,1},{2,18},{18,2},{3,19},{19,3},{4,20},{20... | collective-permute-start | bytes 6291464 | tf_op jit(solution)/shard_map/ppermute | solution.py:578
  33.0 19.6 %collective-permute-start.2 = (bf16[384,1024]{1,0:T(8,128)(2,1)S(1)}, bf16[384,1024]{1,0:T(8,128)(2,1)S(1)}, u32[]{:S(2)}, u32[]{:S(2)}) collective-permute-start(bf16[384,1024]{1,0:T(8,128)(2,1)S(1)} %get-tuple-element.226.refs_0_), channel_id=1, source_target_pairs={{0,8},{4,12},{8,0},{12,4},{1,9},{5,13},{9,1},{13,5},{2,10},{6,14},... | collective-permute-start | bytes 2359304 | tf_op jit(solution)/shard_map/ppermute | solution.py:574
  53.9 16.6 %collective-permute-start.6 = (bf16[192,1024]{1,0:T(8,128)(2,1)S(1)}, bf16[192,1024]{1,0:T(8,128)(2,1)S(1)}, u32[]{:S(2)}, u32[]{:S(2)}) collective-permute-start(bf16[192,1024]{1,0:T(8,128)(2,1)S(1)} %slice.164), channel_id=1, source_target_pairs={{0,8},{4,12},{8,0},{12,4},{1,9},{5,13},{9,1},{13,5},{2,10},{6,14},... | collective-permute-start | bytes 1179656 | tf_op jit(solution)/shard_map/ppermute | solution.py:574
  55.5 15.0 %collective-permute-start.7 = (bf16[192,1024]{1,0:T(8,128)(2,1)S(1)}, bf16[192,1024]{1,0:T(8,128)(2,1)S(1)}, u32[]{:S(2)}, u32[]{:S(2)}) collective-permute-start(bf16[192,1024]{1,0:T(8,128)(2,1)S(1)} %slice.165), channel_id=1, source_target_pairs={{0,4},{4,0},{8,12},{12,8},{1,5},{5,1},{9,13},{13,9},{2,6},{6,2},{1... | collective-permute-start | bytes 1179656 | tf_op jit(solution)/shard_map/ppermute | solution.py:574
  98.6 10.0 %collective-permute-start.10 = (bf16[192,1024]{1,0:T(8,128)(2,1)}, bf16[192,1024]{1,0:T(8,128)(2,1)S(1)}, u32[]{:S(2)}, u32[]{:S(2)}) collective-permute-start(bf16[192,1024]{1,0:T(8,128)(2,1)} %get-tuple-element.278), channel_id=1, source_target_pairs={{0,8},{4,12},{8,0},{12,4},{1,9},{5,13},{9,1},{13,5},{2,10},{6,14},... | collective-permute-start | bytes 1179656 | tf_op jit(solution)/shard_map/ppermute | solution.py:574
  98.9 10.0 %collective-permute-start.11 = (bf16[192,1024]{1,0:T(8,128)(2,1)}, bf16[192,1024]{1,0:T(8,128)(2,1)S(1)}, u32[]{:S(2)}, u32[]{:S(2)}) collective-permute-start(bf16[192,1024]{1,0:T(8,128)(2,1)} %get-tuple-element.279), channel_id=1, source_target_pairs={{0,4},{4,0},{8,12},{12,8},{1,5},{5,1},{9,13},{13,9},{2,6},{6,2},{1... | collective-permute-start | bytes 1179656 | tf_op jit(solution)/shard_map/ppermute | solution.py:574
  115.8 17.6 %collective-permute-start.13 = (bf16[384,1024]{1,0:T(8,128)(2,1)}, bf16[384,1024]{1,0:T(8,128)(2,1)}, u32[]{:S(2)}, u32[]{:S(2)}) collective-permute-start(bf16[384,1024]{1,0:T(8,128)(2,1)} %get-tuple-element.281), channel_id=1, source_target_pairs={{0,8},{4,12},{8,0},{12,4},{1,9},{5,13},{9,1},{13,5},{2,10},{6,14},... | collective-permute-start | bytes 2359304 | tf_op jit(solution)/shard_map/ppermute | solution.py:574
  116.8 17.2 %collective-permute-start.12 = (bf16[384,1024]{1,0:T(8,128)(2,1)}, bf16[384,1024]{1,0:T(8,128)(2,1)}, u32[]{:S(2)}, u32[]{:S(2)}) collective-permute-start(bf16[384,1024]{1,0:T(8,128)(2,1)} %get-tuple-element.280), channel_id=1, source_target_pairs={{0,4},{4,0},{8,12},{12,8},{1,5},{5,1},{9,13},{13,9},{2,6},{6,2},{1... | collective-permute-start | bytes 2359304 | tf_op jit(solution)/shard_map/ppermute | solution.py:574
  136.3 16.0 %collective-permute-start.14 = (bf16[384,1024]{1,0:T(8,128)(2,1)S(1)}, bf16[384,1024]{1,0:T(8,128)(2,1)S(1)}, u32[]{:S(2)}, u32[]{:S(2)}) collective-permute-start(bf16[384,1024]{1,0:T(8,128)(2,1)S(1)} %get-tuple-element.469.refs_0_), channel_id=1, source_target_pairs={{0,4},{4,0},{8,12},{12,8},{1,5},{5,1},{9,13},{13,9},{2,6},{6,2},{1... | collective-permute-start | bytes 2359304 | tf_op jit(solution)/shard_map/ppermute | solution.py:574
  137.6 17.6 %collective-permute-start.15 = (bf16[384,1024]{1,0:T(8,128)(2,1)S(1)}, bf16[384,1024]{1,0:T(8,128)(2,1)S(1)}, u32[]{:S(2)}, u32[]{:S(2)}) collective-permute-start(bf16[384,1024]{1,0:T(8,128)(2,1)S(1)} %get-tuple-element.469.refs_0_), channel_id=1, source_target_pairs={{0,8},{4,12},{8,0},{12,4},{1,9},{5,13},{9,1},{13,5},{2,10},{6,14},... | collective-permute-start | bytes 2359304 | tf_op jit(solution)/shard_map/ppermute | solution.py:574
  155.3 12.1 %collective-permute-start.16 = (bf16[192,1024]{1,0:T(8,128)(2,1)S(1)}, bf16[192,1024]{1,0:T(8,128)(2,1)S(1)}, u32[]{:S(2)}, u32[]{:S(2)}) collective-permute-start(bf16[192,1024]{1,0:T(8,128)(2,1)S(1)} %slice.169), channel_id=1, source_target_pairs={{0,8},{4,12},{8,0},{12,4},{1,9},{5,13},{9,1},{13,5},{2,10},{6,14},... | collective-permute-start | bytes 1179656 | tf_op jit(solution)/shard_map/ppermute | solution.py:574
  156.7 10.7 %collective-permute-start.17 = (bf16[192,1024]{1,0:T(8,128)(2,1)S(1)}, bf16[192,1024]{1,0:T(8,128)(2,1)S(1)}, u32[]{:S(2)}, u32[]{:S(2)}) collective-permute-start(bf16[192,1024]{1,0:T(8,128)(2,1)S(1)} %slice.170), channel_id=1, source_target_pairs={{0,4},{4,0},{8,12},{12,8},{1,5},{5,1},{9,13},{13,9},{2,6},{6,2},{1... | collective-permute-start | bytes 1179656 | tf_op jit(solution)/shard_map/ppermute | solution.py:574
  167.4 35.3 %collective-permute-start.20 = (bf16[384,1024]{1,0:T(8,128)(2,1)S(1)}, bf16[384,1024]{1,0:T(8,128)(2,1)S(1)}, u32[]{:S(2)}, u32[]{:S(2)}) collective-permute-start(bf16[384,1024]{1,0:T(8,128)(2,1)S(1)} %get-tuple-element.306.refs_0_), channel_id=1, source_target_pairs={{0,4},{4,0},{8,12},{12,8},{1,5},{5,1},{9,13},{13,9},{2,6},{6,2},{1... | collective-permute-start | bytes 2359304 | tf_op jit(solution)/shard_map/ppermute | solution.py:574
  168.9 33.7 %collective-permute-start.21 = (bf16[384,1024]{1,0:T(8,128)(2,1)S(1)}, bf16[384,1024]{1,0:T(8,128)(2,1)S(1)}, u32[]{:S(2)}, u32[]{:S(2)}) collective-permute-start(bf16[384,1024]{1,0:T(8,128)(2,1)S(1)} %get-tuple-element.306.refs_0_), channel_id=1, source_target_pairs={{0,8},{4,12},{8,0},{12,4},{1,9},{5,13},{9,1},{13,5},{2,10},{6,14},... | collective-permute-start | bytes 2359304 | tf_op jit(solution)/shard_map/ppermute | solution.py:574
  196.4 9.3 %collective-permute-start.18 = (bf16[192,1024]{1,0:T(8,128)(2,1)}, bf16[192,1024]{1,0:T(8,128)(2,1)S(1)}, u32[]{:S(2)}, u32[]{:S(2)}) collective-permute-start(bf16[192,1024]{1,0:T(8,128)(2,1)} %get-tuple-element.321), channel_id=1, source_target_pairs={{0,8},{4,12},{8,0},{12,4},{1,9},{5,13},{9,1},{13,5},{2,10},{6,14},... | collective-permute-start | bytes 1179656 | tf_op jit(solution)/shard_map/ppermute | solution.py:574
  197.7 8.6 %collective-permute-start.19 = (bf16[192,1024]{1,0:T(8,128)(2,1)}, bf16[192,1024]{1,0:T(8,128)(2,1)S(1)}, u32[]{:S(2)}, u32[]{:S(2)}) collective-permute-start(bf16[192,1024]{1,0:T(8,128)(2,1)} %get-tuple-element.322), channel_id=1, source_target_pairs={{0,4},{4,0},{8,12},{12,8},{1,5},{5,1},{9,13},{13,9},{2,6},{6,2},{1... | collective-permute-start | bytes 1179656 | tf_op jit(solution)/shard_map/ppermute | solution.py:574
  202.7 16.5 %collective-permute-start.22 = (bf16[192,1024]{1,0:T(8,128)(2,1)S(1)}, bf16[192,1024]{1,0:T(8,128)(2,1)S(1)}, u32[]{:S(2)}, u32[]{:S(2)}) collective-permute-start(bf16[192,1024]{1,0:T(8,128)(2,1)S(1)} %slice.171), channel_id=1, source_target_pairs={{0,8},{4,12},{8,0},{12,4},{1,9},{5,13},{9,1},{13,5},{2,10},{6,14},... | collective-permute-start | bytes 1179656 | tf_op jit(solution)/shard_map/ppermute | solution.py:574
  203.7 15.5 %collective-permute-start.23 = (bf16[192,1024]{1,0:T(8,128)(2,1)S(1)}, bf16[192,1024]{1,0:T(8,128)(2,1)S(1)}, u32[]{:S(2)}, u32[]{:S(2)}) collective-permute-start(bf16[192,1024]{1,0:T(8,128)(2,1)S(1)} %slice.172), channel_id=1, source_target_pairs={{0,4},{4,0},{8,12},{12,8},{1,5},{5,1},{9,13},{13,9},{2,6},{6,2},{1... | collective-permute-start | bytes 1179656 | tf_op jit(solution)/shard_map/ppermute | solution.py:574
  225.0 32.7 %collective-permute-start.24 = (bf16[384,1024]{1,0:T(8,128)(2,1)S(1)}, bf16[384,1024]{1,0:T(8,128)(2,1)S(1)}, u32[]{:S(2)}, u32[]{:S(2)}) collective-permute-start(bf16[384,1024]{1,0:T(8,128)(2,1)S(1)} %copy-done.62), channel_id=1, source_target_pairs={{0,4},{4,0},{8,12},{12,8},{1,5},{5,1},{9,13},{13,9},{2,6},{6,2},{1... | collective-permute-start | bytes 2359304 | tf_op jit(solution)/shard_map/ppermute | solution.py:574
  226.5 31.1 %collective-permute-start.25 = (bf16[384,1024]{1,0:T(8,128)(2,1)S(1)}, bf16[384,1024]{1,0:T(8,128)(2,1)S(1)}, u32[]{:S(2)}, u32[]{:S(2)}) collective-permute-start(bf16[384,1024]{1,0:T(8,128)(2,1)S(1)} %copy-done.61), channel_id=1, source_target_pairs={{0,8},{4,12},{8,0},{12,4},{1,9},{5,13},{9,1},{13,5},{2,10},{6,14},... | collective-permute-start | bytes 2359304 | tf_op jit(solution)/shard_map/ppermute | solution.py:574
  266.6 8.1 %collective-permute-start.26 = (bf16[192,1024]{1,0:T(8,128)(2,1)}, bf16[192,1024]{1,0:T(8,128)(2,1)S(1)}, u32[]{:S(2)}, u32[]{:S(2)}) collective-permute-start(bf16[192,1024]{1,0:T(8,128)(2,1)} %get-tuple-element.362), channel_id=1, source_target_pairs={{0,4},{4,0},{8,12},{12,8},{1,5},{5,1},{9,13},{13,9},{2,6},{6,2},{1... | collective-permute-start | bytes 1179656 | tf_op jit(solution)/shard_map/ppermute | solution.py:574
  267.3 8.0 %collective-permute-start.27 = (bf16[192,1024]{1,0:T(8,128)(2,1)}, bf16[192,1024]{1,0:T(8,128)(2,1)S(1)}, u32[]{:S(2)}, u32[]{:S(2)}) collective-permute-start(bf16[192,1024]{1,0:T(8,128)(2,1)} %get-tuple-element.363), channel_id=1, source_target_pairs={{0,8},{4,12},{8,0},{12,4},{1,9},{5,13},{9,1},{13,5},{2,10},{6,14},... | collective-permute-start | bytes 1179656 | tf_op jit(solution)/shard_map/ppermute | solution.py:574
  284.6 16.0 %collective-permute-start.28 = (bf16[384,1024]{1,0:T(8,128)(2,1)}, bf16[384,1024]{1,0:T(8,128)(2,1)S(1)}, u32[]{:S(2)}, u32[]{:S(2)}) collective-permute-start(bf16[384,1024]{1,0:T(8,128)(2,1)} %get-tuple-element.366), channel_id=1, source_target_pairs={{0,4},{4,0},{8,12},{12,8},{1,5},{5,1},{9,13},{13,9},{2,6},{6,2},{1... | collective-permute-start | bytes 2359304 | tf_op jit(solution)/shard_map/ppermute | solution.py:574
  286.1 14.5 %collective-permute-start.29 = (bf16[384,1024]{1,0:T(8,128)(2,1)}, bf16[384,1024]{1,0:T(8,128)(2,1)S(1)}, u32[]{:S(2)}, u32[]{:S(2)}) collective-permute-start(bf16[384,1024]{1,0:T(8,128)(2,1)} %get-tuple-element.367), channel_id=1, source_target_pairs={{0,8},{4,12},{8,0},{12,4},{1,9},{5,13},{9,1},{13,5},{2,10},{6,14},... | collective-permute-start | bytes 2359304 | tf_op jit(solution)/shard_map/ppermute | solution.py:574
  300.7 14.3 %collective-permute-start.30 = (bf16[4,128,2304]{2,1,0:T(8,128)(2,1)}, bf16[4,128,2304]{2,1,0:T(8,128)(2,1)}, u32[]{:S(2)}, u32[]{:S(2)}) collective-permute-start(bf16[4,128,2304]{2,1,0:T(8,128)(2,1)} %get-tuple-element.371), channel_id=1, source_target_pairs={{0,16},{16,0},{1,17},{17,1},{2,18},{18,2},{3,19},{19,3},{4,20},{20... | collective-permute-start | bytes 7077896 | tf_op jit(solution)/shard_map/ppermute | solution.py:578
  300.8 5.3 %collective-permute-start.35 = (bf16[4,128,768]{2,1,0:T(8,128)(2,1)S(1)}, bf16[4,128,768]{2,1,0:T(8,128)(2,1)S(1)}, u32[]{:S(2)}, u32[]{:S(2)}) collective-permute-start(bf16[4,128,768]{2,1,0:T(8,128)(2,1)S(1)} %copy-done.60), channel_id=1, source_target_pairs={{0,16},{16,0},{1,17},{17,1},{2,18},{18,2},{3,19},{19,3},{4,20},{20... | collective-permute-start | bytes 2359304 | tf_op jit(solution)/shard_map/ppermute | solution.py:578
  307.1 94.6 %reduce-scatter.9.cloned.1.call-start = ((), (), s32[]{:S(2)}) async-start(), calls=%async_computation.4 | async-start | bytes 2949120 | tf_op jit(solution)/shard_map/reduce_scatter | solution.py:602
  313.3 19.8 %collective-permute-start.31 = (bf16[384,1024]{1,0:T(8,128)(2,1)S(1)}, bf16[384,1024]{1,0:T(8,128)(2,1)S(1)}, u32[]{:S(2)}, u32[]{:S(2)}) collective-permute-start(bf16[384,1024]{1,0:T(8,128)(2,1)S(1)} %get-tuple-element.467.refs_0_), channel_id=1, source_target_pairs={{0,4},{4,0},{8,12},{12,8},{1,5},{5,1},{9,13},{13,9},{2,6},{6,2},{1... | collective-permute-start | bytes 2359304 | tf_op jit(solution)/shard_map/ppermute | solution.py:574
  313.9 19.5 %collective-permute-start.32 = (bf16[384,1024]{1,0:T(8,128)(2,1)S(1)}, bf16[384,1024]{1,0:T(8,128)(2,1)S(1)}, u32[]{:S(2)}, u32[]{:S(2)}) collective-permute-start(bf16[384,1024]{1,0:T(8,128)(2,1)S(1)} %get-tuple-element.467.refs_0_), channel_id=1, source_target_pairs={{0,8},{4,12},{8,0},{12,4},{1,9},{5,13},{9,1},{13,5},{2,10},{6,14},... | collective-permute-start | bytes 2359304 | tf_op jit(solution)/shard_map/ppermute | solution.py:574
  318.8 149.8 %reduce-scatter.11.cloned.1.call-start = ((), (), s32[]{:S(2)}) async-start(), calls=%async_computation.5 | async-start | bytes 2949120 | tf_op jit(solution)/shard_map/reduce_scatter | solution.py:602
  333.5 10.6 %collective-permute-start.33 = (bf16[192,1024]{1,0:T(8,128)(2,1)S(1)}, bf16[192,1024]{1,0:T(8,128)(2,1)S(1)}, u32[]{:S(2)}, u32[]{:S(2)}) collective-permute-start(bf16[192,1024]{1,0:T(8,128)(2,1)S(1)} %slice.173), channel_id=1, source_target_pairs={{0,8},{4,12},{8,0},{12,4},{1,9},{5,13},{9,1},{13,5},{2,10},{6,14},... | collective-permute-start | bytes 1179656 | tf_op jit(solution)/shard_map/ppermute | solution.py:574
  334.7 10.1 %collective-permute-start.34 = (bf16[192,1024]{1,0:T(8,128)(2,1)S(1)}, bf16[192,1024]{1,0:T(8,128)(2,1)S(1)}, u32[]{:S(2)}, u32[]{:S(2)}) collective-permute-start(bf16[192,1024]{1,0:T(8,128)(2,1)S(1)} %slice.174), channel_id=1, source_target_pairs={{0,4},{4,0},{8,12},{12,8},{1,5},{5,1},{9,13},{13,9},{2,6},{6,2},{1... | collective-permute-start | bytes 1179656 | tf_op jit(solution)/shard_map/ppermute | solution.py:574
  371.5 119.6 %reduce-scatter.15.cloned.1.call-start = ((), (), s32[]{:S(2)}) async-start(), calls=%async_computation.7 | async-start | bytes 983040
  410.2 11.4 %collective-permute-start.37 = (bf16[192,1024]{1,0:T(8,128)(2,1)}, bf16[192,1024]{1,0:T(8,128)(2,1)S(1)}, u32[]{:S(2)}, u32[]{:S(2)}) collective-permute-start(bf16[192,1024]{1,0:T(8,128)(2,1)} %get-tuple-element.414), channel_id=1, source_target_pairs={{0,4},{4,0},{8,12},{12,8},{1,5},{5,1},{9,13},{13,9},{2,6},{6,2},{1... | collective-permute-start | bytes 1179656 | tf_op jit(solution)/shard_map/ppermute | solution.py:574
  411.6 11.1 %collective-permute-start.38 = (bf16[192,1024]{1,0:T(8,128)(2,1)}, bf16[192,1024]{1,0:T(8,128)(2,1)S(1)}, u32[]{:S(2)}, u32[]{:S(2)}) collective-permute-start(bf16[192,1024]{1,0:T(8,128)(2,1)} %get-tuple-element.415), channel_id=1, source_target_pairs={{0,8},{4,12},{8,0},{12,4},{1,9},{5,13},{9,1},{13,5},{2,10},{6,14},... | collective-permute-start | bytes 1179656 | tf_op jit(solution)/shard_map/ppermute | solution.py:574
  432.3 18.9 %collective-permute-start.42 = (bf16[384,1024]{1,0:T(8,128)(2,1)}, bf16[384,1024]{1,0:T(8,128)(2,1)}, u32[]{:S(2)}, u32[]{:S(2)}) collective-permute-start(bf16[384,1024]{1,0:T(8,128)(2,1)} %get-tuple-element.425), channel_id=1, source_target_pairs={{0,4},{4,0},{8,12},{12,8},{1,5},{5,1},{9,13},{13,9},{2,6},{6,2},{1... | collective-permute-start | bytes 2359304 | tf_op jit(solution)/shard_map/ppermute | solution.py:574
  432.9 18.7 %collective-permute-start.43 = (bf16[384,1024]{1,0:T(8,128)(2,1)}, bf16[384,1024]{1,0:T(8,128)(2,1)}, u32[]{:S(2)}, u32[]{:S(2)}) collective-permute-start(bf16[384,1024]{1,0:T(8,128)(2,1)} %get-tuple-element.426), channel_id=1, source_target_pairs={{0,8},{4,12},{8,0},{12,4},{1,9},{5,13},{9,1},{13,5},{2,10},{6,14},... | collective-permute-start | bytes 2359304 | tf_op jit(solution)/shard_map/ppermute | solution.py:574
  435.9 17.8 %collective-permute-start.44 = (bf16[384,1024]{1,0:T(8,128)(2,1)S(1)}, bf16[384,1024]{1,0:T(8,128)(2,1)S(1)}, u32[]{:S(2)}, u32[]{:S(2)}) collective-permute-start(bf16[384,1024]{1,0:T(8,128)(2,1)S(1)} %copy-done.16), channel_id=1, source_target_pairs={{0,16},{1,17},{2,18},{3,19},{4,20},{5,21},{6,22},{7,23},{8,24},{9,... | collective-permute-start | bytes 2359304 | tf_op jit(solution)/shard_map/ppermute | solution.py:782
  442.4 51.1 %collective-permute-start.49 = (bf16[128,768]{0,1:T(8,128)(2,1)S(1)}, bf16[128,768]{0,1:T(8,128)(2,1)S(1)}, u32[]{:S(2)}, u32[]{:S(2)}) collective-permute-start(bf16[128,768]{0,1:T(8,128)(2,1)S(1)} %copy.107), channel_id=1, source_target_pairs={{0,16},{1,17},{2,18},{3,19},{4,20},{5,21},{6,22},{7,23},{8,24},{9,... | collective-permute-start | bytes 589832 | tf_op jit(solution)/shard_map/ppermute | solution.py:782
  444.5 25.4 %collective-permute-start.51 = (bf16[128,2304]{1,0:T(8,128)(2,1)}, bf16[128,2304]{1,0:T(8,128)(2,1)}, u32[]{:S(2)}, u32[]{:S(2)}) collective-permute-start(bf16[128,2304]{1,0:T(8,128)(2,1)} %reduce-scatter.9.cloned.1.call-done), channel_id=1, source_target_pairs={{0,16},{1,17},{2,18},{3,19},{4,20},{5,21},{6,22},{7,23},{8,24},{9,... | collective-permute-start | bytes 1769480 | tf_op jit(solution)/shard_map/ppermute | solution.py:782
  451.2 8.7 %collective-permute-start.48 = (bf16[4,128,768]{2,1,0:T(8,128)(2,1)}, bf16[4,128,768]{2,1,0:T(8,128)(2,1)}, u32[]{:S(2)}, u32[]{:S(2)}) collective-permute-start(bf16[4,128,768]{2,1,0:T(8,128)(2,1)} %get-tuple-element.435), channel_id=1, source_target_pairs={{0,16},{16,0},{1,17},{17,1},{2,18},{18,2},{3,19},{19,3},{4,20},{20... | collective-permute-start | bytes 2359304 | tf_op jit(solution)/shard_map/ppermute | solution.py:578
  457.2 14.1 %collective-permute-start.45 = (bf16[384,1024]{1,0:T(8,128)(2,1)}, bf16[384,1024]{1,0:T(8,128)(2,1)S(1)}, u32[]{:S(2)}, u32[]{:S(2)}) collective-permute-start(bf16[384,1024]{1,0:T(8,128)(2,1)} %get-tuple-element.465), channel_id=1, source_target_pairs={{16,0},{17,1},{18,2},{19,3},{20,4},{21,5},{22,6},{23,7},{24,8},{25... | collective-permute-start | bytes 2359304 | tf_op jit(solution)/shard_map/ppermute | solution.py:783
  (77 other events, 594.2 us)
Sparse Core Ops, SparseCore 0:
  307.2 22.2 reduce-scatter.12
  331.9 47.2 reduce-scatter.8
  381.5 47.5 reduce-scatter.10
  468.8 22.2 reduce-scatter.14
